TPU v7x, 32 devices: a whole 2x2x4 slice. The times are simulated.
32 devices in a mesh: section: 2 (over y), row: 16 (over z, x, core).
Axes of the slice: x: 2, y: 2, z: 4, core: 2. Of those that a mesh axis runs over, the one named last changes fastest.
Arguments:
- pair: bfloat16 [2, 128, 128, 128], P(None, 'row'), may hold values from -6 to 6
- valid_tokens: int32 [2], replicated, may hold values from 32 to 128, as said below
- crop_order: int32 [2], replicated, may hold values from 0 to 1, each once
- w_proj: bfloat16 [2, 128, 384], P('section'), may hold values from -0.5 to 0.5
- w_out: bfloat16 [2, 64, 128], P('section'), may hold values from -0.75 to 0.75
- w_in: bfloat16 [2, 128, 1024], P('section'), may hold values from -0.5 to 0.5
- w_back: bfloat16 [2, 512, 128], P('section'), may hold values from -0.25 to 0.25
Outputs:
- final_pair: bfloat16 [2, 128, 128, 128], P('section', 'row')
Inputs may be any that keep to these rules, and one draw needn't show every extreme that they name: `valid_tokens`: valid tokens of each crop; some crop is full and some other has 32. `crop_order`: each crop is taken at exactly one slot.
All inputs are finite; a program needn't handle non-finite values.
Results may differ from a plain program's by a relative error of at most 0.015.
Values may be sent and summed in bfloat16 or wider, within the bound.
No kernel may reach another device: no remote copies, remote signals or barrier semaphores. Data moves between devices by JAX's collectives and lax.ppermute only.
A program may use at most 64 MiB of HBM per device.

v0:
```python
import jax
import jax.numpy as jnp
from jax import lax
from jax.sharding import PartitionSpec as P


def layer_norm(value):
    mean = jnp.mean(value, -1, keepdims=True)
    centred = value - mean
    var = jnp.mean(centred * centred, -1, keepdims=True)
    return centred * lax.rsqrt(var + 1e-05)


def pair_block(state, valid, row_start, w_proj, w_out, w_in, w_back):
    rows_here = state.shape[0]
    count = state.shape[1]
    width = state.shape[2]
    inner = w_out.shape[0]
    trans = w_back.shape[0]
    normed = (
        layer_norm(state.astype(jnp.float32)).astype(jnp.bfloat16).reshape(rows_here * count, width)
    )
    proj = jnp.dot(normed, w_proj, preferred_element_type=jnp.float32).reshape(rows_here, count, -1)
    keep_cols = (jnp.arange(count) < valid).astype(jnp.float32)
    keep_rows = (row_start + jnp.arange(rows_here) < valid).astype(jnp.float32)
    mask = keep_rows[:, None, None] * keep_cols[None, :, None]
    left = (mask * jax.nn.sigmoid(proj[..., inner : 2 * inner]) * proj[..., :inner]).astype(
        jnp.bfloat16
    )
    right = (
        mask * jax.nn.sigmoid(proj[..., 3 * inner : 4 * inner]) * proj[..., 2 * inner : 3 * inner]
    ).astype(jnp.bfloat16)
    gate = jax.nn.sigmoid(proj[..., 4 * inner :])
    left_whole, right_whole = (
        lax.all_to_all(left, "row", split_axis=2, concat_axis=0, tiled=True),
        lax.all_to_all(right, "row", split_axis=2, concat_axis=0, tiled=True),
    )
    tri_part = jnp.einsum(
        "ikc,jkc->ijc", left_whole, right_whole, preferred_element_type=jnp.float32
    )
    tri = lax.all_to_all(
        tri_part.astype(jnp.bfloat16), "row", split_axis=0, concat_axis=2, tiled=True
    ).astype(tri_part.dtype)
    tri_normed = layer_norm(tri).astype(jnp.bfloat16).reshape(rows_here * count, inner)
    update = jnp.dot(tri_normed, w_out, preferred_element_type=jnp.float32).reshape(
        rows_here, count, width
    )
    first = (state.astype(jnp.float32) + gate * update).astype(jnp.bfloat16)
    second = (
        layer_norm(first.astype(jnp.float32)).astype(jnp.bfloat16).reshape(rows_here * count, width)
    )
    hidden = jnp.dot(second, w_in, preferred_element_type=jnp.float32)
    act = (jax.nn.silu(hidden[:, :trans]) * hidden[:, trans:]).astype(jnp.bfloat16)
    back = jnp.dot(act, w_back, preferred_element_type=jnp.float32).reshape(rows_here, count, width)
    return (first.astype(jnp.float32) + back).astype(jnp.bfloat16)


def on_device(pair, valid_tokens, crop_order, w_proj, w_out, w_in, w_back):
    crops = pair.shape[0]
    rows_here = pair.shape[1]
    row_start = lax.axis_index("row") * rows_here
    sections = lax.axis_size("section")
    section = lax.axis_index("section")
    share = crops // sections
    all_proj, all_out, all_in, all_back = (
        lax.all_gather(w_proj, "section", axis=0, tiled=True),
        lax.all_gather(w_out, "section", axis=0, tiled=True),
        lax.all_gather(w_in, "section", axis=0, tiled=True),
        lax.all_gather(w_back, "section", axis=0, tiled=True),
    )
    blocks = all_proj.shape[0]

    def one_crop(index, outputs):
        crop = crop_order[section * share + index]
        valid = valid_tokens[crop]
        state = lax.dynamic_index_in_dim(pair, crop, 0, keepdims=False)

        def apply_block(block, value):
            return pair_block(
                value,
                valid,
                row_start,
                all_proj[block],
                all_out[block],
                all_in[block],
                all_back[block],
            )

        final = lax.fori_loop(0, blocks, apply_block, state)
        return lax.dynamic_update_index_in_dim(outputs, final, index, 0)

    empty = jnp.zeros((share,) + pair.shape[1:], jnp.bfloat16)
    return lax.fori_loop(0, share, one_crop, empty)


def solution(mesh):
    in_specs = (
        P(None, "row", None, None),
        P(),
        P(),
        P("section", None, None),
        P("section", None, None),
        P("section", None, None),
        P("section", None, None),
    )
    out_specs = P("section", "row", None, None)
    return jax.shard_map(
        on_device, mesh=mesh, in_specs=in_specs, out_specs=out_specs, check_vma=False
    )
```

profile of v0, /device:TPU:0, one launch (start us, length us, event | category | flops | bytes accessed | tf_op | source)
XLA Modules:
  0.0 133.9 jit_solution(968022301504030877)
XLA Ops:
  0.0 1.3 dynamic_slice.41
  3.3 1.2 dynamic_slice.43
  4.5 13.2 %all_gather.14 = bf16[2,128,1024]{2,1,0:T(8,128)(2,1)} all-gather(bf16[1,128,1024]{2,1,0:T(8,128)(2,1)} %param.14), channel_id=1, replica_groups=mesh['section'=2,'row'=16] {'section'}, dimensions={0}, use_global_device_ids=true | all-gather | bytes 786432 | tf_op jit(solution)/shard_map/all_gather | solution.py:68
  17.7 5.9 %all_gather.15 = bf16[2,512,128]{2,1,0:T(8,128)(2,1)} all-gather(bf16[1,512,128]{2,1,0:T(8,128)(2,1)} %param.15), channel_id=1, replica_groups=mesh['section'=2,'row'=16] {'section'}, dimensions={0}, use_global_device_ids=true | all-gather | bytes 393216 | tf_op jit(solution)/shard_map/all_gather | solution.py:69
  23.6 5.5 %all_gather.12 = bf16[2,128,384]{2,1,0:T(8,128)(2,1)S(1)} all-gather(bf16[1,128,384]{2,1,0:T(8,128)(2,1)} %param.12), channel_id=1, replica_groups=mesh['section'=2,'row'=16] {'section'}, dimensions={0}, use_global_device_ids=true | all-gather | bytes 294912 | tf_op jit(solution)/shard_map/all_gather | solution.py:66
  29.1 4.6 %all_gather.13 = bf16[2,64,128]{2,1,0:T(8,128)(2,1)S(1)} all-gather(bf16[1,64,128]{2,1,0:T(8,128)(2,1)} %param.13), channel_id=1, replica_groups=mesh['section'=2,'row'=16] {'section'}, dimensions={0}, use_global_device_ids=true | all-gather | bytes 49152 | tf_op jit(solution)/shard_map/all_gather | solution.py:67
  33.7 99.5 %while.21 = (s32[]{:T(128)}, bf16[8,128,128]{2,1,0:T(8,128)(2,1)S(1)}, bf16[2,128,384]{2,1,0:T(8,128)(2,1)S(1)}, s32[]{:T(128)}, s32[]{:T(128)}, /*index=5*/bf16...) while((s32[]{:T(128)}, ...), condition=%wide.region_7.8_spmd, body=%wide.region_0.7_spmd.sunk | while | flops 545067264 | bytes 30512496 | solution.py:89
  34.4 0.5 fusion.73
  34.9 1.4 %fusion.74 = (f32[8,128,64]{2,1,0:T(8,128)}, f32[8,128,64]{2,1,0:T(8,128)S(1)}, f32[8,128,64]{2,1,0:T(8,128)}, f32[8,128,64]{2,1,0:T(8,128)S(1)}) fusion(f32[8,128,384]{2,1,0:T(8,128)S(1)} %fusion.73), kind=kLoop, calls=%fused_computation.62.clone.1 | loop fusion | bytes 2097152 | tf_op jit(solution)/shard_map/while/body/eval_jaxpr/while/body/eval_jaxpr/slice | solution.py:31
  36.2 1.9 %copy.84 = f32[8,128,64]{1,2,0:T(8,128)} copy(f32[8,128,64]{2,1,0:T(8,128)} %get-tuple-element.272) | data formatting | bytes 524288 | tf_op jit(solution)/shard_map/while/body/eval_jaxpr/while
  38.2 1.9 %copy.85 = f32[8,128,64]{1,2,0:T(8,128)} copy(f32[8,128,64]{2,1,0:T(8,128)} %get-tuple-element.273) | data formatting | bytes 524288 | tf_op jit(solution)/shard_map/while/body/eval_jaxpr/while
  40.1 0.9 copy.86
  41.2 0.5 compare_convert_fusion.4
  41.8 0.5 compare_convert_fusion.5
  42.4 1.3 multiply_convert_fusion.5
  43.6 0.7 copy.88
  44.4 5.9 %all-to-all-start = ((bf16[8,128,64]{1,0,2:T(8,128)(2,1)}), bf16[8,128,64]{1,0,2:T(8,128)(2,1)S(1)}, u32[]{:S(2)}, u32[]{:S(2)}) async-start(bf16[8,128,64]{1,0,2:T(8,128)(2,1)} %copy.88), calls=%async_computation | async-start | bytes 262144 | tf_op jit(solution)/shard_map/while/body/eval_jaxpr/while/body/eval_jaxpr/all_to_all | solution.py:35
  50.4 7.8 %all-to-all-done = bf16[8,128,64]{1,0,2:T(8,128)(2,1)S(1)} async-done(((bf16[8,128,64]{1,0,2:T(8,128)(2,1)}), bf16[8,128,64]{1,0,2:T(8,128)(2,1)S(1)}, u32[]{:S(2)}, u32[]{:S(2)}) %all-to-all-start) | async-done | bytes 131104 | tf_op jit(solution)/shard_map/while/body/eval_jaxpr/while/body/eval_jaxpr/all_to_all | solution.py:35
  58.2 10.5 %all_to_all.88 = bf16[8,128,64]{1,0,2:T(8,128)(2,1)S(1)} all-to-all(bf16[8,128,64]{1,0,2:T(8,128)(2,1)S(1)} %copy.89), channel_id=1, replica_groups=mesh['section'=2,'row'=16] {'row'}, dimensions={2} | all-to-all | bytes 262144 | tf_op jit(solution)/shard_map/while/body/eval_jaxpr/while/body/eval_jaxpr/all_to_all | solution.py:36
  68.9 0.8 copy.90
  69.7 3.5 %all-to-all-start.2 = ((bf16[128,128,4]{1,2,0:T(4,128)(2,1)}), bf16[128,128,4]{1,2,0:T(4,128)(2,1)S(1)}, u32[]{:S(2)}, u32[]{:S(2)}) async-start(bf16[128,128,4]{1,2,0:T(4,128)(2,1)} %copy.90), calls=%async_computation.2 | async-start | bytes 262144 | tf_op jit(solution)/shard_map/while/body/eval_jaxpr/while/body/eval_jaxpr/all_to_all | solution.py:41
  73.2 7.9 %all-to-all-done.2 = bf16[128,128,4]{1,2,0:T(4,128)(2,1)S(1)} async-done(((bf16[128,128,4]{1,2,0:T(4,128)(2,1)}), bf16[128,128,4]{1,2,0:T(4,128)(2,1)S(1)}, u32[]{:S(2)}, u32[]{:S(2)}) %all-to-all-start.2) | async-done | bytes 131104 | tf_op jit(solution)/shard_map/while/body/eval_jaxpr/while/body/eval_jaxpr/all_to_all | solution.py:41
  81.3 0.4 fusion.79
  81.8 0.4 multiply_reduce_fusion.2
  82.5 0.7 fusion.80
  83.3 0.7 fusion.81
  84.2 0.4 fusion.82
  85.3 0.5 fusion.73
  85.8 1.4 %fusion.74 = (f32[8,128,64]{2,1,0:T(8,128)}, f32[8,128,64]{2,1,0:T(8,128)S(1)}, f32[8,128,64]{2,1,0:T(8,128)}, f32[8,128,64]{2,1,0:T(8,128)S(1)}) fusion(f32[8,128,384]{2,1,0:T(8,128)S(1)} %fusion.73), kind=kLoop, calls=%fused_computation.62.clone.1 | loop fusion | bytes 2097152 | tf_op jit(solution)/shard_map/while/body/eval_jaxpr/while/body/eval_jaxpr/slice | solution.py:31
  87.2 1.9 %copy.84 = f32[8,128,64]{1,2,0:T(8,128)} copy(f32[8,128,64]{2,1,0:T(8,128)} %get-tuple-element.272) | data formatting | bytes 524288 | tf_op jit(solution)/shard_map/while/body/eval_jaxpr/while
  89.1 1.9 %copy.85 = f32[8,128,64]{1,2,0:T(8,128)} copy(f32[8,128,64]{2,1,0:T(8,128)} %get-tuple-element.273) | data formatting | bytes 524288 | tf_op jit(solution)/shard_map/while/body/eval_jaxpr/while
  91.1 0.9 copy.86
  92.2 0.5 compare_convert_fusion.4
  92.7 0.5 compare_convert_fusion.5
  93.3 1.3 multiply_convert_fusion.5
  94.6 0.7 copy.88
  95.3 3.5 %all-to-all-start = ((bf16[8,128,64]{1,0,2:T(8,128)(2,1)}), bf16[8,128,64]{1,0,2:T(8,128)(2,1)S(1)}, u32[]{:S(2)}, u32[]{:S(2)}) async-start(bf16[8,128,64]{1,0,2:T(8,128)(2,1)} %copy.88), calls=%async_computation | async-start | bytes 262144 | tf_op jit(solution)/shard_map/while/body/eval_jaxpr/while/body/eval_jaxpr/all_to_all | solution.py:35
  99.0 7.8 %all-to-all-done = bf16[8,128,64]{1,0,2:T(8,128)(2,1)S(1)} async-done(((bf16[8,128,64]{1,0,2:T(8,128)(2,1)}), bf16[8,128,64]{1,0,2:T(8,128)(2,1)S(1)}, u32[]{:S(2)}, u32[]{:S(2)}) %all-to-all-start) | async-done | bytes 131104 | tf_op jit(solution)/shard_map/while/body/eval_jaxpr/while/body/eval_jaxpr/all_to_all | solution.py:35
  106.7 10.5 %all_to_all.88 = bf16[8,128,64]{1,0,2:T(8,128)(2,1)S(1)} all-to-all(bf16[8,128,64]{1,0,2:T(8,128)(2,1)S(1)} %copy.89), channel_id=1, replica_groups=mesh['section'=2,'row'=16] {'row'}, dimensions={2} | all-to-all | bytes 262144 | tf_op jit(solution)/shard_map/while/body/eval_jaxpr/while/body/eval_jaxpr/all_to_all | solution.py:36
  117.4 0.8 copy.90
  118.2 3.5 %all-to-all-start.2 = ((bf16[128,128,4]{1,2,0:T(4,128)(2,1)}), bf16[128,128,4]{1,2,0:T(4,128)(2,1)S(1)}, u32[]{:S(2)}, u32[]{:S(2)}) async-start(bf16[128,128,4]{1,2,0:T(4,128)(2,1)} %copy.90), calls=%async_computation.2 | async-start | bytes 262144 | tf_op jit(solution)/shard_map/while/body/eval_jaxpr/while/body/eval_jaxpr/all_to_all | solution.py:41
  121.7 7.9 %all-to-all-done.2 = bf16[128,128,4]{1,2,0:T(4,128)(2,1)S(1)} async-done(((bf16[128,128,4]{1,2,0:T(4,128)(2,1)}), bf16[128,128,4]{1,2,0:T(4,128)(2,1)S(1)}, u32[]{:S(2)}, u32[]{:S(2)}) %all-to-all-start.2) | async-done | bytes 131104 | tf_op jit(solution)/shard_map/while/body/eval_jaxpr/while/body/eval_jaxpr/all_to_all | solution.py:41
  129.9 0.4 fusion.79
  130.3 0.4 multiply_reduce_fusion.2
  131.0 0.7 fusion.80
  131.8 0.7 fusion.81
  132.7 0.4 fusion.82
  133.2 0.7 copy-done.1
  (54 shorter events, 4.0 us)
Async XLA Ops:
  0.0 3.2 %copy-start = (bf16[2,8,128,128]{3,2,1,0:T(8,128)(2,1)S(1)}, bf16[2,8,128,128]{3,2,1,0:T(8,128)(2,1)}, u32[]{:S(2)}) copy-start(bf16[2,8,128,128]{3,2,1,0:T(8,128)(2,1)} %param.9) | copy-start | bytes 1572868
  33.7 0.7 copy-start.4
  44.4 13.8 %all-to-all-start = ((bf16[8,128,64]{1,0,2:T(8,128)(2,1)}), bf16[8,128,64]{1,0,2:T(8,128)(2,1)S(1)}, u32[]{:S(2)}, u32[]{:S(2)}) async-start(bf16[8,128,64]{1,0,2:T(8,128)(2,1)} %copy.88), calls=%async_computation | async-start | bytes 262144 | tf_op jit(solution)/shard_map/while/body/eval_jaxpr/while/body/eval_jaxpr/all_to_all | solution.py:35
  69.7 11.4 %all-to-all-start.2 = ((bf16[128,128,4]{1,2,0:T(4,128)(2,1)}), bf16[128,128,4]{1,2,0:T(4,128)(2,1)S(1)}, u32[]{:S(2)}, u32[]{:S(2)}) async-start(bf16[128,128,4]{1,2,0:T(4,128)(2,1)} %copy.90), calls=%async_computation.2 | async-start | bytes 262144 | tf_op jit(solution)/shard_map/while/body/eval_jaxpr/while/body/eval_jaxpr/all_to_all | solution.py:41
  81.3 1.2 copy-start.2
  83.2 1.0 copy-start.3
  83.2 1.4 %copy-start.5 = (bf16[2,128,384]{2,1,0:T(8,128)(2,1)S(1)}, bf16[2,128,384]{2,1,0:T(8,128)(2,1)}, u32[]{:S(2)}) copy-start(bf16[2,128,384]{2,1,0:T(8,128)(2,1)} %copy-done.4) | copy-start | bytes 589828 | tf_op jit(solution)/shard_map/while/body/eval_jaxpr/while
  84.7 0.7 copy-start.4
  95.3 11.4 %all-to-all-start = ((bf16[8,128,64]{1,0,2:T(8,128)(2,1)}), bf16[8,128,64]{1,0,2:T(8,128)(2,1)S(1)}, u32[]{:S(2)}, u32[]{:S(2)}) async-start(bf16[8,128,64]{1,0,2:T(8,128)(2,1)} %copy.88), calls=%async_computation | async-start | bytes 262144 | tf_op jit(solution)/shard_map/while/body/eval_jaxpr/while/body/eval_jaxpr/all_to_all | solution.py:35
  118.2 11.4 %all-to-all-start.2 = ((bf16[128,128,4]{1,2,0:T(4,128)(2,1)}), bf16[128,128,4]{1,2,0:T(4,128)(2,1)S(1)}, u32[]{:S(2)}, u32[]{:S(2)}) async-start(bf16[128,128,4]{1,2,0:T(4,128)(2,1)} %copy.90), calls=%async_computation.2 | async-start | bytes 262144 | tf_op jit(solution)/shard_map/while/body/eval_jaxpr/while/body/eval_jaxpr/all_to_all | solution.py:41
  129.8 1.2 copy-start.2
  131.8 1.0 copy-start.3
  131.8 1.4 %copy-start.5 = (bf16[2,128,384]{2,1,0:T(8,128)(2,1)S(1)}, bf16[2,128,384]{2,1,0:T(8,128)(2,1)}, u32[]{:S(2)}) copy-start(bf16[2,128,384]{2,1,0:T(8,128)(2,1)} %copy-done.4) | copy-start | bytes 589828 | tf_op jit(solution)/shard_map/while/body/eval_jaxpr/while
  133.2 0.7 copy-start.1
where the time goes:
time: 135 us; the launch traced here: 134 us
  blocking collectives  50.2 us (37%)
  waiting for transfers between devices  31.3 us (23%)
  local copies, waits for them, and re-layouts  19.9 us (15%)
  starting transfers between devices  16.4 us (12%)
  other arithmetic  9.13 us (7%)
  matrix products  4.56 us (3%)
  between operations  1.98 us (1%)
    all_to_all x2, blocking collectives, pair_block(): lax.all_to_all(right, 'row', split_axis=2, concat_axis=0, tiled=True)  21 us
    all_to_all x2, waiting for transfers between devices, pair_block(): lax.all_to_all(tri_part.astype(jnp.bfloat16), 'row', split_axis=0, concat...  15.7 us
    all_to_all x2, waiting for transfers between devices, pair_block(): lax.all_to_all(left, 'row', split_axis=2, concat_axis=0, tiled=True)  15.6 us
    all_gather x1, blocking collectives, on_device(): lax.all_gather(w_in, 'section', axis=0, tiled=True)  13.2 us
    while x24, local copies, waits for them, and re-layouts  10.6 us
    all_to_all x2, starting transfers between devices, pair_block(): lax.all_to_all(left, 'row', split_axis=2, concat_axis=0, tiled=True)  9.42 us
    all_to_all x2, starting transfers between devices, pair_block(): lax.all_to_all(tri_part.astype(jnp.bfloat16), 'row', split_axis=0, concat...  7.03 us
    all_gather x1, blocking collectives, on_device(): lax.all_gather(w_back, 'section', axis=0, tiled=True)  5.94 us
  transfers between devices with their start and end apart: 4, of which 4 were waited for; matrix products, arithmetic and copies ran while one was open for 0% of the time, Pallas kernels for 0%

commit v1 on v0

v1 whole, which is shorter than its diff:
```python
import functools

import jax
import jax.numpy as jnp
from jax import lax
from jax.experimental import pallas as pl
from jax.experimental.pallas import tpu as pltpu
from jax.sharding import PartitionSpec as P

F32 = jnp.float32
BF16 = jnp.bfloat16


def layer_norm(value, axis=-1):
    mean = jnp.mean(value, axis, keepdims=True)
    centred = value - mean
    var = jnp.mean(centred * centred, axis, keepdims=True)
    return centred * lax.rsqrt(var + 1e-05)


def fetch(condition, own, other, target, sem):
    @pl.when(condition)
    def _():
        pltpu.make_async_copy(own, target, sem).start()

    @pl.when(jnp.logical_not(condition))
    def _():
        pltpu.make_async_copy(other, target, sem).start()

    return pltpu.make_async_copy(own, target, sem)


def ordered_weights(weights, inner, share):
    wide = 2 * share
    row = lax.broadcasted_iota(jnp.int32, (4 * inner, 4 * inner), 0)
    column = lax.broadcasted_iota(jnp.int32, (4 * inner, 4 * inner), 1)
    gates, rest = lax.div(row, 2 * inner), lax.rem(row, 2 * inner)
    peer, slot = lax.div(rest, wide), lax.rem(rest, wide)
    side, channel = lax.div(slot, share), lax.rem(slot, share)
    source = side * (2 * inner) + gates * inner + peer * share + channel
    pick = jnp.where(column == source, 1.0, 0.0).astype(BF16)
    return lax.dot_general(
        pick, weights, (((1,), (1,)), ((), ())), preferred_element_type=F32
    ).astype(BF16)


def project(normed_ref, w_ref, valid, row_start, lr_ref, gate_ref, inner):
    peers, rows, wide, count = lr_ref.shape
    turned = ordered_weights(w_ref[:, : 4 * inner], inner, wide // 2)
    gate_w = w_ref[:, 4 * inner :]
    column = lax.broadcasted_iota(jnp.int32, (1, count), 1)
    for r in range(rows):
        normed = normed_ref[r * count : (r + 1) * count, :]
        proj = lax.dot_general(
            turned, normed, (((1,), (1,)), ((), ())), preferred_element_type=F32
        )
        keep = jnp.logical_and(column < valid, row_start + r < valid)
        mask = jnp.where(keep, 1.0, 0.0)
        sides = mask * jax.nn.sigmoid(proj[2 * inner :]) * proj[: 2 * inner]
        lr_ref[:, r] = sides.reshape(peers, wide, count).astype(BF16)
        gate_ref[r * count : (r + 1) * count, :] = jax.nn.sigmoid(
            jnp.dot(normed, gate_w, preferred_element_type=F32)
        )


def first_kernel(
    inner, order_ref, valid_ref, pair_ref, own_ref, other_ref, lr_ref, gate_ref, z_ref, w_ref, n_ref, sems
):
    section = lax.axis_index("section")
    rows, count = pair_ref.shape[1:3]
    row_start = lax.axis_index("row") * rows
    crop = order_ref[section]
    valid = valid_ref[crop]
    state = pltpu.make_async_copy(pair_ref.at[crop], z_ref, sems.at[0])
    state.start()
    weights = fetch(section == 0, own_ref.at[0], other_ref.at[0], w_ref, sems.at[1])
    state.wait()
    for r in range(rows):
        n_ref[r * count : (r + 1) * count, :] = layer_norm(z_ref[r].astype(F32)).astype(BF16)
    weights.wait()
    project(n_ref, w_ref, valid, row_start, lr_ref, gate_ref, inner)


def tri_kernel(in_ref, out_ref, wide_ref):
    peers, rows, wide, count = in_ref.shape
    share = wide // 2
    total = peers * rows
    wide_ref[...] = in_ref[...].astype(F32).reshape(total * wide, count)
    for c in range(share):
        left = wide_ref[pl.ds(c, total, stride=wide), :].astype(BF16)
        right = wide_ref[pl.ds(share + c, total, stride=wide), :].astype(BF16)
        tri = lax.dot_general(
            left, right, (((1,), (1,)), ((), ())), preferred_element_type=F32
        )
        out_ref[:, c] = tri.reshape(peers, rows, total).astype(BF16)


def update_kernel(
    block,
    blocks,
    inner,
    trans,
    order_ref,
    valid_ref,
    tri_ref,
    gate_ref,
    z_ref,
    own_ref,
    other_ref,
    wp_own_ref,
    wp_other_ref,
    *refs,
):
    last = block == blocks - 1
    if last:
        out_ref, t_ref, w_ref, n_ref, z1_ref, zs_ref, sems = refs
    else:
        out_ref, lr_ref, gate_out_ref, t_ref, w_ref, n_ref, z1_ref, zs_ref, sems, wp_ref = refs
    section = lax.axis_index("section")
    rows, count, width = out_ref.shape
    row_start = lax.axis_index("row") * rows
    crop = order_ref[section]
    valid = valid_ref[crop]
    if block == 0:
        state = pltpu.make_async_copy(z_ref.at[crop], zs_ref, sems.at[0])
    else:
        state = pltpu.make_async_copy(z_ref, zs_ref, sems.at[0])
    state.start()
    weights = fetch(section == block, own_ref, other_ref, w_ref, sems.at[1])
    if not last:
        following = fetch(
            section == block + 1, wp_own_ref.at[0], wp_other_ref.at[0], wp_ref, sems.at[2]
        )
    parts = width * (2 * trans // width)
    t_ref[...] = layer_norm(tri_ref[...].reshape(inner, rows, count).astype(F32), 0).reshape(
        inner * rows, count
    )
    weights.wait()
    state.wait()
    w_out = w_ref[parts + trans : parts + trans + inner, :]
    for r in range(rows):
        here = slice(r * count, (r + 1) * count)
        tri = t_ref[pl.ds(r, inner, stride=rows), :].astype(BF16)
        update = lax.dot_general(
            tri, w_out, (((0,), (0,)), ((), ())), preferred_element_type=F32
        )
        first = (zs_ref[r].astype(F32) + gate_ref[here, :] * update).astype(BF16)
        z1_ref[here, :] = first
        n_ref[here, :] = layer_norm(first.astype(F32)).astype(BF16)
    step = 2 * count
    for m in range(rows * count // step):
        here = slice(m * step, (m + 1) * step)
        normed = n_ref[here, :]
        total = z1_ref[here, :].astype(F32)
        for j in range(trans // width):
            gate_w = w_ref[j * width : (j + 1) * width, :]
            up_w = w_ref[trans + j * width : trans + (j + 1) * width, :]
            gate = jnp.dot(normed, gate_w, preferred_element_type=F32)
            up = jnp.dot(normed, up_w, preferred_element_type=F32)
            act = (jax.nn.silu(gate) * up).astype(BF16)
            back_w = w_ref[parts + j * width : parts + (j + 1) * width, :]
            total = total + jnp.dot(act, back_w, preferred_element_type=F32)
        done = total.astype(BF16)
        out_ref[2 * m : 2 * m + 2] = done.reshape(2, count, width)
        if not last:
            n_ref[here, :] = layer_norm(done.astype(F32)).astype(BF16)
    if not last:
        following.wait()
        project(n_ref, wp_ref, valid, row_start, lr_ref, gate_out_ref, inner)


def fast_body(pair, valid_tokens, crop_order, w_proj, w_out, w_in, w_back):
    crops, rows, count, width = pair.shape
    peers = lax.axis_size("row")
    inner, trans = w_out.shape[1], w_back.shape[1]
    share = inner // peers
    wide = 2 * share
    blocks = lax.axis_size("section")
    swap = [(0, 1), (1, 0)]
    rest = jnp.concatenate(
        [
            w_in[0].reshape(width, 2 * trans // width, width).transpose(1, 0, 2).reshape(2 * trans, width),
            w_back[0],
            w_out[0],
        ],
        0,
    )
    wp_other = lax.ppermute(w_proj, "section", swap)
    rest_other = lax.ppermute(rest, "section", swap)

    smem = pl.BlockSpec(memory_space=pltpu.SMEM)
    vmem = pl.BlockSpec(memory_space=pltpu.VMEM)
    anywhere = pl.BlockSpec(memory_space=pl.ANY)
    sides = jax.ShapeDtypeStruct((peers, rows, wide, count), BF16)
    gates = jax.ShapeDtypeStruct((rows * count, width), F32)
    state = jax.ShapeDtypeStruct((rows, count, width), BF16)

    lr, gate = pl.pallas_call(
        functools.partial(first_kernel, inner),
        out_shape=(sides, gates),
        in_specs=[smem, smem, anywhere, anywhere, anywhere],
        out_specs=(vmem, vmem),
        scratch_shapes=[
            pltpu.VMEM((rows, count, width), BF16),
            pltpu.VMEM(w_proj.shape[1:], BF16),
            pltpu.VMEM((rows * count, width), BF16),
            pltpu.SemaphoreType.DMA((2,)),
        ],
        name="project_first",
    )(crop_order, valid_tokens, pair, w_proj, wp_other)

    z = pair
    for block in range(blocks):
        last = block == blocks - 1
        whole = lax.all_to_all(lr, "row", split_axis=0, concat_axis=0, tiled=True)
        tri_part = pl.pallas_call(
            tri_kernel,
            out_shape=jax.ShapeDtypeStruct((peers, share, rows, count), BF16),
            in_specs=[vmem],
            out_specs=vmem,
            scratch_shapes=[pltpu.VMEM((peers * rows * wide, count), F32)],
            name="triangle",
        )(whole)
        tri = lax.all_to_all(tri_part, "row", split_axis=0, concat_axis=0, tiled=True)
        scratch = [
            pltpu.VMEM((inner * rows, count), F32),
            pltpu.VMEM(rest.shape, BF16),
            pltpu.VMEM((rows * count, width), BF16),
            pltpu.VMEM((rows * count, width), BF16),
            pltpu.VMEM((rows, count, width), BF16),
            pltpu.SemaphoreType.DMA((3,)),
        ]
        if not last:
            scratch.append(pltpu.VMEM(w_proj.shape[1:], BF16))
        result = pl.pallas_call(
            functools.partial(update_kernel, block, blocks, inner, trans),
            out_shape=(state,) if last else (state, sides, gates),
            in_specs=[smem, smem, vmem, vmem] + [anywhere] * 5,
            out_specs=(vmem,) if last else (vmem,) * 3,
            scratch_shapes=scratch,
            name="update_last" if last else "update",
        )(crop_order, valid_tokens, tri, gate, z, rest, rest_other, w_proj, wp_other)
        if last:
            (z,) = result
        else:
            z, lr, gate = result
    return z[None]


def pair_block(state, valid, row_start, w_proj, w_out, w_in, w_back):
    rows_here, count, width = state.shape
    inner, trans = w_out.shape[0], w_back.shape[0]
    normed = layer_norm(state.astype(F32)).astype(BF16).reshape(rows_here * count, width)
    proj = jnp.dot(normed, w_proj, preferred_element_type=F32).reshape(rows_here, count, -1)
    keep_cols = (jnp.arange(count) < valid).astype(F32)
    keep_rows = (row_start + jnp.arange(rows_here) < valid).astype(F32)
    mask = keep_rows[:, None, None] * keep_cols[None, :, None]
    left = (mask * jax.nn.sigmoid(proj[..., inner : 2 * inner]) * proj[..., :inner]).astype(BF16)
    right = (
        mask * jax.nn.sigmoid(proj[..., 3 * inner : 4 * inner]) * proj[..., 2 * inner : 3 * inner]
    ).astype(BF16)
    gate = jax.nn.sigmoid(proj[..., 4 * inner :])
    left_whole = lax.all_to_all(left, "row", split_axis=2, concat_axis=0, tiled=True)
    right_whole = lax.all_to_all(right, "row", split_axis=2, concat_axis=0, tiled=True)
    tri_part = jnp.einsum("ikc,jkc->ijc", left_whole, right_whole, preferred_element_type=F32)
    tri = lax.all_to_all(
        tri_part.astype(BF16), "row", split_axis=0, concat_axis=2, tiled=True
    ).astype(F32)
    tri_normed = layer_norm(tri).astype(BF16).reshape(rows_here * count, inner)
    update = jnp.dot(tri_normed, w_out, preferred_element_type=F32).reshape(rows_here, count, width)
    first = (state.astype(F32) + gate * update).astype(BF16)
    second = layer_norm(first.astype(F32)).astype(BF16).reshape(rows_here * count, width)
    hidden = jnp.dot(second, w_in, preferred_element_type=F32)
    act = (jax.nn.silu(hidden[:, :trans]) * hidden[:, trans:]).astype(BF16)
    back = jnp.dot(act, w_back, preferred_element_type=F32).reshape(rows_here, count, width)
    return (first.astype(F32) + back).astype(BF16)


def general_body(pair, valid_tokens, crop_order, w_proj, w_out, w_in, w_back):
    crops, rows_here = pair.shape[:2]
    row_start = lax.axis_index("row") * rows_here
    share = crops // lax.axis_size("section")
    section = lax.axis_index("section")
    weights = [
        lax.all_gather(w, "section", axis=0, tiled=True) for w in (w_proj, w_out, w_in, w_back)
    ]
    blocks = weights[0].shape[0]

    def one_crop(index, outputs):
        crop = crop_order[section * share + index]
        valid = valid_tokens[crop]
        state = lax.dynamic_index_in_dim(pair, crop, 0, keepdims=False)

        def apply_block(block, value):
            return pair_block(value, valid, row_start, *[w[block] for w in weights])

        final = lax.fori_loop(0, blocks, apply_block, state)
        return lax.dynamic_update_index_in_dim(outputs, final, index, 0)

    empty = jnp.zeros((share,) + pair.shape[1:], BF16)
    return lax.fori_loop(0, share, one_crop, empty)


def solution(mesh):
    sections, peers = mesh.shape["section"], mesh.shape["row"]

    def body(pair, valid_tokens, crop_order, w_proj, w_out, w_in, w_back):
        crops, rows, count, width = pair.shape
        inner, trans = w_out.shape[1], w_back.shape[1]
        fits = (
            sections == 2
            and crops == sections
            and w_proj.shape[0] == 1
            and rows == 8
            and count == width == 128
            and inner == 4 * peers
            and trans % width == 0
        )
        run = fast_body if fits else general_body
        return run(pair, valid_tokens, crop_order, w_proj, w_out, w_in, w_back)

    weights = P("section", None, None)
    return jax.shard_map(
        body,
        mesh=mesh,
        in_specs=(P(None, "row", None, None), P(), P(), weights, weights, weights, weights),
        out_specs=P("section", "row", None, None),
        check_vma=False,
    )
```

time: 135 us -> 81.2 us (0.60)
  blocking collectives: 50.2 us -> 26.3 us
  Pallas kernels: 0 us -> 18.5 us
  local copies, waits for them, and re-layouts: 19.9 us -> 2.93 us
  waiting for transfers between devices: 31.3 us -> 18.3 us
  other arithmetic: 9.13 us -> 0.03 us
  matrix products: 4.56 us -> 0 us
  starting transfers between devices: 16.4 us -> 14.5 us
  between operations: 1.98 us -> 0.12 us
    all_gather x4 -> x0, blocking collectives: 29.2 us -> none  [the longest x1 13.2 us: on_device(): lax.all_gather(w_in, 'section', axis=0, tiled=True)]
    pallas_call x0 -> x5, Pallas kernels: none -> 18.5 us  [the longest x2 11.2 us: fast_body(): pl.pallas_call(functools.partial(update_kernel, block, blocks, inner, tra...]
    all_to_all x4 -> x2, waiting for transfers between devices: 31.3 us -> 15.3 us  [the longest x1 7.85 us: fast_body(): lax.all_to_all(tri_part, 'row', split_axis=0, concat_axis=0, tiled=True)]
    while x24 -> x0, local copies, waits for them, and re-layouts: 10.6 us -> none
    convert_element_type x12 -> x0, other arithmetic: 6.87 us -> none  [the longest x2 2.51 us: pair_block(): right = (mask * jax.nn.sigmoid(proj[..., 3 * inner:4 * inner]) * proj[......]
    all_to_all x4 -> x2, starting transfers between devices: 16.4 us -> 9.87 us  [the longest x1 6.36 us: fast_body(): whole = lax.all_to_all(lr, 'row', split_axis=0, concat_axis=0, tiled=True)]
    all_to_all x2, blocking collectives: 21 us -> 26.3 us  [the longest x1 14.2 us: fast_body(): whole = lax.all_to_all(lr, 'row', split_axis=0, concat_axis=0, tiled=True)]
    ppermute x0 -> x2, starting transfers between devices: none -> 4.58 us  [the longest x1 3 us: fast_body(): wp_other = lax.ppermute(w_proj, 'section', swap)]
  transfers between devices with their start and end apart: 4 -> 4, of which waited for: 4 -> 3; matrix products, arithmetic and copies ran while one was open for 0% -> 0% of each run, Pallas kernels for 0% -> 2%
where the time goes in v1:
time: 81.2 us; the launch traced here: 80.5 us
  blocking collectives  26.3 us (32%)
  Pallas kernels  18.5 us (23%)
  waiting for transfers between devices  18.3 us (23%)
  starting transfers between devices  14.5 us (18%)
  local copies, waits for them, and re-layouts  2.93 us (4%)
    all_to_all x1, blocking collectives, fast_body(): whole = lax.all_to_all(lr, 'row', split_axis=0, concat_axis=0, tiled=True)  14.2 us
    all_to_all x1, blocking collectives, fast_body(): lax.all_to_all(tri_part, 'row', split_axis=0, concat_axis=0, tiled=True)  12.1 us
    pallas_call x2, Pallas kernels, fast_body(): pl.pallas_call(functools.partial(update_kernel, block, blocks, inner, tra...  11.2 us
    all_to_all x1, waiting for transfers between devices, fast_body(): lax.all_to_all(tri_part, 'row', split_axis=0, concat_axis=0, tiled=True)  7.85 us
    all_to_all x1, waiting for transfers between devices, fast_body(): whole = lax.all_to_all(lr, 'row', split_axis=0, concat_axis=0, tiled=True)  7.42 us
    all_to_all x1, starting transfers between devices, fast_body(): whole = lax.all_to_all(lr, 'row', split_axis=0, concat_axis=0, tiled=True)  6.36 us
    pallas_call x2, Pallas kernels, fast_body(): pl.pallas_call(tri_kernel, out_shape=jax.ShapeDtypeStruct((peers, share,...  3.67 us
    pallas_call x1, Pallas kernels, fast_body(): pl.pallas_call(functools.partial(first_kernel, inner), out_shape=(sides,...  3.61 us
  transfers between devices with their start and end apart: 4, of which 3 were waited for; matrix products, arithmetic and copies ran while one was open for 0% of the time, Pallas kernels for 2%

profile of v1, /device:TPU:0, one launch (start us, length us, event | category | flops | bytes accessed | tf_op | source)
XLA Modules:
  0.0 80.5 jit_solution(9001464931423066459)
XLA Ops:
  0.0 3.0 %collective-permute-start = (bf16[1,128,384]{2,1,0:T(8,128)(2,1)}, bf16[1,128,384]{2,1,0:T(8,128)(2,1)S(1)}, u32[]{:S(2)}, u32[]{:S(2)}) collective-permute-start(bf16[1,128,384]{2,1,0:T(8,128)(2,1)} %wp_own_ref.3), channel_id=1, source_target_pairs={{0,16},{16,0},{1,17},{17,1},{2,18},{18,2},{3,19},{19,3},{4,20},{20... | collective-permute-start | bytes 294920 | tf_op jit(solution)/shard_map/ppermute | solution.py:188
  3.0 3.0 %collective-permute-done.other_ref.wp_other_ref = bf16[1,128,384]{2,1,0:T(8,128)(2,1)S(1)} collective-permute-done((bf16[1,128,384]{2,1,0:T(8,128)(2,1)}, bf16[1,128,384]{2,1,0:T(8,128)(2,1)S(1)}, u32[]{:S(2)}, u32[]{:S(2)}) %collective-permute-start) | collective-permute-done | bytes 98336 | tf_op jit(solution)/shard_map/ppermute | solution.py:188
  6.0 0.0 copy-start.3
  6.0 0.6 copy-done.3
  6.6 3.6 %project_first.1 = (bf16[16,8,8,128]{3,2,1,0:T(8,128)(2,1)}, f32[1024,128]{1,0:T(8,128)}) custom-call(s32[2]{0:T(128)} %order_ref.5, s32[2]{0:T(128)} %valid_ref.5, bf16[2,8,128,128]{3,2,1,0:T(8,128)(2,1)} %z_ref.1, bf16[1,128,384]{2,1,0:T(8,128)(2,1)} %wp_own_ref.3, bf16[1,128,384]{2,1,0:T(8,128)(2,1)} %copy-done.3), custom_call_target="tpu_custom_call" | custom-call | tf_op jit(solution)/shard_map/project_first/pallas_call | solution.py:198
  10.3 0.0 copy-start.5
  10.3 6.4 %all-to-all-start = ((bf16[16,8,8,128]{3,2,1,0:T(8,128)(2,1)}), bf16[16,8,8,128]{3,2,1,0:T(8,128)(2,1)S(1)}, u32[]{:S(2)}, u32[]{:S(2)}) async-start(bf16[16,8,8,128]{3,2,1,0:T(8,128)(2,1)} %get-tuple-element.10), calls=%async_computation | async-start | bytes 524288 | tf_op jit(solution)/shard_map/all_to_all | solution.py:215
  16.6 0.0 copy-done.5
  16.7 0.0 copy-start.6
  16.7 0.0 copy-start.7
  16.8 0.8 %copy-done.6 = bf16[1,512,128]{2,1,0:T(8,128)(2,1)S(1)} copy-done((bf16[1,512,128]{2,1,0:T(8,128)(2,1)S(1)}, bf16[1,512,128]{2,1,0:T(8,128)(2,1)}, u32[]{:S(2)}) %copy-start.6) | copy-done | bytes 131096
  17.6 0.0 copy-done.7
  17.6 0.0 copy-start
  17.7 1.6 %collective-permute-start.1 = (bf16[1600,128]{1,0:T(8,128)(2,1)S(1)}, bf16[1600,128]{1,0:T(8,128)(2,1)S(1)}, u32[]{:S(2)}, u32[]{:S(2)}) collective-permute-start(bf16[1600,128]{1,0:T(8,128)(2,1)S(1)} %pad_maximum_fusion.own_ref), channel_id=1, source_target_pairs={{0,16},{16,0},{1,17},{17,1},{2,18},{18,2},{3,19},{19,3},{4,20},{20... | collective-permute-start | bytes 1228808 | tf_op jit(solution)/shard_map/ppermute | solution.py:189
  19.2 7.4 %all-to-all-done.in_ref = bf16[16,8,8,128]{3,2,1,0:T(8,128)(2,1)S(1)} async-done(((bf16[16,8,8,128]{3,2,1,0:T(8,128)(2,1)}), bf16[16,8,8,128]{3,2,1,0:T(8,128)(2,1)S(1)}, u32[]{:S(2)}, u32[]{:S(2)}) %all-to-all-start) | async-done | bytes 262176 | tf_op jit(solution)/shard_map/all_to_all | solution.py:215
  26.7 0.0 copy-start.2
  26.7 0.7 copy-done.2
  27.4 1.8 %triangle.2 = bf16[16,4,8,128]{3,2,1,0:T(8,128)(2,1)} custom-call(bf16[16,8,8,128]{3,2,1,0:T(8,128)(2,1)} %copy-done.2), custom_call_target="tpu_custom_call" | custom-call | tf_op jit(solution)/shard_map/triangle/pallas_call | solution.py:216
  29.2 3.5 %all-to-all-start.1 = ((bf16[16,4,8,128]{3,2,1,0:T(8,128)(2,1)}), bf16[16,4,8,128]{3,2,1,0:T(8,128)(2,1)S(1)}, u32[]{:S(2)}, u32[]{:S(2)}) async-start(bf16[16,4,8,128]{3,2,1,0:T(8,128)(2,1)} %triangle.2), calls=%async_computation.1 | async-start | bytes 262144 | tf_op jit(solution)/shard_map/all_to_all | solution.py:224
  32.7 0.0 collective-permute-done.1.other_ref
  32.7 0.0 copy-start.1
  32.7 7.9 %all-to-all-done.1.tri_ref = bf16[16,4,8,128]{3,2,1,0:T(8,128)(2,1)S(1)} async-done(((bf16[16,4,8,128]{3,2,1,0:T(8,128)(2,1)}), bf16[16,4,8,128]{3,2,1,0:T(8,128)(2,1)S(1)}, u32[]{:S(2)}, u32[]{:S(2)}) %all-to-all-start.1) | async-done | bytes 131104 | tf_op jit(solution)/shard_map/all_to_all | solution.py:224
  40.6 0.0 copy-start.4
  40.6 0.0 copy-done
  40.6 0.0 copy-done.1
  40.6 0.6 copy-done.4
  41.2 6.0 %update.1 = (bf16[8,128,128]{2,1,0:T(8,128)(2,1)}, bf16[16,8,8,128]{3,2,1,0:T(8,128)(2,1)}, f32[1024,128]{1,0:T(8,128)}) custom-call(s32[2]{0:T(128)} %order_ref.5, s32[2]{0:T(128)} %valid_ref.5, bf16[16,4,8,128]{3,2,1,0:T(8,128)(2,1)} %copy-done.4, f32[1024,128]{1,0:T(8,128)} %get-tuple-element.11.gate_ref, bf16[2,8,128,128]{3,2,1,0:T(8,128)(2,1)} %z_ref.1, ...), custom_call_target="tpu_custom_call" | custom-call | tf_op jit(solution)/shard_map/update/pallas_call | solution.py:235
  47.3 14.2 %all_to_all.20.in_ref = bf16[16,8,8,128]{3,2,1,0:T(8,128)(2,1)} all-to-all(bf16[16,8,8,128]{3,2,1,0:T(8,128)(2,1)} %get-tuple-element.12), channel_id=1, replica_groups=mesh['section'=2,'row'=16] {'row'}, dimensions={0} | all-to-all | bytes 524288 | tf_op jit(solution)/shard_map/all_to_all | solution.py:215
  61.5 1.8 %triangle.3 = bf16[16,4,8,128]{3,2,1,0:T(8,128)(2,1)} custom-call(bf16[16,8,8,128]{3,2,1,0:T(8,128)(2,1)} %all_to_all.20.in_ref), custom_call_target="tpu_custom_call" | custom-call | tf_op jit(solution)/shard_map/triangle/pallas_call | solution.py:216
  63.3 12.1 %all_to_all.21.tri_ref = bf16[16,4,8,128]{3,2,1,0:T(8,128)(2,1)} all-to-all(bf16[16,4,8,128]{3,2,1,0:T(8,128)(2,1)} %triangle.3), channel_id=1, replica_groups=mesh['section'=2,'row'=16] {'row'}, dimensions={0} | all-to-all | bytes 262144 | tf_op jit(solution)/shard_map/all_to_all | solution.py:224
  75.4 5.2 %update_last.1 = bf16[8,128,128]{2,1,0:T(8,128)(2,1)} custom-call(s32[2]{0:T(128)} %order_ref.5, s32[2]{0:T(128)} %valid_ref.5, bf16[16,4,8,128]{3,2,1,0:T(8,128)(2,1)} %all_to_all.21.tri_ref, f32[1024,128]{1,0:T(8,128)} %get-tuple-element.13.gate_ref, bf16[8,128,128]{2,1,0:T(8,128)(2,1)} %get-tuple-element.14.z_ref, bf16[1600,128]{1,0:T(8,128)(2,1)} %copy-done, ...), custom_call_target="tpu_custom_call" | custom-call | tf_op jit(solution)/shard_map/update_last/pallas_call | solution.py:235
  (3 shorter events, 0.1 us)
Async XLA Ops:
  0.0 6.0 %collective-permute-start = (bf16[1,128,384]{2,1,0:T(8,128)(2,1)}, bf16[1,128,384]{2,1,0:T(8,128)(2,1)S(1)}, u32[]{:S(2)}, u32[]{:S(2)}) collective-permute-start(bf16[1,128,384]{2,1,0:T(8,128)(2,1)} %wp_own_ref.3), channel_id=1, source_target_pairs={{0,16},{16,0},{1,17},{17,1},{2,18},{18,2},{3,19},{19,3},{4,20},{20... | collective-permute-start | bytes 294920 | tf_op jit(solution)/shard_map/ppermute | solution.py:188
  6.0 0.6 copy-start.3
  10.3 6.4 %copy-start.5 = (bf16[1,128,1024]{2,1,0:T(8,128)(2,1)S(1)}, bf16[1,128,1024]{2,1,0:T(8,128)(2,1)}, u32[]{:S(2)}) copy-start(bf16[1,128,1024]{2,1,0:T(8,128)(2,1)} %param.12) | copy-start | bytes 786436
  10.3 16.4 %all-to-all-start = ((bf16[16,8,8,128]{3,2,1,0:T(8,128)(2,1)}), bf16[16,8,8,128]{3,2,1,0:T(8,128)(2,1)S(1)}, u32[]{:S(2)}, u32[]{:S(2)}) async-start(bf16[16,8,8,128]{3,2,1,0:T(8,128)(2,1)} %get-tuple-element.10), calls=%async_computation | async-start | bytes 524288 | tf_op jit(solution)/shard_map/all_to_all | solution.py:215
  16.7 0.9 %copy-start.6 = (bf16[1,512,128]{2,1,0:T(8,128)(2,1)S(1)}, bf16[1,512,128]{2,1,0:T(8,128)(2,1)}, u32[]{:S(2)}) copy-start(bf16[1,512,128]{2,1,0:T(8,128)(2,1)} %param.13) | copy-start | bytes 393220
  16.7 0.9 %copy-start.7 = (bf16[1,64,128]{2,1,0:T(8,128)(2,1)S(1)}, bf16[1,64,128]{2,1,0:T(8,128)(2,1)}, u32[]{:S(2)}) copy-start(bf16[1,64,128]{2,1,0:T(8,128)(2,1)} %param.11) | copy-start | bytes 49156
  17.6 22.9 %copy-start = (bf16[1600,128]{1,0:T(8,128)(2,1)}, bf16[1600,128]{1,0:T(8,128)(2,1)S(1)}, u32[]{:S(2)}) copy-start(bf16[1600,128]{1,0:T(8,128)(2,1)S(1)} %pad_maximum_fusion.own_ref) | copy-start | bytes 1228804
  17.7 15.1 %collective-permute-start.1 = (bf16[1600,128]{1,0:T(8,128)(2,1)S(1)}, bf16[1600,128]{1,0:T(8,128)(2,1)S(1)}, u32[]{:S(2)}, u32[]{:S(2)}) collective-permute-start(bf16[1600,128]{1,0:T(8,128)(2,1)S(1)} %pad_maximum_fusion.own_ref), channel_id=1, source_target_pairs={{0,16},{16,0},{1,17},{17,1},{2,18},{18,2},{3,19},{19,3},{4,20},{20... | collective-permute-start | bytes 1228808 | tf_op jit(solution)/shard_map/ppermute | solution.py:189
  26.7 0.7 copy-start.2
  29.2 11.4 %all-to-all-start.1 = ((bf16[16,4,8,128]{3,2,1,0:T(8,128)(2,1)}), bf16[16,4,8,128]{3,2,1,0:T(8,128)(2,1)S(1)}, u32[]{:S(2)}, u32[]{:S(2)}) async-start(bf16[16,4,8,128]{3,2,1,0:T(8,128)(2,1)} %triangle.2), calls=%async_computation.1 | async-start | bytes 262144 | tf_op jit(solution)/shard_map/all_to_all | solution.py:224
  32.7 7.9 %copy-start.1 = (bf16[1600,128]{1,0:T(8,128)(2,1)}, bf16[1600,128]{1,0:T(8,128)(2,1)S(1)}, u32[]{:S(2)}) copy-start(bf16[1600,128]{1,0:T(8,128)(2,1)S(1)} %collective-permute-done.1.other_ref) | copy-start | bytes 1228804
  40.6 0.6 copy-start.4

commit v2 on v1

--- a/solution.py
+++ b/solution.py
@@ -9,6 +9,7 @@
 
 F32 = jnp.float32
 BF16 = jnp.bfloat16
+LIMIT = pltpu.CompilerParams(vmem_limit_bytes=16 * 2**20)
 
 
 def layer_norm(value, axis=-1):
@@ -44,41 +45,92 @@
     ).astype(BF16)
 
 
-def project(normed_ref, w_ref, valid, row_start, lr_ref, gate_ref, inner):
+def project(normed_ref, w_ref, keep_ref, lr_ref, inner):
     peers, rows, wide, count = lr_ref.shape
     turned = ordered_weights(w_ref[:, : 4 * inner], inner, wide // 2)
-    gate_w = w_ref[:, 4 * inner :]
-    column = lax.broadcasted_iota(jnp.int32, (1, count), 1)
     for r in range(rows):
         normed = normed_ref[r * count : (r + 1) * count, :]
         proj = lax.dot_general(
             turned, normed, (((1,), (1,)), ((), ())), preferred_element_type=F32
         )
-        keep = jnp.logical_and(column < valid, row_start + r < valid)
-        mask = jnp.where(keep, 1.0, 0.0)
+        mask = keep_ref[r : r + 1, :]
         sides = mask * jax.nn.sigmoid(proj[2 * inner :]) * proj[: 2 * inner]
         lr_ref[:, r] = sides.reshape(peers, wide, count).astype(BF16)
-        gate_ref[r * count : (r + 1) * count, :] = jax.nn.sigmoid(
-            jnp.dot(normed, gate_w, preferred_element_type=F32)
-        )
-
-
-def first_kernel(
-    inner, order_ref, valid_ref, pair_ref, own_ref, other_ref, lr_ref, gate_ref, z_ref, w_ref, n_ref, sems
+
+
+def output_gates(normed_ref, w_ref, gate_ref, inner):
+    step = 256
+    for m in range(normed_ref.shape[0] // step):
+        here = slice(m * step, (m + 1) * step)
+        gate_ref[here, :] = jax.nn.sigmoid(
+            jnp.dot(normed_ref[here, :], w_ref[:, 4 * inner :], preferred_element_type=F32)
+        )
+
+
+def prepare_kernel(
+    order_ref,
+    valid_ref,
+    pair_ref,
+    w_in_ref,
+    w_back_ref,
+    w_out_ref,
+    z_ref,
+    n_ref,
+    keep_ref,
+    rest_ref,
+    order_s,
+    valid_s,
+    both_ref,
+    sems,
 ):
-    section = lax.axis_index("section")
-    rows, count = pair_ref.shape[1:3]
-    row_start = lax.axis_index("row") * rows
-    crop = order_ref[section]
-    valid = valid_ref[crop]
-    state = pltpu.make_async_copy(pair_ref.at[crop], z_ref, sems.at[0])
+    rows, count, width = z_ref.shape
+    trans = w_back_ref.shape[1]
+    scalars = [
+        pltpu.make_async_copy(order_ref, order_s, sems.at[0]),
+        pltpu.make_async_copy(valid_ref, valid_s, sems.at[1]),
+    ]
+    state = pltpu.make_async_copy(pair_ref, both_ref, sems.at[2])
+    for copy in scalars:
+        copy.start()
     state.start()
-    weights = fetch(section == 0, own_ref.at[0], other_ref.at[0], w_ref, sems.at[1])
+    parts = 2 * trans // width
+    sources = [w_in_ref.at[0, :, pl.ds(j * width, width)] for j in range(parts)]
+    sources += [w_back_ref.at[0], w_out_ref.at[0]]
+    packing, at = [], 0
+    for i, source in enumerate(sources):
+        size = source.shape[0]
+        packing.append(
+            pltpu.make_async_copy(source, rest_ref.at[pl.ds(at, size)], sems.at[3 + i])
+        )
+        packing[-1].start()
+        at += size
+    for copy in scalars:
+        copy.wait()
+    crop = order_s[lax.axis_index("section")]
+    valid = valid_s[crop]
+    row = lax.axis_index("row") * rows + lax.broadcasted_iota(jnp.int32, (rows, count), 0)
+    column = lax.broadcasted_iota(jnp.int32, (rows, count), 1)
+    keep = jnp.logical_and(row < valid, column < valid)
+    keep_ref[...] = jnp.where(keep, 1.0, 0.0)
     state.wait()
     for r in range(rows):
-        n_ref[r * count : (r + 1) * count, :] = layer_norm(z_ref[r].astype(F32)).astype(BF16)
-    weights.wait()
-    project(n_ref, w_ref, valid, row_start, lr_ref, gate_ref, inner)
+        here = both_ref[crop, r]
+        z_ref[r] = here
+        n_ref[r * count : (r + 1) * count, :] = layer_norm(here.astype(F32)).astype(BF16)
+    for copy in packing:
+        copy.wait()
+
+
+def project_kernel(inner, n_ref, keep_ref, own_ref, other_ref, lr_ref, w_ref, sems):
+    section = lax.axis_index("section")
+    fetch(section == 0, own_ref.at[0], other_ref.at[0], w_ref, sems.at[0]).wait()
+    project(n_ref, w_ref, keep_ref, lr_ref, inner)
+
+
+def gates_kernel(inner, n_ref, own_ref, other_ref, gate_ref, w_ref, sems):
+    section = lax.axis_index("section")
+    fetch(section == 0, own_ref.at[0], other_ref.at[0], w_ref, sems.at[0]).wait()
+    output_gates(n_ref, w_ref, gate_ref, inner)
 
 
 def tri_kernel(in_ref, out_ref, wide_ref):
@@ -100,8 +152,7 @@
     blocks,
     inner,
     trans,
-    order_ref,
-    valid_ref,
+    keep_ref,
     tri_ref,
     gate_ref,
     z_ref,
@@ -113,30 +164,21 @@
 ):
     last = block == blocks - 1
     if last:
-        out_ref, t_ref, w_ref, n_ref, z1_ref, zs_ref, sems = refs
+        out_ref, t_ref, w_ref, n_ref, z1_ref, sems = refs
     else:
-        out_ref, lr_ref, gate_out_ref, t_ref, w_ref, n_ref, z1_ref, zs_ref, sems, wp_ref = refs
+        out_ref, lr_ref, gate_out_ref, t_ref, w_ref, n_ref, z1_ref, sems, wp_ref = refs
     section = lax.axis_index("section")
     rows, count, width = out_ref.shape
-    row_start = lax.axis_index("row") * rows
-    crop = order_ref[section]
-    valid = valid_ref[crop]
-    if block == 0:
-        state = pltpu.make_async_copy(z_ref.at[crop], zs_ref, sems.at[0])
-    else:
-        state = pltpu.make_async_copy(z_ref, zs_ref, sems.at[0])
-    state.start()
-    weights = fetch(section == block, own_ref, other_ref, w_ref, sems.at[1])
+    weights = fetch(section == block, own_ref, other_ref, w_ref, sems.at[0])
     if not last:
         following = fetch(
-            section == block + 1, wp_own_ref.at[0], wp_other_ref.at[0], wp_ref, sems.at[2]
+            section == block + 1, wp_own_ref.at[0], wp_other_ref.at[0], wp_ref, sems.at[1]
         )
     parts = width * (2 * trans // width)
     t_ref[...] = layer_norm(tri_ref[...].reshape(inner, rows, count).astype(F32), 0).reshape(
         inner * rows, count
     )
     weights.wait()
-    state.wait()
     w_out = w_ref[parts + trans : parts + trans + inner, :]
     for r in range(rows):
         here = slice(r * count, (r + 1) * count)
@@ -144,7 +186,7 @@
         update = lax.dot_general(
             tri, w_out, (((0,), (0,)), ((), ())), preferred_element_type=F32
         )
-        first = (zs_ref[r].astype(F32) + gate_ref[here, :] * update).astype(BF16)
+        first = (z_ref[r].astype(F32) + gate_ref[here, :] * update).astype(BF16)
         z1_ref[here, :] = first
         n_ref[here, :] = layer_norm(first.astype(F32)).astype(BF16)
     step = 2 * count
@@ -166,7 +208,8 @@
             n_ref[here, :] = layer_norm(done.astype(F32)).astype(BF16)
     if not last:
         following.wait()
-        project(n_ref, wp_ref, valid, row_start, lr_ref, gate_out_ref, inner)
+        project(n_ref, wp_ref, keep_ref, lr_ref, inner)
+        output_gates(n_ref, wp_ref, gate_out_ref, inner)
 
 
 def fast_body(pair, valid_tokens, crop_order, w_proj, w_out, w_in, w_back):
@@ -177,39 +220,60 @@
     wide = 2 * share
     blocks = lax.axis_size("section")
     swap = [(0, 1), (1, 0)]
-    rest = jnp.concatenate(
-        [
-            w_in[0].reshape(width, 2 * trans // width, width).transpose(1, 0, 2).reshape(2 * trans, width),
-            w_back[0],
-            w_out[0],
-        ],
-        0,
-    )
-    wp_other = lax.ppermute(w_proj, "section", swap)
-    rest_other = lax.ppermute(rest, "section", swap)
-
-    smem = pl.BlockSpec(memory_space=pltpu.SMEM)
+    rest_rows = 2 * trans + trans + inner
+
     vmem = pl.BlockSpec(memory_space=pltpu.VMEM)
+    hbm = pl.BlockSpec(memory_space=pltpu.HBM)
     anywhere = pl.BlockSpec(memory_space=pl.ANY)
     sides = jax.ShapeDtypeStruct((peers, rows, wide, count), BF16)
     gates = jax.ShapeDtypeStruct((rows * count, width), F32)
     state = jax.ShapeDtypeStruct((rows, count, width), BF16)
-
-    lr, gate = pl.pallas_call(
-        functools.partial(first_kernel, inner),
-        out_shape=(sides, gates),
-        in_specs=[smem, smem, anywhere, anywhere, anywhere],
-        out_specs=(vmem, vmem),
+    tokens = jax.ShapeDtypeStruct((rows * count, width), BF16)
+
+    wp_other = lax.ppermute(w_proj, "section", swap)
+    z, normed, keep, rest = pl.pallas_call(
+        prepare_kernel,
+        out_shape=(
+            state,
+            tokens,
+            jax.ShapeDtypeStruct((rows, count), F32),
+            jax.ShapeDtypeStruct((rest_rows, width), BF16),
+        ),
+        in_specs=[hbm] * 6,
+        out_specs=(vmem,) * 4,
         scratch_shapes=[
-            pltpu.VMEM((rows, count, width), BF16),
-            pltpu.VMEM(w_proj.shape[1:], BF16),
-            pltpu.VMEM((rows * count, width), BF16),
-            pltpu.SemaphoreType.DMA((2,)),
+            pltpu.SMEM(crop_order.shape, jnp.int32),
+            pltpu.SMEM(valid_tokens.shape, jnp.int32),
+            pltpu.VMEM(pair.shape, BF16),
+            pltpu.SemaphoreType.DMA((5 + 2 * trans // width,)),
         ],
-        name="project_first",
-    )(crop_order, valid_tokens, pair, w_proj, wp_other)
-
-    z = pair
+        compiler_params=LIMIT,
+        cost_estimate=pl.CostEstimate(flops=10**6, bytes_accessed=3 * 10**6, transcendentals=0),
+        name="prepare",
+    )(*[pltpu.with_memory_space_constraint(x, pltpu.HBM) for x in (crop_order, valid_tokens, pair, w_in, w_back, w_out)])
+    rest_other = lax.ppermute(rest, "section", swap)
+
+    weights = pltpu.VMEM(w_proj.shape[1:], BF16)
+    lr = pl.pallas_call(
+        functools.partial(project_kernel, inner),
+        out_shape=sides,
+        in_specs=[vmem, vmem, anywhere, anywhere],
+        out_specs=vmem,
+        scratch_shapes=[weights, pltpu.SemaphoreType.DMA((1,))],
+        compiler_params=LIMIT,
+        name="project",
+    )(normed, keep, w_proj, wp_other)
+    gate = pl.pallas_call(
+        functools.partial(gates_kernel, inner),
+        out_shape=gates,
+        in_specs=[vmem, anywhere, anywhere],
+        out_specs=vmem,
+        scratch_shapes=[weights, pltpu.SemaphoreType.DMA((1,))],
+        compiler_params=LIMIT,
+        cost_estimate=pl.CostEstimate(flops=34 * 10**6, bytes_accessed=10**6, transcendentals=2 * 10**5),
+        name="gates",
+    )(normed, w_proj, wp_other)
+
     for block in range(blocks):
         last = block == blocks - 1
         whole = lax.all_to_all(lr, "row", split_axis=0, concat_axis=0, tiled=True)
@@ -219,27 +283,28 @@
             in_specs=[vmem],
             out_specs=vmem,
             scratch_shapes=[pltpu.VMEM((peers * rows * wide, count), F32)],
+            compiler_params=LIMIT,
             name="triangle",
         )(whole)
         tri = lax.all_to_all(tri_part, "row", split_axis=0, concat_axis=0, tiled=True)
         scratch = [
             pltpu.VMEM((inner * rows, count), F32),
-            pltpu.VMEM(rest.shape, BF16),
+            pltpu.VMEM((rest_rows, width), BF16),
             pltpu.VMEM((rows * count, width), BF16),
             pltpu.VMEM((rows * count, width), BF16),
-            pltpu.VMEM((rows, count, width), BF16),
-            pltpu.SemaphoreType.DMA((3,)),
+            pltpu.SemaphoreType.DMA((2,)),
         ]
         if not last:
             scratch.append(pltpu.VMEM(w_proj.shape[1:], BF16))
         result = pl.pallas_call(
             functools.partial(update_kernel, block, blocks, inner, trans),
             out_shape=(state,) if last else (state, sides, gates),
-            in_specs=[smem, smem, vmem, vmem] + [anywhere] * 5,
+            in_specs=[vmem] * 4 + [anywhere] * 4,
             out_specs=(vmem,) if last else (vmem,) * 3,
             scratch_shapes=scratch,
+            compiler_params=LIMIT,
             name="update_last" if last else "update",
-        )(crop_order, valid_tokens, tri, gate, z, rest, rest_other, w_proj, wp_other)
+        )(keep, tri, gate, z, rest, rest_other, w_proj, wp_other)
         if last:
             (z,) = result
         else:

time: 81.2 us -> 66.4 us (0.82)
  Pallas kernels: 18.5 us -> 11.2 us
  blocking collectives: 26.3 us -> 23.2 us
  local copies, waits for them, and re-layouts: 2.93 us -> 0.01 us
  waiting for transfers between devices: 18.3 us -> 17.3 us
    pallas_call x2, Pallas kernels: 11.2 us -> 6.69 us  [fast_body(): pl.pallas_call(functools.partial(update_kernel, block, blocks, inner, tra...]
    unnamed x17 -> x2, local copies, waits for them, and re-layouts: 2.9 us -> 0.01 us
    pallas_call x2, Pallas kernels: 3.67 us -> 1.12 us  [fast_body(): pl.pallas_call(tri_kernel, out_shape=jax.ShapeDtypeStruct((peers, share,...]
    ppermute x1, waiting for transfers between devices: 3 us -> 1.36 us  [fast_body(): wp_other = lax.ppermute(w_proj, 'section', swap)]
    all_to_all x1, blocking collectives: 14.2 us -> 12.6 us  [fast_body(): whole = lax.all_to_all(lr, 'row', split_axis=0, concat_axis=0, tiled=True)]
    all_to_all x1, blocking collectives: 12.1 us -> 10.6 us  [fast_body(): lax.all_to_all(tri_part, 'row', split_axis=0, concat_axis=0, tiled=True)]
    all_to_all x1, waiting for transfers between devices: 7.42 us -> 8.43 us  [fast_body(): whole = lax.all_to_all(lr, 'row', split_axis=0, concat_axis=0, tiled=True)]
    pallas_call x1 -> x3, Pallas kernels: 3.61 us -> 3.39 us  [the longest x1 1.71 us: fast_body(): pl.pallas_call(prepare_kernel, out_shape=(state, tokens, jax.ShapeDtypeSt...]
  transfers between devices with their start and end apart: 4 -> 4, of which waited for: 3 -> 3; matrix products, arithmetic and copies ran while one was open for 0% -> 0% of each run, Pallas kernels for 2% -> 5%
where the time goes in v2:
time: 66.4 us; the launch traced here: 66 us
  blocking collectives  23.2 us (35%)
  waiting for transfers between devices  17.3 us (26%)
  starting transfers between devices  14.2 us (21%)
  Pallas kernels  11.2 us (17%)
    all_to_all x1, blocking collectives, fast_body(): whole = lax.all_to_all(lr, 'row', split_axis=0, concat_axis=0, tiled=True)  12.6 us
    all_to_all x1, blocking collectives, fast_body(): lax.all_to_all(tri_part, 'row', split_axis=0, concat_axis=0, tiled=True)  10.6 us
    all_to_all x1, waiting for transfers between devices, fast_body(): whole = lax.all_to_all(lr, 'row', split_axis=0, concat_axis=0, tiled=True)  8.43 us
    all_to_all x1, waiting for transfers between devices, fast_body(): lax.all_to_all(tri_part, 'row', split_axis=0, concat_axis=0, tiled=True)  7.48 us
    pallas_call x2, Pallas kernels, fast_body(): pl.pallas_call(functools.partial(update_kernel, block, blocks, inner, tra...  6.69 us
    all_to_all x1, starting transfers between devices, fast_body(): whole = lax.all_to_all(lr, 'row', split_axis=0, concat_axis=0, tiled=True)  6.16 us
    all_to_all x1, starting transfers between devices, fast_body(): lax.all_to_all(tri_part, 'row', split_axis=0, concat_axis=0, tiled=True)  3.51 us
    ppermute x1, starting transfers between devices, fast_body(): wp_other = lax.ppermute(w_proj, 'section', swap)  3 us
  transfers between devices with their start and end apart: 4, of which 3 were waited for; matrix products, arithmetic and copies ran while one was open for 0% of the time, Pallas kernels for 5%

profile of v2, /device:TPU:0, one launch (start us, length us, event | category | flops | bytes accessed | tf_op | source)
XLA Modules:
  0.0 66.0 jit_solution(14192186033492397338)
XLA Ops:
  0.0 0.0 copy-start
  0.0 3.0 %collective-permute-start = (bf16[1,128,384]{2,1,0:T(8,128)(2,1)}, bf16[1,128,384]{2,1,0:T(8,128)(2,1)S(1)}, u32[]{:S(2)}, u32[]{:S(2)}) collective-permute-start(bf16[1,128,384]{2,1,0:T(8,128)(2,1)} %wp_own_ref.3), channel_id=1, source_target_pairs={{0,16},{16,0},{1,17},{17,1},{2,18},{18,2},{3,19},{19,3},{4,20},{20... | collective-permute-start | bytes 294920 | tf_op jit(solution)/shard_map/ppermute | solution.py:233
  3.0 1.7 %prepare.1 = (bf16[8,128,128]{2,1,0:T(8,128)(2,1)S(1)}, bf16[1024,128]{1,0:T(8,128)(2,1)S(1)}, f32[8,128]{1,0:T(8,128)S(1)}, bf16[1600,128]{1,0:T(8,128)(2,1)S(1)}) custom-call(s32[2]{0:T(128)} %order_ref.1, s32[2]{0:T(128)} %valid_ref.1, bf16[2,8,128,128]{3,2,1,0:T(8,128)(2,1)} %pair_ref.1, bf16[1,128,1024]{2,1,0:T(8,128)(2,1)} %w_in_ref.1, ...), custom_call_target="tpu_custom_call" | custom-call | flops 1000000 | bytes 3000000 | tf_op jit(solution)/shard_map/prepare/pallas_call | solution.py:234
  4.7 1.4 %collective-permute-done.other_ref.wp_other_ref = bf16[1,128,384]{2,1,0:T(8,128)(2,1)S(1)} collective-permute-done((bf16[1,128,384]{2,1,0:T(8,128)(2,1)}, bf16[1,128,384]{2,1,0:T(8,128)(2,1)S(1)}, u32[]{:S(2)}, u32[]{:S(2)}) %collective-permute-start) | collective-permute-done | bytes 98336 | tf_op jit(solution)/shard_map/ppermute | solution.py:233
  6.1 0.0 copy-done
  6.1 1.3 %project.1 = bf16[16,8,8,128]{3,2,1,0:T(8,128)(2,1)} custom-call(bf16[1024,128]{1,0:T(8,128)(2,1)S(1)} %get-tuple-element.13.n_ref, f32[8,128]{1,0:T(8,128)S(1)} %get-tuple-element.12.keep_ref, bf16[1,128,384]{2,1,0:T(8,128)(2,1)S(1)} %copy-done, bf16[1,128,384]{2,1,0:T(8,128)(2,1)S(1)} %collective-permute-done.other_ref.wp_other_ref), custom_call_target="tpu_custom_call" | custom-call | tf_op jit(solution)/shard_map/project/pallas_call | solution.py:257
  7.4 6.2 %all-to-all-start = ((bf16[16,8,8,128]{3,2,1,0:T(8,128)(2,1)}), bf16[16,8,8,128]{3,2,1,0:T(8,128)(2,1)S(1)}, u32[]{:S(2)}, u32[]{:S(2)}) async-start(bf16[16,8,8,128]{3,2,1,0:T(8,128)(2,1)} %project.1), calls=%async_computation | async-start | bytes 524288 | tf_op jit(solution)/shard_map/all_to_all | solution.py:279
  13.6 1.6 %collective-permute-start.1 = (bf16[1600,128]{1,0:T(8,128)(2,1)S(1)}, bf16[1600,128]{1,0:T(8,128)(2,1)S(1)}, u32[]{:S(2)}, u32[]{:S(2)}) collective-permute-start(bf16[1600,128]{1,0:T(8,128)(2,1)S(1)} %get-tuple-element.15.own_ref), channel_id=1, source_target_pairs={{0,16},{16,0},{1,17},{17,1},{2,18},{18,2},{3,19},{19,3},{4,20},{20... | collective-permute-start | bytes 1228808 | tf_op jit(solution)/shard_map/ppermute | solution.py:254
  15.1 8.4 %all-to-all-done.in_ref = bf16[16,8,8,128]{3,2,1,0:T(8,128)(2,1)S(1)} async-done(((bf16[16,8,8,128]{3,2,1,0:T(8,128)(2,1)}), bf16[16,8,8,128]{3,2,1,0:T(8,128)(2,1)S(1)}, u32[]{:S(2)}, u32[]{:S(2)}) %all-to-all-start) | async-done | bytes 262176 | tf_op jit(solution)/shard_map/all_to_all | solution.py:279
  23.6 0.9 %triangle.2 = bf16[16,4,8,128]{3,2,1,0:T(8,128)(2,1)} custom-call(bf16[16,8,8,128]{3,2,1,0:T(8,128)(2,1)S(1)} %all-to-all-done.in_ref), custom_call_target="tpu_custom_call" | custom-call | tf_op jit(solution)/shard_map/triangle/pallas_call | solution.py:280
  24.5 3.5 %all-to-all-start.1 = ((bf16[16,4,8,128]{3,2,1,0:T(8,128)(2,1)}), bf16[16,4,8,128]{3,2,1,0:T(8,128)(2,1)S(1)}, u32[]{:S(2)}, u32[]{:S(2)}) async-start(bf16[16,4,8,128]{3,2,1,0:T(8,128)(2,1)} %triangle.2), calls=%async_computation.1 | async-start | bytes 262144 | tf_op jit(solution)/shard_map/all_to_all | solution.py:289
  28.0 0.4 gates.1.gate_ref
  28.4 0.0 collective-permute-done.1.other_ref
  28.4 7.5 %all-to-all-done.1.tri_ref = bf16[16,4,8,128]{3,2,1,0:T(8,128)(2,1)S(1)} async-done(((bf16[16,4,8,128]{3,2,1,0:T(8,128)(2,1)}), bf16[16,4,8,128]{3,2,1,0:T(8,128)(2,1)S(1)}, u32[]{:S(2)}, u32[]{:S(2)}) %all-to-all-start.1) | async-done | bytes 131104 | tf_op jit(solution)/shard_map/all_to_all | solution.py:289
  35.9 3.4 %update.1 = (bf16[8,128,128]{2,1,0:T(8,128)(2,1)S(1)}, bf16[16,8,8,128]{3,2,1,0:T(8,128)(2,1)S(1)}, f32[1024,128]{1,0:T(8,128)S(1)}) custom-call(f32[8,128]{1,0:T(8,128)S(1)} %get-tuple-element.12.keep_ref, bf16[16,4,8,128]{3,2,1,0:T(8,128)(2,1)S(1)} %all-to-all-done.1.tri_ref, f32[1024,128]{1,0:T(8,128)S(1)} %gates.1.gate_ref, ...), custom_call_target="tpu_custom_call" | custom-call | tf_op jit(solution)/shard_map/update/pallas_call | solution.py:299
  39.2 12.6 %all_to_all.20.in_ref = bf16[16,8,8,128]{3,2,1,0:T(8,128)(2,1)S(1)} all-to-all(bf16[16,8,8,128]{3,2,1,0:T(8,128)(2,1)S(1)} %get-tuple-element.16), channel_id=1, replica_groups=mesh['section'=2,'row'=16] {'row'}, dimensions={0} | all-to-all | bytes 524288 | tf_op jit(solution)/shard_map/all_to_all | solution.py:279
  51.8 0.2 triangle.3
  52.1 10.6 %all_to_all.21.tri_ref = bf16[16,4,8,128]{3,2,1,0:T(8,128)(2,1)S(1)} all-to-all(bf16[16,4,8,128]{3,2,1,0:T(8,128)(2,1)S(1)} %triangle.3), channel_id=1, replica_groups=mesh['section'=2,'row'=16] {'row'}, dimensions={0} | all-to-all | bytes 262144 | tf_op jit(solution)/shard_map/all_to_all | solution.py:289
  62.7 3.3 %update_last.1 = bf16[8,128,128]{2,1,0:T(8,128)(2,1)} custom-call(f32[8,128]{1,0:T(8,128)S(1)} %get-tuple-element.12.keep_ref, bf16[16,4,8,128]{3,2,1,0:T(8,128)(2,1)S(1)} %all_to_all.21.tri_ref, f32[1024,128]{1,0:T(8,128)S(1)} %get-tuple-element.17.gate_ref, bf16[8,128,128]{2,1,0:T(8,128)(2,1)S(1)} %get-tuple-element.18.z_ref, ...), custom_call_target="tpu_custom_call" | custom-call | tf_op jit(solution)/shard_map/update_last/pallas_call | solution.py:299
Async XLA Ops:
  0.0 6.1 %copy-start = (bf16[1,128,384]{2,1,0:T(8,128)(2,1)S(1)}, bf16[1,128,384]{2,1,0:T(8,128)(2,1)}, u32[]{:S(2)}) copy-start(bf16[1,128,384]{2,1,0:T(8,128)(2,1)} %wp_own_ref.3) | copy-start | bytes 294916
  0.0 6.1 %collective-permute-start = (bf16[1,128,384]{2,1,0:T(8,128)(2,1)}, bf16[1,128,384]{2,1,0:T(8,128)(2,1)S(1)}, u32[]{:S(2)}, u32[]{:S(2)}) collective-permute-start(bf16[1,128,384]{2,1,0:T(8,128)(2,1)} %wp_own_ref.3), channel_id=1, source_target_pairs={{0,16},{16,0},{1,17},{17,1},{2,18},{18,2},{3,19},{19,3},{4,20},{20... | collective-permute-start | bytes 294920 | tf_op jit(solution)/shard_map/ppermute | solution.py:233
  7.4 16.2 %all-to-all-start = ((bf16[16,8,8,128]{3,2,1,0:T(8,128)(2,1)}), bf16[16,8,8,128]{3,2,1,0:T(8,128)(2,1)S(1)}, u32[]{:S(2)}, u32[]{:S(2)}) async-start(bf16[16,8,8,128]{3,2,1,0:T(8,128)(2,1)} %project.1), calls=%async_computation | async-start | bytes 524288 | tf_op jit(solution)/shard_map/all_to_all | solution.py:279
  13.6 14.8 %collective-permute-start.1 = (bf16[1600,128]{1,0:T(8,128)(2,1)S(1)}, bf16[1600,128]{1,0:T(8,128)(2,1)S(1)}, u32[]{:S(2)}, u32[]{:S(2)}) collective-permute-start(bf16[1600,128]{1,0:T(8,128)(2,1)S(1)} %get-tuple-element.15.own_ref), channel_id=1, source_target_pairs={{0,16},{16,0},{1,17},{17,1},{2,18},{18,2},{3,19},{19,3},{4,20},{20... | collective-permute-start | bytes 1228808 | tf_op jit(solution)/shard_map/ppermute | solution.py:254
  24.5 11.4 %all-to-all-start.1 = ((bf16[16,4,8,128]{3,2,1,0:T(8,128)(2,1)}), bf16[16,4,8,128]{3,2,1,0:T(8,128)(2,1)S(1)}, u32[]{:S(2)}, u32[]{:S(2)}) async-start(bf16[16,4,8,128]{3,2,1,0:T(8,128)(2,1)} %triangle.2), calls=%async_computation.1 | async-start | bytes 262144 | tf_op jit(solution)/shard_map/all_to_all | solution.py:289

commit v3 on v2

--- a/solution.py
+++ b/solution.py
@@ -9,6 +9,7 @@
 
 F32 = jnp.float32
 BF16 = jnp.bfloat16
+STEP = 512
 LIMIT = pltpu.CompilerParams(vmem_limit_bytes=16 * 2**20)
 
 
@@ -19,16 +20,8 @@
     return centred * lax.rsqrt(var + 1e-05)
 
 
-def fetch(condition, own, other, target, sem):
-    @pl.when(condition)
-    def _():
-        pltpu.make_async_copy(own, target, sem).start()
-
-    @pl.when(jnp.logical_not(condition))
-    def _():
-        pltpu.make_async_copy(other, target, sem).start()
-
-    return pltpu.make_async_copy(own, target, sem)
+def row_norm(value):
+    return layer_norm(value.astype(F32)).astype(BF16)
 
 
 def ordered_weights(weights, inner, share):
@@ -45,9 +38,9 @@
     ).astype(BF16)
 
 
-def project(normed_ref, w_ref, keep_ref, lr_ref, inner):
+def project(normed_ref, weights, keep_ref, lr_ref, inner):
     peers, rows, wide, count = lr_ref.shape
-    turned = ordered_weights(w_ref[:, : 4 * inner], inner, wide // 2)
+    turned = ordered_weights(weights, inner, wide // 2)
     for r in range(rows):
         normed = normed_ref[r * count : (r + 1) * count, :]
         proj = lax.dot_general(
@@ -58,12 +51,12 @@
         lr_ref[:, r] = sides.reshape(peers, wide, count).astype(BF16)
 
 
-def output_gates(normed_ref, w_ref, gate_ref, inner):
+def output_gates(normed_ref, weights, gate_ref):
     step = 256
     for m in range(normed_ref.shape[0] // step):
         here = slice(m * step, (m + 1) * step)
         gate_ref[here, :] = jax.nn.sigmoid(
-            jnp.dot(normed_ref[here, :], w_ref[:, 4 * inner :], preferred_element_type=F32)
+            jnp.dot(normed_ref[here, :], weights, preferred_element_type=F32)
         )
 
 
@@ -116,21 +109,21 @@
     for r in range(rows):
         here = both_ref[crop, r]
         z_ref[r] = here
-        n_ref[r * count : (r + 1) * count, :] = layer_norm(here.astype(F32)).astype(BF16)
+        n_ref[r * count : (r + 1) * count, :] = row_norm(here)
     for copy in packing:
         copy.wait()
 
 
-def project_kernel(inner, n_ref, keep_ref, own_ref, other_ref, lr_ref, w_ref, sems):
-    section = lax.axis_index("section")
-    fetch(section == 0, own_ref.at[0], other_ref.at[0], w_ref, sems.at[0]).wait()
-    project(n_ref, w_ref, keep_ref, lr_ref, inner)
-
-
-def gates_kernel(inner, n_ref, own_ref, other_ref, gate_ref, w_ref, sems):
-    section = lax.axis_index("section")
-    fetch(section == 0, own_ref.at[0], other_ref.at[0], w_ref, sems.at[0]).wait()
-    output_gates(n_ref, w_ref, gate_ref, inner)
+def project_kernel(inner, n_ref, keep_ref, own_ref, other_ref, lr_ref):
+    mine = lax.axis_index("section") == 0
+    weights = jnp.where(mine, own_ref[0, :, : 4 * inner], other_ref[0, :, : 4 * inner])
+    project(n_ref, weights, keep_ref, lr_ref, inner)
+
+
+def gates_kernel(inner, n_ref, own_ref, other_ref, gate_ref):
+    mine = lax.axis_index("section") == 0
+    weights = jnp.where(mine, own_ref[0, :, 4 * inner :], other_ref[0, :, 4 * inner :])
+    output_gates(n_ref, weights, gate_ref)
 
 
 def tri_kernel(in_ref, out_ref, wide_ref):
@@ -164,22 +157,25 @@
 ):
     last = block == blocks - 1
     if last:
-        out_ref, t_ref, w_ref, n_ref, z1_ref, sems = refs
+        out_ref, t_ref, in_ref, back_ref, n_ref, z1_ref, o_ref, sems = refs
     else:
-        out_ref, lr_ref, gate_out_ref, t_ref, w_ref, n_ref, z1_ref, sems, wp_ref = refs
+        o_ref, lr_ref, gate_out_ref, t_ref, in_ref, back_ref, n_ref, z1_ref = refs
     section = lax.axis_index("section")
-    rows, count, width = out_ref.shape
-    weights = fetch(section == block, own_ref, other_ref, w_ref, sems.at[0])
-    if not last:
-        following = fetch(
-            section == block + 1, wp_own_ref.at[0], wp_other_ref.at[0], wp_ref, sems.at[1]
-        )
-    parts = width * (2 * trans // width)
+    rows, count, width = o_ref.shape
+    mine = section == block
+    hidden, both = 2 * trans, 3 * trans
+
+    def pick(start, size):
+        here = slice(start, start + size)
+        return jnp.where(mine, own_ref[here, :], other_ref[here, :])
+
+    for j in range(hidden // width):
+        in_ref[:, j * width : (j + 1) * width] = pick(j * width, width)
+    back_ref[...] = pick(hidden, trans)
+    w_out = pick(both, inner)
     t_ref[...] = layer_norm(tri_ref[...].reshape(inner, rows, count).astype(F32), 0).reshape(
         inner * rows, count
     )
-    weights.wait()
-    w_out = w_ref[parts + trans : parts + trans + inner, :]
     for r in range(rows):
         here = slice(r * count, (r + 1) * count)
         tri = t_ref[pl.ds(r, inner, stride=rows), :].astype(BF16)
@@ -188,28 +184,37 @@
         )
         first = (z_ref[r].astype(F32) + gate_ref[here, :] * update).astype(BF16)
         z1_ref[here, :] = first
-        n_ref[here, :] = layer_norm(first.astype(F32)).astype(BF16)
-    step = 2 * count
+        n_ref[here, :] = row_norm(first)
+    step, piece = STEP, 256
+    copies = []
     for m in range(rows * count // step):
         here = slice(m * step, (m + 1) * step)
         normed = n_ref[here, :]
-        total = z1_ref[here, :].astype(F32)
-        for j in range(trans // width):
-            gate_w = w_ref[j * width : (j + 1) * width, :]
-            up_w = w_ref[trans + j * width : trans + (j + 1) * width, :]
+        acts = []
+        for j in range(trans // piece):
+            gate_w = in_ref[:, j * piece : (j + 1) * piece]
+            up_w = in_ref[:, trans + j * piece : trans + (j + 1) * piece]
             gate = jnp.dot(normed, gate_w, preferred_element_type=F32)
             up = jnp.dot(normed, up_w, preferred_element_type=F32)
-            act = (jax.nn.silu(gate) * up).astype(BF16)
-            back_w = w_ref[parts + j * width : parts + (j + 1) * width, :]
-            total = total + jnp.dot(act, back_w, preferred_element_type=F32)
-        done = total.astype(BF16)
-        out_ref[2 * m : 2 * m + 2] = done.reshape(2, count, width)
-        if not last:
-            n_ref[here, :] = layer_norm(done.astype(F32)).astype(BF16)
+            acts.append((jax.nn.silu(gate) * up).astype(BF16))
+        act = jnp.concatenate(acts, -1)
+        back = jnp.dot(act, back_ref[...], preferred_element_type=F32)
+        done = (z1_ref[here, :].astype(F32) + back).astype(BF16)
+        n = step // count
+        o_ref[n * m : n * (m + 1)] = done.reshape(n, count, width)
+        if last:
+            part = pl.ds(n * m, n)
+            copies.append(pltpu.make_async_copy(o_ref.at[part], out_ref.at[part], sems.at[m]))
+            copies[-1].start()
+        else:
+            n_ref[here, :] = row_norm(done)
+    for copy in copies:
+        copy.wait()
     if not last:
-        following.wait()
-        project(n_ref, wp_ref, keep_ref, lr_ref, inner)
-        output_gates(n_ref, wp_ref, gate_out_ref, inner)
+        following = section == block + 1
+        weights = jnp.where(following, wp_own_ref[0], wp_other_ref[0])
+        project(n_ref, weights[:, : 4 * inner], keep_ref, lr_ref, inner)
+        output_gates(n_ref, weights[:, 4 * inner :], gate_out_ref)
 
 
 def fast_body(pair, valid_tokens, crop_order, w_proj, w_out, w_in, w_back):
@@ -224,7 +229,6 @@
 
     vmem = pl.BlockSpec(memory_space=pltpu.VMEM)
     hbm = pl.BlockSpec(memory_space=pltpu.HBM)
-    anywhere = pl.BlockSpec(memory_space=pl.ANY)
     sides = jax.ShapeDtypeStruct((peers, rows, wide, count), BF16)
     gates = jax.ShapeDtypeStruct((rows * count, width), F32)
     state = jax.ShapeDtypeStruct((rows, count, width), BF16)
@@ -253,22 +257,19 @@
     )(*[pltpu.with_memory_space_constraint(x, pltpu.HBM) for x in (crop_order, valid_tokens, pair, w_in, w_back, w_out)])
     rest_other = lax.ppermute(rest, "section", swap)
 
-    weights = pltpu.VMEM(w_proj.shape[1:], BF16)
     lr = pl.pallas_call(
         functools.partial(project_kernel, inner),
         out_shape=sides,
-        in_specs=[vmem, vmem, anywhere, anywhere],
+        in_specs=[vmem] * 4,
         out_specs=vmem,
-        scratch_shapes=[weights, pltpu.SemaphoreType.DMA((1,))],
         compiler_params=LIMIT,
         name="project",
     )(normed, keep, w_proj, wp_other)
     gate = pl.pallas_call(
         functools.partial(gates_kernel, inner),
         out_shape=gates,
-        in_specs=[vmem, anywhere, anywhere],
+        in_specs=[vmem] * 3,
         out_specs=vmem,
-        scratch_shapes=[weights, pltpu.SemaphoreType.DMA((1,))],
         compiler_params=LIMIT,
         cost_estimate=pl.CostEstimate(flops=34 * 10**6, bytes_accessed=10**6, transcendentals=2 * 10**5),
         name="gates",
@@ -289,18 +290,21 @@
         tri = lax.all_to_all(tri_part, "row", split_axis=0, concat_axis=0, tiled=True)
         scratch = [
             pltpu.VMEM((inner * rows, count), F32),
-            pltpu.VMEM((rest_rows, width), BF16),
-            pltpu.VMEM((rows * count, width), BF16),
-            pltpu.VMEM((rows * count, width), BF16),
-            pltpu.SemaphoreType.DMA((2,)),
+            pltpu.VMEM(w_in.shape[1:], BF16),
+            pltpu.VMEM(w_back.shape[1:], BF16),
+            pltpu.VMEM(tokens.shape, BF16),
+            pltpu.VMEM(tokens.shape, BF16),
         ]
-        if not last:
-            scratch.append(pltpu.VMEM(w_proj.shape[1:], BF16))
+        if last:
+            scratch += [
+                pltpu.VMEM(state.shape, BF16),
+                pltpu.SemaphoreType.DMA((rows * count // STEP,)),
+            ]
         result = pl.pallas_call(
             functools.partial(update_kernel, block, blocks, inner, trans),
             out_shape=(state,) if last else (state, sides, gates),
-            in_specs=[vmem] * 4 + [anywhere] * 4,
-            out_specs=(vmem,) if last else (vmem,) * 3,
+            in_specs=[vmem] * 8,
+            out_specs=(hbm,) if last else (vmem,) * 3,
             scratch_shapes=scratch,
             compiler_params=LIMIT,
             name="update_last" if last else "update",

time: 66.4 us -> 64.1 us (0.965)
  Pallas kernels: 11.2 us -> 8.75 us
    pallas_call x2, Pallas kernels: 6.69 us -> 4.49 us  [fast_body(): pl.pallas_call(functools.partial(update_kernel, block, blocks, inner, tra...]
  transfers between devices with their start and end apart: 4 -> 4, of which waited for: 3 -> 3; matrix products, arithmetic and copies ran while one was open for 0% -> 0% of each run, Pallas kernels for 5% -> 4%
where the time goes in v3:
time: 64.1 us; the launch traced here: 63.7 us
  blocking collectives  23.2 us (36%)
  waiting for transfers between devices  17.4 us (27%)
  starting transfers between devices  14.2 us (22%)
  Pallas kernels  8.75 us (14%)
    all_to_all x1, blocking collectives, fast_body(): whole = lax.all_to_all(lr, 'row', split_axis=0, concat_axis=0, tiled=True)  12.6 us
    all_to_all x1, blocking collectives, fast_body(): lax.all_to_all(tri_part, 'row', split_axis=0, concat_axis=0, tiled=True)  10.6 us
    all_to_all x1, waiting for transfers between devices, fast_body(): whole = lax.all_to_all(lr, 'row', split_axis=0, concat_axis=0, tiled=True)  8.43 us
    all_to_all x1, waiting for transfers between devices, fast_body(): lax.all_to_all(tri_part, 'row', split_axis=0, concat_axis=0, tiled=True)  7.62 us
    all_to_all x1, starting transfers between devices, fast_body(): whole = lax.all_to_all(lr, 'row', split_axis=0, concat_axis=0, tiled=True)  6.14 us
    pallas_call x2, Pallas kernels, fast_body(): pl.pallas_call(functools.partial(update_kernel, block, blocks, inner, tra...  4.49 us
    all_to_all x1, starting transfers between devices, fast_body(): lax.all_to_all(tri_part, 'row', split_axis=0, concat_axis=0, tiled=True)  3.51 us
    ppermute x1, starting transfers between devices, fast_body(): wp_other = lax.ppermute(w_proj, 'section', swap)  3 us
  transfers between devices with their start and end apart: 4, of which 3 were waited for; matrix products, arithmetic and copies ran while one was open for 0% of the time, Pallas kernels for 4%

profile of v3, /device:TPU:0, one launch (start us, length us, event | category | flops | bytes accessed | tf_op | source)
XLA Modules:
  0.0 63.7 jit_solution(14371445930752372592)
XLA Ops:
  0.0 0.0 copy-start
  0.0 3.0 %collective-permute-start = (bf16[1,128,384]{2,1,0:T(8,128)(2,1)}, bf16[1,128,384]{2,1,0:T(8,128)(2,1)S(1)}, u32[]{:S(2)}, u32[]{:S(2)}) collective-permute-start(bf16[1,128,384]{2,1,0:T(8,128)(2,1)} %wp_own_ref.3), channel_id=1, source_target_pairs={{0,16},{16,0},{1,17},{17,1},{2,18},{18,2},{3,19},{19,3},{4,20},{20... | collective-permute-start | bytes 294920 | tf_op jit(solution)/shard_map/ppermute | solution.py:237
  3.0 1.7 %prepare.1 = (bf16[8,128,128]{2,1,0:T(8,128)(2,1)S(1)}, bf16[1024,128]{1,0:T(8,128)(2,1)S(1)}, f32[8,128]{1,0:T(8,128)S(1)}, bf16[1600,128]{1,0:T(8,128)(2,1)S(1)}) custom-call(s32[2]{0:T(128)} %order_ref.1, s32[2]{0:T(128)} %valid_ref.1, bf16[2,8,128,128]{3,2,1,0:T(8,128)(2,1)} %pair_ref.1, bf16[1,128,1024]{2,1,0:T(8,128)(2,1)} %w_in_ref.1, ...), custom_call_target="tpu_custom_call" | custom-call | flops 1000000 | bytes 3000000 | tf_op jit(solution)/shard_map/prepare/pallas_call | solution.py:238
  4.7 1.4 %collective-permute-done.other_ref.wp_other_ref = bf16[1,128,384]{2,1,0:T(8,128)(2,1)S(1)} collective-permute-done((bf16[1,128,384]{2,1,0:T(8,128)(2,1)}, bf16[1,128,384]{2,1,0:T(8,128)(2,1)S(1)}, u32[]{:S(2)}, u32[]{:S(2)}) %collective-permute-start) | collective-permute-done | bytes 98336 | tf_op jit(solution)/shard_map/ppermute | solution.py:237
  6.1 0.0 copy-done
  6.1 1.2 %project.1 = bf16[16,8,8,128]{3,2,1,0:T(8,128)(2,1)} custom-call(bf16[1024,128]{1,0:T(8,128)(2,1)S(1)} %get-tuple-element.13.n_ref, f32[8,128]{1,0:T(8,128)S(1)} %get-tuple-element.12.keep_ref, bf16[1,128,384]{2,1,0:T(8,128)(2,1)S(1)} %copy-done, bf16[1,128,384]{2,1,0:T(8,128)(2,1)S(1)} %collective-permute-done.other_ref.wp_other_ref), custom_call_target="tpu_custom_call" | custom-call | tf_op jit(solution)/shard_map/project/pallas_call | solution.py:260
  7.3 6.1 %all-to-all-start = ((bf16[16,8,8,128]{3,2,1,0:T(8,128)(2,1)}), bf16[16,8,8,128]{3,2,1,0:T(8,128)(2,1)S(1)}, u32[]{:S(2)}, u32[]{:S(2)}) async-start(bf16[16,8,8,128]{3,2,1,0:T(8,128)(2,1)} %project.1), calls=%async_computation | async-start | bytes 524288 | tf_op jit(solution)/shard_map/all_to_all | solution.py:280
  13.4 1.6 %collective-permute-start.1 = (bf16[1600,128]{1,0:T(8,128)(2,1)S(1)}, bf16[1600,128]{1,0:T(8,128)(2,1)S(1)}, u32[]{:S(2)}, u32[]{:S(2)}) collective-permute-start(bf16[1600,128]{1,0:T(8,128)(2,1)S(1)} %get-tuple-element.15.own_ref), channel_id=1, source_target_pairs={{0,16},{16,0},{1,17},{17,1},{2,18},{18,2},{3,19},{19,3},{4,20},{20... | collective-permute-start | bytes 1228808 | tf_op jit(solution)/shard_map/ppermute | solution.py:258
  15.0 8.4 %all-to-all-done.in_ref = bf16[16,8,8,128]{3,2,1,0:T(8,128)(2,1)S(1)} async-done(((bf16[16,8,8,128]{3,2,1,0:T(8,128)(2,1)}), bf16[16,8,8,128]{3,2,1,0:T(8,128)(2,1)S(1)}, u32[]{:S(2)}, u32[]{:S(2)}) %all-to-all-start) | async-done | bytes 262176 | tf_op jit(solution)/shard_map/all_to_all | solution.py:280
  23.4 0.9 %triangle.2 = bf16[16,4,8,128]{3,2,1,0:T(8,128)(2,1)} custom-call(bf16[16,8,8,128]{3,2,1,0:T(8,128)(2,1)S(1)} %all-to-all-done.in_ref), custom_call_target="tpu_custom_call" | custom-call | tf_op jit(solution)/shard_map/triangle/pallas_call | solution.py:281
  24.3 3.5 %all-to-all-start.1 = ((bf16[16,4,8,128]{3,2,1,0:T(8,128)(2,1)}), bf16[16,4,8,128]{3,2,1,0:T(8,128)(2,1)S(1)}, u32[]{:S(2)}, u32[]{:S(2)}) async-start(bf16[16,4,8,128]{3,2,1,0:T(8,128)(2,1)} %triangle.2), calls=%async_computation.1 | async-start | bytes 262144 | tf_op jit(solution)/shard_map/all_to_all | solution.py:290
  27.9 0.2 gates.1.gate_ref
  28.1 0.0 collective-permute-done.1.other_ref
  28.1 7.6 %all-to-all-done.1.tri_ref = bf16[16,4,8,128]{3,2,1,0:T(8,128)(2,1)S(1)} async-done(((bf16[16,4,8,128]{3,2,1,0:T(8,128)(2,1)}), bf16[16,4,8,128]{3,2,1,0:T(8,128)(2,1)S(1)}, u32[]{:S(2)}, u32[]{:S(2)}) %all-to-all-start.1) | async-done | bytes 131104 | tf_op jit(solution)/shard_map/all_to_all | solution.py:290
  35.7 2.1 %update.1 = (bf16[8,128,128]{2,1,0:T(8,128)(2,1)S(1)}, bf16[16,8,8,128]{3,2,1,0:T(8,128)(2,1)S(1)}, f32[1024,128]{1,0:T(8,128)S(1)}) custom-call(f32[8,128]{1,0:T(8,128)S(1)} %get-tuple-element.12.keep_ref, bf16[16,4,8,128]{3,2,1,0:T(8,128)(2,1)S(1)} %all-to-all-done.1.tri_ref, f32[1024,128]{1,0:T(8,128)S(1)} %gates.1.gate_ref, ...), custom_call_target="tpu_custom_call" | custom-call | tf_op jit(solution)/shard_map/update/pallas_call | solution.py:303
  37.8 12.6 %all_to_all.20.in_ref = bf16[16,8,8,128]{3,2,1,0:T(8,128)(2,1)S(1)} all-to-all(bf16[16,8,8,128]{3,2,1,0:T(8,128)(2,1)S(1)} %get-tuple-element.16), channel_id=1, replica_groups=mesh['section'=2,'row'=16] {'row'}, dimensions={0} | all-to-all | bytes 524288 | tf_op jit(solution)/shard_map/all_to_all | solution.py:280
  50.5 0.2 triangle.3
  50.7 10.6 %all_to_all.21.tri_ref = bf16[16,4,8,128]{3,2,1,0:T(8,128)(2,1)S(1)} all-to-all(bf16[16,4,8,128]{3,2,1,0:T(8,128)(2,1)S(1)} %triangle.3), channel_id=1, replica_groups=mesh['section'=2,'row'=16] {'row'}, dimensions={0} | all-to-all | bytes 262144 | tf_op jit(solution)/shard_map/all_to_all | solution.py:290
  61.3 2.4 %update_last.1 = bf16[8,128,128]{2,1,0:T(8,128)(2,1)} custom-call(f32[8,128]{1,0:T(8,128)S(1)} %get-tuple-element.12.keep_ref, bf16[16,4,8,128]{3,2,1,0:T(8,128)(2,1)S(1)} %all_to_all.21.tri_ref, f32[1024,128]{1,0:T(8,128)S(1)} %get-tuple-element.17.gate_ref, bf16[8,128,128]{2,1,0:T(8,128)(2,1)S(1)} %get-tuple-element.18.z_ref, ...), custom_call_target="tpu_custom_call" | custom-call | tf_op jit(solution)/shard_map/update_last/pallas_call | solution.py:303
Async XLA Ops:
  0.0 6.1 %copy-start = (bf16[1,128,384]{2,1,0:T(8,128)(2,1)S(1)}, bf16[1,128,384]{2,1,0:T(8,128)(2,1)}, u32[]{:S(2)}) copy-start(bf16[1,128,384]{2,1,0:T(8,128)(2,1)} %wp_own_ref.3) | copy-start | bytes 294916
  0.0 6.1 %collective-permute-start = (bf16[1,128,384]{2,1,0:T(8,128)(2,1)}, bf16[1,128,384]{2,1,0:T(8,128)(2,1)S(1)}, u32[]{:S(2)}, u32[]{:S(2)}) collective-permute-start(bf16[1,128,384]{2,1,0:T(8,128)(2,1)} %wp_own_ref.3), channel_id=1, source_target_pairs={{0,16},{16,0},{1,17},{17,1},{2,18},{18,2},{3,19},{19,3},{4,20},{20... | collective-permute-start | bytes 294920 | tf_op jit(solution)/shard_map/ppermute | solution.py:237
  7.3 16.2 %all-to-all-start = ((bf16[16,8,8,128]{3,2,1,0:T(8,128)(2,1)}), bf16[16,8,8,128]{3,2,1,0:T(8,128)(2,1)S(1)}, u32[]{:S(2)}, u32[]{:S(2)}) async-start(bf16[16,8,8,128]{3,2,1,0:T(8,128)(2,1)} %project.1), calls=%async_computation | async-start | bytes 524288 | tf_op jit(solution)/shard_map/all_to_all | solution.py:280
  13.4 14.7 %collective-permute-start.1 = (bf16[1600,128]{1,0:T(8,128)(2,1)S(1)}, bf16[1600,128]{1,0:T(8,128)(2,1)S(1)}, u32[]{:S(2)}, u32[]{:S(2)}) collective-permute-start(bf16[1600,128]{1,0:T(8,128)(2,1)S(1)} %get-tuple-element.15.own_ref), channel_id=1, source_target_pairs={{0,16},{16,0},{1,17},{17,1},{2,18},{18,2},{3,19},{19,3},{4,20},{20... | collective-permute-start | bytes 1228808 | tf_op jit(solution)/shard_map/ppermute | solution.py:258
  24.3 11.4 %all-to-all-start.1 = ((bf16[16,4,8,128]{3,2,1,0:T(8,128)(2,1)}), bf16[16,4,8,128]{3,2,1,0:T(8,128)(2,1)S(1)}, u32[]{:S(2)}, u32[]{:S(2)}) async-start(bf16[16,4,8,128]{3,2,1,0:T(8,128)(2,1)} %triangle.2), calls=%async_computation.1 | async-start | bytes 262144 | tf_op jit(solution)/shard_map/all_to_all | solution.py:290

commit v4 on v0

v4 whole, which is shorter than its diff:
```python
import functools

import jax
import jax.numpy as jnp
from jax import lax
from jax.experimental import pallas as pl
from jax.experimental.pallas import tpu as pltpu
from jax.sharding import PartitionSpec as P

F32 = jnp.float32
BF16 = jnp.bfloat16
STEP = 512
CHANNELS = 2
SHORT = 32
LIMIT = pltpu.CompilerParams(vmem_limit_bytes=16 * 2**20)


def layer_norm(value, axis=-1):
    mean = jnp.mean(value, axis, keepdims=True)
    centred = value - mean
    var = jnp.mean(centred * centred, axis, keepdims=True)
    return centred * lax.rsqrt(var + 1e-05)


def row_norm(value):
    return layer_norm(value.astype(F32)).astype(BF16)


def contract(left, right, left_axis, right_axis):
    return lax.dot_general(
        left, right, (((left_axis,), (right_axis,)), ((), ())), preferred_element_type=F32
    )


def tile_weights(weights, inner):
    total = 8 * inner
    row = lax.broadcasted_iota(jnp.int32, (total, 4 * inner), 0)
    column = lax.broadcasted_iota(jnp.int32, (total, 4 * inner), 1)
    gates, rest = lax.div(row, 4 * inner), lax.rem(row, 4 * inner)
    peer, slot = lax.div(rest, 8), lax.rem(rest, 8)
    half, side, channel = lax.div(slot, 4), lax.rem(lax.div(slot, 2), 2), lax.rem(slot, 2)
    source = side * (2 * inner) + gates * inner + peer * CHANNELS + channel
    parts = []
    for h in range(2):
        chosen = jnp.logical_and(column == source, half == h)
        pick = jnp.where(chosen, 1.0, 0.0).astype(BF16)
        parts.append(contract(pick, weights, 1, 1).astype(BF16))
    return jnp.concatenate(parts, -1)


def put_tiles(turned, halves, masks, lr_ref, first, inner):
    peers, count = lr_ref.shape[0], lr_ref.shape[-1]
    normed = jnp.concatenate([jnp.concatenate(pair, -1) for pair in halves], 0)
    proj = contract(turned, normed, 1, 1)
    sides = jax.nn.sigmoid(proj[4 * inner :]) * proj[: 4 * inner]
    for i, mask in enumerate(masks):
        tile = sides[:, i * count : (i + 1) * count].reshape(peers, 8, count)
        lr_ref[:, first + i] = (tile * mask[None]).astype(BF16)


def full_mask(row, valid, count):
    half = lax.div(lax.broadcasted_iota(jnp.int32, (8, count), 0), 4)
    token = lax.broadcasted_iota(jnp.int32, (8, count), 1)
    return jnp.where(jnp.logical_and(row + half < valid, token < valid), 1.0, 0.0)


def short_mask(row, valid, count):
    half = lax.div(lax.broadcasted_iota(jnp.int32, (8, count), 0), 4)
    lane = lax.broadcasted_iota(jnp.int32, (8, count), 1)
    inside = row + 4 * half + lax.div(lane, SHORT) < valid
    return jnp.where(jnp.logical_and(inside, lax.rem(lane, SHORT) < valid), 1.0, 0.0)


def read_scalars(order_ref, valid_ref, order_s, valid_s, sems):
    copies = [
        pltpu.make_async_copy(order_ref, order_s, sems.at[0]),
        pltpu.make_async_copy(valid_ref, valid_s, sems.at[1]),
    ]
    for copy in copies:
        copy.start()
    return copies


def first_kernel(
    inner,
    order_ref,
    valid_ref,
    pair_ref,
    wp_ref,
    w_in_ref,
    w_back_ref,
    w_out_ref,
    lr_ref,
    pack_ref,
    z_ref,
    owns_ref,
    masks_ref,
    order_s,
    valid_s,
    both_ref,
    w_ref,
    sems,
):
    rows, count, width = pair_ref.shape[1:]
    trans = w_back_ref.shape[1]
    scalars = read_scalars(order_ref, valid_ref, order_s, valid_s, sems)
    weights = pltpu.make_async_copy(wp_ref.at[0], w_ref, sems.at[2])
    weights.start()
    state = pltpu.make_async_copy(pair_ref, both_ref, sems.at[3])
    state.start()
    sources = [w_in_ref.at[0, :, pl.ds(j * width, width)] for j in range(2 * trans // width)]
    sources += [w_back_ref.at[0], w_out_ref.at[0]]
    sources += [wp_ref.at[0, :, pl.ds(j * width, width)] for j in range(w_ref.shape[1] // width)]
    packing, at = [], 0
    for i, source in enumerate(sources):
        size = source.shape[0]
        packing.append(
            pltpu.make_async_copy(source, pack_ref.at[pl.ds(at, size)], sems.at[4 + i])
        )
        packing[-1].start()
        at += size
    weights.wait()
    turned = tile_weights(w_ref[:, : 4 * inner], inner)
    for copy in scalars:
        copy.wait()
    section = lax.axis_index("section")
    full = jnp.where(valid_s[1] > valid_s[0], 1, 0)
    short = 1 - full
    owns_ref[...] = jnp.full(owns_ref.shape, jnp.where(order_s[section] == full, 1.0, 0.0))
    start = lax.axis_index("row") * rows
    mine = start + (rows // 2) * section
    masks_ref[0] = full_mask(mine, valid_s[full], count)
    masks_ref[1] = full_mask(mine + 2, valid_s[full], count)
    masks_ref[2] = short_mask(mine, valid_s[short], count)
    state.wait()
    half = pl.ds((rows // 2) * section, rows // 2)
    z_ref[: rows // 2] = both_ref[full, half]
    z_ref[rows // 2 :] = both_ref[short, half]
    for t in range(0, rows // 2, 2):
        normed = [row_norm(both_ref[full, 2 * t + r]) for r in range(4)]
        put_tiles(
            turned,
            [normed[:2], normed[2:]],
            [full_mask(start + 2 * t + r, valid_s[full], count) for r in (0, 2)],
            lr_ref,
            t,
            inner,
        )
    fours = [
        row_norm(both_ref[short, 4 * h : 4 * h + 4, :SHORT].reshape(4 * SHORT, width))
        for h in range(2)
    ]
    put_tiles(turned, [fours], [short_mask(start, valid_s[short], count)], lr_ref, rows // 2, inner)
    for copy in packing:
        copy.wait()


def short_triangle(left, right, place_ref):
    count = left.shape[1]
    block = lax.div(lax.broadcasted_iota(jnp.int32, left.shape, 1), SHORT)
    lefts = jnp.concatenate([jnp.where(block == q, left, 0.0) for q in range(4)], 0)
    rights = jnp.concatenate(
        [right if q == 0 else pltpu.roll(right, SHORT * q, 1) for q in range(4)], 0
    )
    product = contract(lefts.astype(BF16), rights.astype(BF16), 1, 1).astype(BF16)
    source = lax.broadcasted_iota(jnp.int32, (32, count), 0)
    target = lax.broadcasted_iota(jnp.int32, (32, count), 1)
    moved, token = lax.div(source, 8), lax.rem(source, 8)
    for q in range(4):
        lane = 4 * token + lax.rem(q - moved + 4, 4)
        pick = jnp.where(target == lane, 1.0, 0.0).astype(BF16)
        place_ref[pl.ds(q, 8, stride=4), :] = jnp.dot(
            product[8 * q : 8 * q + 8], pick, preferred_element_type=F32
        )


def triangles(wide_ref, few_ref, few_stride, place_ref, count):
    results = []
    for c in range(CHANNELS):
        left = wide_ref[pl.ds(c, count, stride=4), :].astype(BF16)
        right = wide_ref[pl.ds(2 + c, count, stride=4), :].astype(BF16)
        short_triangle(
            few_ref[pl.ds(c, 8, stride=few_stride), :],
            few_ref[pl.ds(2 + c, 8, stride=few_stride), :],
            place_ref.at[c],
        )
        results.append((contract(left, right, 1, 1), place_ref[c]))
    return results


def first_triangle_kernel(in_ref, out_ref, wide_ref, few_ref, place_ref):
    peers, count = in_ref.shape[0], in_ref.shape[-1]
    rows = peers // 2
    tiles = in_ref.shape[1] - 1
    wide_ref[...] = in_ref[:rows, :tiles].astype(F32).reshape(rows * tiles * 8, count)
    few_ref[...] = in_ref[:4, tiles].astype(F32).reshape(32, count)
    results = triangles(wide_ref, few_ref, 4, place_ref, count)
    for q in range(2):
        one, two = [r[q].reshape(-1, 8, count) for r in results]
        low = lax.broadcasted_iota(jnp.int32, one.shape, 1) < 4
        groups = one.shape[0]
        tiles = (
            jnp.where(low, one, pltpu.roll(two, 4, 1)),
            jnp.where(low, pltpu.roll(one, 4, 1), two),
        )
        for section, tile in enumerate(tiles):
            out_ref[section * rows : section * rows + groups, q] = tile.astype(BF16)
            if groups < rows:
                out_ref[section * rows + groups : (section + 1) * rows, q] = jnp.zeros(
                    (rows - groups, 8, count), BF16
                )


def last_triangle_kernel(in_ref, owns_ref, out_ref, wide_ref, few_ref, place_ref):
    peers, count = in_ref.shape[0], in_ref.shape[-1]
    rows = peers // 2
    for r in range(rows):
        for section in range(2):
            at = 2 * r + section
            tiles = in_ref[section * rows + r]
            wide_ref[16 * at : 16 * at + 16, :] = tiles[:2].astype(F32).reshape(16, count)
            if at < 8:
                few_ref[8 * at : 8 * at + 8, :] = tiles[2].astype(F32)
    zero_owns = jnp.where(lax.axis_index("section") == 0, owns_ref[...], 1.0 - owns_ref[...]) > 0.5
    results = triangles(wide_ref, few_ref, 8, place_ref, count)
    for c, (full, short) in enumerate(results):
        full = full.reshape(rows, 8, count)
        short = short.reshape(-1, 8, count)
        groups = short.shape[0]
        for section in range(2):
            is_full = zero_owns if section == 0 else jnp.logical_not(zero_owns)
            at = section * rows
            out_ref[at : at + groups, c] = jnp.where(is_full[None], full[:groups], short).astype(BF16)
            out_ref[at + groups : at + rows, c] = jnp.where(
                is_full[None], full[groups:], 0.0
            ).astype(BF16)


def picker(block, own_ref, other_ref):
    mine = lax.axis_index("section") == block

    def pick(start, size):
        here = slice(start, start + size)
        return jnp.where(mine, own_ref[here, :], other_ref[here, :])

    return pick


def gates_kernel(block, inner, trans, z_ref, own_ref, other_ref, gate_ref):
    rows, count, width = z_ref.shape
    pick = picker(block, own_ref, other_ref)
    weights = pick(3 * trans + inner + 2 * width, width)
    for r in range(0, rows, 2):
        normed = row_norm(z_ref[r : r + 2].reshape(2 * count, width))
        gate_ref[r * count : (r + 2) * count, :] = jax.nn.sigmoid(
            jnp.dot(normed, weights, preferred_element_type=F32)
        )


def join_kernel(keep_ref, other_ref, z_ref):
    half = keep_ref.shape[0]
    first = lax.axis_index("section") == 0
    z_ref[:half] = jnp.where(first, keep_ref[...], other_ref[...])
    z_ref[half:] = jnp.where(first, other_ref[...], keep_ref[...])


def out_project(t_ref, offsets, stride, z_ref, gate_ref, w_out, z1_ref, n_ref):
    rows, count, width = z_ref.shape
    inner = w_out.shape[0]
    for r in range(rows):
        here = slice(r * count, (r + 1) * count)
        tri = t_ref[pl.ds(offsets[r], inner, stride=stride), :].astype(BF16)
        update = contract(tri, w_out, 0, 0)
        first = (z_ref[r].astype(F32) + gate_ref[here, :] * update).astype(BF16)
        z1_ref[here, :] = first
        n_ref[here, :] = row_norm(first)


def transition(pick, trans, in_ref, back_ref, n_ref, z1_ref, width, finish):
    hidden = 2 * trans
    for j in range(hidden // width):
        in_ref[:, j * width : (j + 1) * width] = pick(j * width, width)
    back_ref[...] = pick(hidden, trans)

    def run():
        piece = 256
        for m in range(n_ref.shape[0] // STEP):
            here = slice(m * STEP, (m + 1) * STEP)
            normed = n_ref[here, :]
            acts = []
            for j in range(trans // piece):
                gate_w = in_ref[:, j * piece : (j + 1) * piece]
                up_w = in_ref[:, trans + j * piece : trans + (j + 1) * piece]
                gate = jnp.dot(normed, gate_w, preferred_element_type=F32)
                up = jnp.dot(normed, up_w, preferred_element_type=F32)
                acts.append((jax.nn.silu(gate) * up).astype(BF16))
            back = jnp.dot(jnp.concatenate(acts, -1), back_ref[...], preferred_element_type=F32)
            finish(m, (z1_ref[here, :].astype(F32) + back).astype(BF16))

    return run


def update_kernel(
    inner,
    trans,
    tri_ref,
    gate_ref,
    z_ref,
    own_ref,
    other_ref,
    masks_ref,
    owns_ref,
    lr_ref,
    keep_ref,
    send_ref,
    t_ref,
    in_ref,
    back_ref,
    n_ref,
    z1_ref,
    o_ref,
):
    rows, count, width = z_ref.shape
    half = rows // 2
    pick = picker(0, own_ref, other_ref)

    def finish(m, done):
        o_ref[m * STEP : (m + 1) * STEP, :] = done

    run = transition(pick, trans, in_ref, back_ref, n_ref, z1_ref, width, finish)
    for q in range(2):
        part = tri_ref[:, q].astype(F32)

        def mean(value):
            total = jnp.sum(value, 0)
            return (total + pltpu.roll(total, 4, 0)) * (1.0 / inner)

        centred = part - mean(part)[None]
        var = mean(centred * centred)
        normed = centred * lax.rsqrt(var + 1e-05)[None]
        t_ref[q * 4 * inner : (q + 1) * 4 * inner, :] = normed.reshape(4 * inner, count)
    offsets = [q * 4 * inner + r for q in range(2) for r in range(half)]
    out_project(t_ref, offsets, 4, z_ref, gate_ref, pick(3 * trans, inner), z1_ref, n_ref)
    run()
    owns = (owns_ref[:1, :] > 0.5)[None]
    full = o_ref[: half * count, :].reshape(half, count, width)
    short = o_ref[half * count :, :].reshape(half, count, width)
    keep_ref[...] = jnp.where(owns, full.astype(F32), short.astype(F32)).astype(BF16)
    send_ref[...] = jnp.where(owns, short.astype(F32), full.astype(F32)).astype(BF16)
    next_pick = picker(1, own_ref, other_ref)
    at = 3 * trans + inner
    weights = jnp.concatenate([next_pick(at, width), next_pick(at + width, width)], -1)
    turned = tile_weights(weights, inner)
    normed = [row_norm(o_ref[r * count : (r + 1) * count, :]) for r in range(half)]
    put_tiles(
        turned, [normed[:2], normed[2:]], [masks_ref[0], masks_ref[1]], lr_ref, 0, inner
    )
    four = row_norm(
        jnp.concatenate(
            [o_ref[r * count : r * count + SHORT, :] for r in range(half, rows)], 0
        )
    )
    put_tiles(turned, [[four, jnp.zeros_like(four)]], [masks_ref[2]], lr_ref, 2, inner)


def last_kernel(
    inner,
    trans,
    tri_ref,
    gate_ref,
    z_ref,
    own_ref,
    other_ref,
    out_ref,
    t_ref,
    in_ref,
    back_ref,
    n_ref,
    z1_ref,
    o_ref,
    sems,
):
    rows, count, width = z_ref.shape
    pick = picker(1, own_ref, other_ref)
    copies = []

    def finish(m, done):
        part = pl.ds(m * (STEP // count), STEP // count)
        o_ref[m * (STEP // count) : (m + 1) * (STEP // count)] = done.reshape(-1, count, width)
        copies.append(pltpu.make_async_copy(o_ref.at[part], out_ref.at[part], sems.at[m]))
        copies[-1].start()

    run = transition(pick, trans, in_ref, back_ref, n_ref, z1_ref, width, finish)
    t_ref[...] = layer_norm(tri_ref[...].reshape(inner, rows, count).astype(F32), 0).reshape(
        inner * rows, count
    )
    out_project(
        t_ref, range(rows), rows, z_ref, gate_ref, pick(3 * trans, inner), z1_ref, n_ref
    )
    run()
    for copy in copies:
        copy.wait()


def fast_body(pair, valid_tokens, crop_order, w_proj, w_out, w_in, w_back):
    crops, rows, count, width = pair.shape
    devices = lax.axis_size("section") * lax.axis_size("row")
    inner, trans = w_out.shape[1], w_back.shape[1]
    swap = [(0, 1), (1, 0)]
    packed = 3 * trans + inner + w_proj.shape[2]

    vmem = pl.BlockSpec(memory_space=pltpu.VMEM)
    hbm = pl.BlockSpec(memory_space=pltpu.HBM)
    shape = jax.ShapeDtypeStruct
    flat = pltpu.VMEM((rows * count, width), BF16)
    gates = shape((rows * count, width), F32)
    sems = pltpu.SemaphoreType.DMA

    def call(kernel, name, out_shape, n_in, scratch=(), out_specs=None, in_spec=vmem, cost=None):
        many = isinstance(out_shape, tuple)
        specs = out_specs or ((vmem,) * len(out_shape) if many else vmem)
        return pl.pallas_call(
            kernel,
            out_shape=out_shape,
            in_specs=[in_spec] * n_in,
            out_specs=specs,
            scratch_shapes=list(scratch),
            compiler_params=LIMIT,
            cost_estimate=cost,
            name=name,
        )

    def exchange(value):
        return lax.all_to_all(value, ("section", "row"), split_axis=0, concat_axis=0, tiled=True)

    inputs = (crop_order, valid_tokens, pair, w_proj, w_in, w_back, w_out)
    lr, own, z, owns, masks = call(
        functools.partial(first_kernel, inner),
        "first",
        (
            shape((devices, rows // 2 + 1, 8, count), BF16),
            shape((packed, width), BF16),
            shape((rows, count, width), BF16),
            shape((8, count), F32),
            shape((3, 8, count), F32),
        ),
        len(inputs),
        [
            pltpu.SMEM(crop_order.shape, jnp.int32),
            pltpu.SMEM(valid_tokens.shape, jnp.int32),
            pltpu.VMEM(pair.shape, BF16),
            pltpu.VMEM(w_proj.shape[1:], BF16),
            sems((6 + (2 * trans + w_proj.shape[2]) // width,)),
        ],
        in_spec=hbm,
    )(*[pltpu.with_memory_space_constraint(x, pltpu.HBM) for x in inputs])

    sides = exchange(lr)
    other = lax.ppermute(own, "section", swap)
    light = pl.CostEstimate(flops=34 * 10**6, bytes_accessed=10**6, transcendentals=2 * 10**5)
    gate = call(
        functools.partial(gates_kernel, 0, inner, trans), "gates", gates, 3, cost=light
    )(z, own, other)
    tri_scratch = [
        pltpu.VMEM((4 * count, count), F32),
        pltpu.VMEM((32, count), F32),
        pltpu.VMEM((CHANNELS, 32, count), F32),
    ]
    tri = exchange(
        call(
            first_triangle_kernel, "triangle", shape((devices, 2, 8, count), BF16), 1, tri_scratch
        )(sides)
    )
    work = [
        pltpu.VMEM((8 * inner, count), F32),
        pltpu.VMEM(w_in.shape[1:], BF16),
        pltpu.VMEM(w_back.shape[1:], BF16),
        flat,
        flat,
    ]
    halves = shape((rows // 2, count, width), BF16)
    lr, keep, send = call(
        functools.partial(update_kernel, inner, trans),
        "update",
        (shape((devices, 3, 8, count), BF16), halves, halves),
        7,
        work + [flat],
    )(tri, gate, z, own, other, masks, owns)

    sides = exchange(lr)
    came = lax.ppermute(send, "section", swap)
    z = call(join_kernel, "join", shape((rows, count, width), BF16), 2)(keep, came)
    gate = call(
        functools.partial(gates_kernel, 1, inner, trans), "gates_last", gates, 3, cost=light
    )(z, own, other)
    tri_scratch[1] = pltpu.VMEM((64, count), F32)
    tri = exchange(
        call(
            last_triangle_kernel,
            "triangle_last",
            shape((devices, CHANNELS, 8, count), BF16),
            2,
            tri_scratch,
        )(sides, owns)
    )
    out = call(
        functools.partial(last_kernel, inner, trans),
        "last",
        shape((rows, count, width), BF16),
        5,
        work + [pltpu.VMEM((rows, count, width), BF16), sems((rows * count // STEP,))],
        out_specs=hbm,
    )(tri, gate, z, own, other)
    return out[None]


def pair_block(state, valid, row_start, w_proj, w_out, w_in, w_back):
    rows_here, count, width = state.shape
    inner, trans = w_out.shape[0], w_back.shape[0]
    normed = layer_norm(state.astype(F32)).astype(BF16).reshape(rows_here * count, width)
    proj = jnp.dot(normed, w_proj, preferred_element_type=F32).reshape(rows_here, count, -1)
    keep_cols = (jnp.arange(count) < valid).astype(F32)
    keep_rows = (row_start + jnp.arange(rows_here) < valid).astype(F32)
    mask = keep_rows[:, None, None] * keep_cols[None, :, None]
    left = (mask * jax.nn.sigmoid(proj[..., inner : 2 * inner]) * proj[..., :inner]).astype(BF16)
    right = (
        mask * jax.nn.sigmoid(proj[..., 3 * inner : 4 * inner]) * proj[..., 2 * inner : 3 * inner]
    ).astype(BF16)
    gate = jax.nn.sigmoid(proj[..., 4 * inner :])
    left_whole = lax.all_to_all(left, "row", split_axis=2, concat_axis=0, tiled=True)
    right_whole = lax.all_to_all(right, "row", split_axis=2, concat_axis=0, tiled=True)
    tri_part = jnp.einsum("ikc,jkc->ijc", left_whole, right_whole, preferred_element_type=F32)
    tri = lax.all_to_all(
        tri_part.astype(BF16), "row", split_axis=0, concat_axis=2, tiled=True
    ).astype(F32)
    tri_normed = layer_norm(tri).astype(BF16).reshape(rows_here * count, inner)
    update = jnp.dot(tri_normed, w_out, preferred_element_type=F32).reshape(rows_here, count, width)
    first = (state.astype(F32) + gate * update).astype(BF16)
    second = layer_norm(first.astype(F32)).astype(BF16).reshape(rows_here * count, width)
    hidden = jnp.dot(second, w_in, preferred_element_type=F32)
    act = (jax.nn.silu(hidden[:, :trans]) * hidden[:, trans:]).astype(BF16)
    back = jnp.dot(act, w_back, preferred_element_type=F32).reshape(rows_here, count, width)
    return (first.astype(F32) + back).astype(BF16)


def general_body(pair, valid_tokens, crop_order, w_proj, w_out, w_in, w_back):
    crops, rows_here = pair.shape[:2]
    row_start = lax.axis_index("row") * rows_here
    share = crops // lax.axis_size("section")
    section = lax.axis_index("section")
    weights = [
        lax.all_gather(w, "section", axis=0, tiled=True) for w in (w_proj, w_out, w_in, w_back)
    ]
    blocks = weights[0].shape[0]

    def one_crop(index, outputs):
        crop = crop_order[section * share + index]
        valid = valid_tokens[crop]
        state = lax.dynamic_index_in_dim(pair, crop, 0, keepdims=False)

        def apply_block(block, value):
            return pair_block(value, valid, row_start, *[w[block] for w in weights])

        final = lax.fori_loop(0, blocks, apply_block, state)
        return lax.dynamic_update_index_in_dim(outputs, final, index, 0)

    empty = jnp.zeros((share,) + pair.shape[1:], BF16)
    return lax.fori_loop(0, share, one_crop, empty)


def solution(mesh):
    sections, peers = mesh.shape["section"], mesh.shape["row"]

    def body(pair, valid_tokens, crop_order, w_proj, w_out, w_in, w_back):
        crops, rows, count, width = pair.shape
        inner, trans = w_out.shape[1], w_back.shape[1]
        fits = (
            sections == 2
            and crops == sections
            and w_proj.shape[0] == 1
            and rows == 8
            and count == width == 4 * SHORT
            and peers * rows == count
            and inner == 2 * CHANNELS * peers
            and w_proj.shape[2] == 3 * width
            and trans % 256 == 0
        )
        run = fast_body if fits else general_body
        return run(pair, valid_tokens, crop_order, w_proj, w_out, w_in, w_back)

    weights = P("section", None, None)
    return jax.shard_map(
        body,
        mesh=mesh,
        in_specs=(P(None, "row", None, None), P(), P(), weights, weights, weights, weights),
        out_specs=P("section", "row", None, None),
        check_vma=False,
    )
```

time: 135 us -> 61.6 us (0.46)
  blocking collectives: 50.2 us -> 10.7 us
  local copies, waits for them, and re-layouts: 19.9 us -> 0 us
  Pallas kernels: 0 us -> 11.1 us
  other arithmetic: 9.13 us -> 0 us
  waiting for transfers between devices: 31.3 us -> 23.5 us
  matrix products: 4.56 us -> 0 us
  between operations: 1.98 us -> 0.07 us
    all_gather x4 -> x0, blocking collectives: 29.2 us -> none  [the longest x1 13.2 us: on_device(): lax.all_gather(w_in, 'section', axis=0, tiled=True)]
    all_to_all x4 -> x3, waiting for transfers between devices: 31.3 us -> 16.7 us  [exchange(): lax.all_to_all(value, ('section', 'row'), split_axis=0, concat_axis=0, ti...]
    pallas_call x0 -> x8, Pallas kernels: none -> 11.1 us  [the longest x1 3.06 us: fast_body(): call(functools.partial(first_kernel, inner), 'first', (shape((devices, ro...]
    while x24 -> x0, local copies, waits for them, and re-layouts: 10.6 us -> none
    all_to_all x2 -> x1, blocking collectives: 21 us -> 10.7 us  [exchange(): lax.all_to_all(value, ('section', 'row'), split_axis=0, concat_axis=0, ti...]
    convert_element_type x12 -> x0, other arithmetic: 6.87 us -> none  [the longest x2 2.51 us: pair_block(): right = (mask * jax.nn.sigmoid(proj[..., 3 * inner:4 * inner]) * proj[......]
    ppermute x0 -> x2, waiting for transfers between devices: none -> 6.76 us  [the longest x1 5.01 us: fast_body(): came = lax.ppermute(send, 'section', swap)]
    dot_general x10 -> x0, matrix products: 4.56 us -> none  [the longest x2 1.41 us: pair_block(): hidden = jnp.dot(second, w_in, preferred_element_type=jnp.float32)]
  transfers between devices with their start and end apart: 4 -> 5, of which waited for: 4 -> 5; matrix products, arithmetic and copies ran while one was open for 0% -> 0% of each run, Pallas kernels for 0% -> 4%
where the time goes in v4:
time: 61.6 us; the launch traced here: 61.3 us
  waiting for transfers between devices  23.5 us (38%)
  starting transfers between devices  16 us (26%)
  Pallas kernels  11.1 us (18%)
  blocking collectives  10.7 us (17%)
    all_to_all x3, waiting for transfers between devices, exchange(): lax.all_to_all(value, ('section', 'row'), split_axis=0, concat_axis=0, ti...  16.7 us
    all_to_all x3, starting transfers between devices, exchange(): lax.all_to_all(value, ('section', 'row'), split_axis=0, concat_axis=0, ti...  12.5 us
    all_to_all x1, blocking collectives, exchange(): lax.all_to_all(value, ('section', 'row'), split_axis=0, concat_axis=0, ti...  10.7 us
    ppermute x1, waiting for transfers between devices, fast_body(): came = lax.ppermute(send, 'section', swap)  5.01 us
    pallas_call x1, Pallas kernels, fast_body(): call(functools.partial(first_kernel, inner), 'first', (shape((devices, ro...  3.06 us
    pallas_call x1, Pallas kernels, fast_body(): call(functools.partial(last_kernel, inner, trans), 'last', shape((rows, c...  2.39 us
    pallas_call x1, Pallas kernels, fast_body(): call(functools.partial(update_kernel, inner, trans), 'update', (shape((de...  2.16 us
    ppermute x1, starting transfers between devices, fast_body(): other = lax.ppermute(own, 'section', swap)  1.83 us
  transfers between devices with their start and end apart: 5, of which 5 were waited for; matrix products, arithmetic and copies ran while one was open for 0% of the time, Pallas kernels for 4%

profile of v4, /device:TPU:0, one launch (start us, length us, event | category | flops | bytes accessed | tf_op | source)
XLA Modules:
  0.0 61.3 jit_solution(7185030468493756715)
XLA Ops:
  0.0 3.1 %first.1 = (bf16[32,5,8,128]{3,2,1,0:T(8,128)(2,1)}, bf16[1984,128]{1,0:T(8,128)(2,1)S(1)}, bf16[8,128,128]{2,1,0:T(8,128)(2,1)S(1)}, f32[8,128]{1,0:T(8,128)S(1)}, f32[3,8,128]{2,1,0:T(8,128)S(1)}) custom-call(s32[2]{0:T(128)} %order_ref.1, s32[2]{0:T(128)} %valid_ref.1, bf16[2,8,128,128]{3,2,1,0:T(8,128)(2,1)} %pair_ref.1, bf16[1,128,384]{2,1,0:T(8,128)(2,1)} %wp_ref.1, ...), custom_call_target="tpu_custom_call" | custom-call | tf_op jit(solution)/shard_map/first/pallas_call | solution.py:437
  3.1 7.3 %all-to-all-start = ((bf16[32,5,8,128]{3,2,1,0:T(8,128)(2,1)}), bf16[32,5,8,128]{3,2,1,0:T(8,128)(2,1)S(1)}, u32[]{:S(2)}, u32[]{:S(2)}) async-start(bf16[32,5,8,128]{3,2,1,0:T(8,128)(2,1)} %get-tuple-element.13), calls=%async_computation | async-start | bytes 655360 | tf_op jit(solution)/shard_map/all_to_all | solution.py:434
  10.4 1.8 %collective-permute-start = (bf16[1984,128]{1,0:T(8,128)(2,1)S(1)}, bf16[1984,128]{1,0:T(8,128)(2,1)S(1)}, u32[]{:S(2)}, u32[]{:S(2)}) collective-permute-start(bf16[1984,128]{1,0:T(8,128)(2,1)S(1)} %get-tuple-element.15.own_ref), channel_id=1, source_target_pairs={{0,16},{16,0},{1,17},{17,1},{2,18},{18,2},{3,19},{19,3},{4,20},{20... | collective-permute-start | bytes 1523720 | tf_op jit(solution)/shard_map/ppermute | solution.py:459
  12.2 9.8 %all-to-all-done.in_ref = bf16[32,5,8,128]{3,2,1,0:T(8,128)(2,1)S(1)} async-done(((bf16[32,5,8,128]{3,2,1,0:T(8,128)(2,1)}), bf16[32,5,8,128]{3,2,1,0:T(8,128)(2,1)S(1)}, u32[]{:S(2)}, u32[]{:S(2)}) %all-to-all-start) | async-done | bytes 327712 | tf_op jit(solution)/shard_map/all_to_all | solution.py:434
  22.1 1.2 %triangle.1 = bf16[32,2,8,128]{3,2,1,0:T(8,128)(2,1)} custom-call(bf16[32,5,8,128]{3,2,1,0:T(8,128)(2,1)S(1)} %all-to-all-done.in_ref), custom_call_target="tpu_custom_call" | custom-call | tf_op jit(solution)/shard_map/triangle/pallas_call | solution.py:470
  23.3 2.6 %all-to-all-start.1 = ((bf16[32,2,8,128]{3,2,1,0:T(8,128)(2,1)}), bf16[32,2,8,128]{3,2,1,0:T(8,128)(2,1)S(1)}, u32[]{:S(2)}, u32[]{:S(2)}) async-start(bf16[32,2,8,128]{3,2,1,0:T(8,128)(2,1)} %triangle.1), calls=%async_computation.1 | async-start | bytes 262144 | tf_op jit(solution)/shard_map/all_to_all | solution.py:434
  25.9 1.8 %collective-permute-done.other_ref = bf16[1984,128]{1,0:T(8,128)(2,1)S(1)} collective-permute-done((bf16[1984,128]{1,0:T(8,128)(2,1)S(1)}, bf16[1984,128]{1,0:T(8,128)(2,1)S(1)}, u32[]{:S(2)}, u32[]{:S(2)}) %collective-permute-start) | collective-permute-done | bytes 507936 | tf_op jit(solution)/shard_map/ppermute | solution.py:459
  27.6 0.5 gates.1.gate_ref
  28.1 6.0 %all-to-all-done.1.tri_ref = bf16[32,2,8,128]{3,2,1,0:T(8,128)(2,1)S(1)} async-done(((bf16[32,2,8,128]{3,2,1,0:T(8,128)(2,1)}), bf16[32,2,8,128]{3,2,1,0:T(8,128)(2,1)S(1)}, u32[]{:S(2)}, u32[]{:S(2)}) %all-to-all-start.1) | async-done | bytes 131104 | tf_op jit(solution)/shard_map/all_to_all | solution.py:434
  34.1 2.2 %update.1 = (bf16[32,3,8,128]{3,2,1,0:T(8,128)(2,1)S(1)}, bf16[4,128,128]{2,1,0:T(8,128)(2,1)S(1)}, bf16[4,128,128]{2,1,0:T(8,128)(2,1)S(1)}) custom-call(bf16[32,2,8,128]{3,2,1,0:T(8,128)(2,1)S(1)} %all-to-all-done.1.tri_ref, f32[1024,128]{1,0:T(8,128)S(1)} %gates.1.gate_ref, bf16[8,128,128]{2,1,0:T(8,128)(2,1)S(1)} %get-tuple-element.14.z_ref, ...), custom_call_target="tpu_custom_call" | custom-call | tf_op jit(solution)/shard_map/update/pallas_call | solution.py:482
  36.3 10.7 %all_to_all.20.in_ref = bf16[32,3,8,128]{3,2,1,0:T(8,128)(2,1)S(1)} all-to-all(bf16[32,3,8,128]{3,2,1,0:T(8,128)(2,1)S(1)} %get-tuple-element.18), channel_id=1, replica_groups=mesh['section'=2,'row'=16] {'section','row'}, dimensions={0} | all-to-all | bytes 393216 | tf_op jit(solution)/shard_map/all_to_all | solution.py:434
  46.9 1.2 %triangle_last.1 = bf16[32,2,8,128]{3,2,1,0:T(8,128)(2,1)} custom-call(bf16[32,3,8,128]{3,2,1,0:T(8,128)(2,1)S(1)} %all_to_all.20.in_ref, f32[8,128]{1,0:T(8,128)S(1)} %get-tuple-element.17.owns_ref), custom_call_target="tpu_custom_call" | custom-call | tf_op jit(solution)/shard_map/triangle_last/pallas_call | solution.py:498
  48.1 2.6 %all-to-all-start.3 = ((bf16[32,2,8,128]{3,2,1,0:T(8,128)(2,1)}), bf16[32,2,8,128]{3,2,1,0:T(8,128)(2,1)S(1)}, u32[]{:S(2)}, u32[]{:S(2)}) async-start(bf16[32,2,8,128]{3,2,1,0:T(8,128)(2,1)} %triangle_last.1), calls=%async_computation.3 | async-start | bytes 262144 | tf_op jit(solution)/shard_map/all_to_all | solution.py:434
  50.7 1.7 %collective-permute-start.1 = (bf16[4,128,128]{2,1,0:T(8,128)(2,1)S(1)}, bf16[4,128,128]{2,1,0:T(8,128)(2,1)S(1)}, u32[]{:S(2)}, u32[]{:S(2)}) collective-permute-start(bf16[4,128,128]{2,1,0:T(8,128)(2,1)S(1)} %get-tuple-element.20), channel_id=1, source_target_pairs={{0,16},{16,0},{1,17},{17,1},{2,18},{18,2},{3,19},{19,3},{4,20},{20... | collective-permute-start | bytes 393224 | tf_op jit(solution)/shard_map/ppermute | solution.py:491
  52.4 5.0 %collective-permute-done.1.other_ref = bf16[4,128,128]{2,1,0:T(8,128)(2,1)S(1)} collective-permute-done((bf16[4,128,128]{2,1,0:T(8,128)(2,1)S(1)}, bf16[4,128,128]{2,1,0:T(8,128)(2,1)S(1)}, u32[]{:S(2)}, u32[]{:S(2)}) %collective-permute-start.1) | collective-permute-done | bytes 131104 | tf_op jit(solution)/shard_map/ppermute | solution.py:491
  57.4 0.1 join.1.z_ref
  57.5 0.5 gates_last.1.gate_ref
  58.0 0.9 %all-to-all-done.3.tri_ref = bf16[32,2,8,128]{3,2,1,0:T(8,128)(2,1)S(1)} async-done(((bf16[32,2,8,128]{3,2,1,0:T(8,128)(2,1)}), bf16[32,2,8,128]{3,2,1,0:T(8,128)(2,1)S(1)}, u32[]{:S(2)}, u32[]{:S(2)}) %all-to-all-start.3) | async-done | bytes 131104 | tf_op jit(solution)/shard_map/all_to_all | solution.py:434
  58.9 2.4 %last.1 = bf16[8,128,128]{2,1,0:T(8,128)(2,1)} custom-call(bf16[32,2,8,128]{3,2,1,0:T(8,128)(2,1)S(1)} %all-to-all-done.3.tri_ref, f32[1024,128]{1,0:T(8,128)S(1)} %gates_last.1.gate_ref, bf16[8,128,128]{2,1,0:T(8,128)(2,1)S(1)} %join.1.z_ref, bf16[1984,128]{1,0:T(8,128)(2,1)S(1)} %get-tuple-element.15.own_ref, ...), custom_call_target="tpu_custom_call" | custom-call | tf_op jit(solution)/shard_map/last/pallas_call | solution.py:506
Async XLA Ops:
  3.1 19.0 %all-to-all-start = ((bf16[32,5,8,128]{3,2,1,0:T(8,128)(2,1)}), bf16[32,5,8,128]{3,2,1,0:T(8,128)(2,1)S(1)}, u32[]{:S(2)}, u32[]{:S(2)}) async-start(bf16[32,5,8,128]{3,2,1,0:T(8,128)(2,1)} %get-tuple-element.13), calls=%async_computation | async-start | bytes 655360 | tf_op jit(solution)/shard_map/all_to_all | solution.py:434
  10.4 17.2 %collective-permute-start = (bf16[1984,128]{1,0:T(8,128)(2,1)S(1)}, bf16[1984,128]{1,0:T(8,128)(2,1)S(1)}, u32[]{:S(2)}, u32[]{:S(2)}) collective-permute-start(bf16[1984,128]{1,0:T(8,128)(2,1)S(1)} %get-tuple-element.15.own_ref), channel_id=1, source_target_pairs={{0,16},{16,0},{1,17},{17,1},{2,18},{18,2},{3,19},{19,3},{4,20},{20... | collective-permute-start | bytes 1523720 | tf_op jit(solution)/shard_map/ppermute | solution.py:459
  23.3 10.8 %all-to-all-start.1 = ((bf16[32,2,8,128]{3,2,1,0:T(8,128)(2,1)}), bf16[32,2,8,128]{3,2,1,0:T(8,128)(2,1)S(1)}, u32[]{:S(2)}, u32[]{:S(2)}) async-start(bf16[32,2,8,128]{3,2,1,0:T(8,128)(2,1)} %triangle.1), calls=%async_computation.1 | async-start | bytes 262144 | tf_op jit(solution)/shard_map/all_to_all | solution.py:434
  48.1 10.8 %all-to-all-start.3 = ((bf16[32,2,8,128]{3,2,1,0:T(8,128)(2,1)}), bf16[32,2,8,128]{3,2,1,0:T(8,128)(2,1)S(1)}, u32[]{:S(2)}, u32[]{:S(2)}) async-start(bf16[32,2,8,128]{3,2,1,0:T(8,128)(2,1)} %triangle_last.1), calls=%async_computation.3 | async-start | bytes 262144 | tf_op jit(solution)/shard_map/all_to_all | solution.py:434
  50.7 6.7 %collective-permute-start.1 = (bf16[4,128,128]{2,1,0:T(8,128)(2,1)S(1)}, bf16[4,128,128]{2,1,0:T(8,128)(2,1)S(1)}, u32[]{:S(2)}, u32[]{:S(2)}) collective-permute-start(bf16[4,128,128]{2,1,0:T(8,128)(2,1)S(1)} %get-tuple-element.20), channel_id=1, source_target_pairs={{0,16},{16,0},{1,17},{17,1},{2,18},{18,2},{3,19},{19,3},{4,20},{20... | collective-permute-start | bytes 393224 | tf_op jit(solution)/shard_map/ppermute | solution.py:491

commit v5 on v4

--- a/solution.py
+++ b/solution.py
@@ -7,6 +7,7 @@
 from jax.experimental.pallas import tpu as pltpu
 from jax.sharding import PartitionSpec as P
 
+
 F32 = jnp.float32
 BF16 = jnp.bfloat16
 STEP = 512
@@ -33,19 +34,24 @@
 
 
 def tile_weights(weights, inner):
-    total = 8 * inner
-    row = lax.broadcasted_iota(jnp.int32, (total, 4 * inner), 0)
-    column = lax.broadcasted_iota(jnp.int32, (total, 4 * inner), 1)
-    gates, rest = lax.div(row, 4 * inner), lax.rem(row, 4 * inner)
-    peer, slot = lax.div(rest, 8), lax.rem(rest, 8)
-    half, side, channel = lax.div(slot, 4), lax.rem(lax.div(slot, 2), 2), lax.rem(slot, 2)
-    source = side * (2 * inner) + gates * inner + peer * CHANNELS + channel
-    parts = []
-    for h in range(2):
-        chosen = jnp.logical_and(column == source, half == h)
-        pick = jnp.where(chosen, 1.0, 0.0).astype(BF16)
-        parts.append(contract(pick, weights, 1, 1).astype(BF16))
-    return jnp.concatenate(parts, -1)
+    row = lax.broadcasted_iota(jnp.int32, (4 * inner, 2 * inner), 0)
+    column = lax.broadcasted_iota(jnp.int32, (4 * inner, 2 * inner), 1)
+    peer, slot = lax.div(row, 8), lax.rem(row, 4)
+    source = lax.div(slot, 2) * inner + peer * CHANNELS + lax.rem(slot, 2)
+    pick = jnp.where(column == source, 1.0, 0.0).astype(BF16)
+    left, right = weights[:, : 2 * inner].astype(F32), weights[:, 2 * inner :].astype(F32)
+    low = lax.broadcasted_iota(jnp.int32, left.shape, 1) < inner
+    values = jnp.where(low, left, pltpu.roll(right, inner, 1)).astype(BF16)
+    gates = jnp.where(low, pltpu.roll(left, inner, 1), right).astype(BF16)
+    both = [contract(pick, part, 1, 1) for part in (values, gates)]
+    half = lax.rem(lax.broadcasted_iota(jnp.int32, both[0].shape, 0), 8) < 4
+    return jnp.concatenate(
+        [
+            jnp.concatenate([jnp.where(half, part, 0.0), jnp.where(half, 0.0, part)], -1)
+            for part in both
+        ],
+        0,
+    ).astype(BF16)
 
 
 def put_tiles(turned, halves, masks, lr_ref, first, inner):
@@ -82,7 +88,57 @@
 
 
 def first_kernel(
-    inner,
+    inner, order_ref, valid_ref, pair_ref, wp_ref, out_ref, lr_ref, order_s, valid_s, both_ref, w_ref, sems
+):
+    rows, count, width = pair_ref.shape[1:]
+    copies = []
+
+    def send(first, tiles):
+        part = pl.ds(first, tiles)
+        copies.append(
+            pltpu.make_async_copy(lr_ref.at[:, part], out_ref.at[:, part], sems.at[4 + len(copies)])
+        )
+        copies[-1].start()
+
+    @pl.when(lax.axis_index("section") == 0)
+    def _():
+        weights = pltpu.make_async_copy(wp_ref.at[0], w_ref, sems.at[2])
+        weights.start()
+        state = pltpu.make_async_copy(pair_ref, both_ref, sems.at[3])
+        state.start()
+        scalars = read_scalars(order_ref, valid_ref, order_s, valid_s, sems)
+        weights.wait()
+        turned = tile_weights(w_ref[:, : 4 * inner], inner)
+        for copy in scalars:
+            copy.wait()
+        full = jnp.where(valid_s[1] > valid_s[0], 1, 0)
+        short = 1 - full
+        start = lax.axis_index("row") * rows
+        state.wait()
+        for t in range(0, rows // 2, 2):
+            normed = [row_norm(both_ref[full, 2 * t + r]) for r in range(4)]
+            put_tiles(
+                turned,
+                [normed[:2], normed[2:]],
+                [full_mask(start + 2 * t + r, valid_s[full], count) for r in (0, 2)],
+                lr_ref,
+                t,
+                inner,
+            )
+            send(t, 2)
+        fours = [
+            row_norm(both_ref[short, 4 * h : 4 * h + 4, :SHORT].reshape(4 * SHORT, width))
+            for h in range(2)
+        ]
+        put_tiles(
+            turned, [fours], [short_mask(start, valid_s[short], count)], lr_ref, rows // 2, inner
+        )
+        send(rows // 2, 1)
+        for copy in copies:
+            copy.wait()
+
+
+def stage_kernel(
     order_ref,
     valid_ref,
     pair_ref,
@@ -90,45 +146,40 @@
     w_in_ref,
     w_back_ref,
     w_out_ref,
-    lr_ref,
+    after_ref,
     pack_ref,
     z_ref,
+    n_ref,
     owns_ref,
     masks_ref,
     order_s,
     valid_s,
     both_ref,
-    w_ref,
     sems,
 ):
-    rows, count, width = pair_ref.shape[1:]
+    rows, count, width = z_ref.shape
     trans = w_back_ref.shape[1]
-    scalars = read_scalars(order_ref, valid_ref, order_s, valid_s, sems)
-    weights = pltpu.make_async_copy(wp_ref.at[0], w_ref, sems.at[2])
-    weights.start()
-    state = pltpu.make_async_copy(pair_ref, both_ref, sems.at[3])
-    state.start()
     sources = [w_in_ref.at[0, :, pl.ds(j * width, width)] for j in range(2 * trans // width)]
     sources += [w_back_ref.at[0], w_out_ref.at[0]]
-    sources += [wp_ref.at[0, :, pl.ds(j * width, width)] for j in range(w_ref.shape[1] // width)]
+    sources += [wp_ref.at[0, :, pl.ds(j * width, width)] for j in range(wp_ref.shape[2] // width)]
     packing, at = [], 0
     for i, source in enumerate(sources):
         size = source.shape[0]
         packing.append(
-            pltpu.make_async_copy(source, pack_ref.at[pl.ds(at, size)], sems.at[4 + i])
+            pltpu.make_async_copy(source, pack_ref.at[pl.ds(at, size)], sems.at[3 + i])
         )
         packing[-1].start()
         at += size
-    weights.wait()
-    turned = tile_weights(w_ref[:, : 4 * inner], inner)
+    scalars = read_scalars(order_ref, valid_ref, order_s, valid_s, sems)
+    state = pltpu.make_async_copy(pair_ref, both_ref, sems.at[2])
+    state.start()
     for copy in scalars:
         copy.wait()
     section = lax.axis_index("section")
     full = jnp.where(valid_s[1] > valid_s[0], 1, 0)
     short = 1 - full
     owns_ref[...] = jnp.full(owns_ref.shape, jnp.where(order_s[section] == full, 1.0, 0.0))
-    start = lax.axis_index("row") * rows
-    mine = start + (rows // 2) * section
+    mine = lax.axis_index("row") * rows + (rows // 2) * section
     masks_ref[0] = full_mask(mine, valid_s[full], count)
     masks_ref[1] = full_mask(mine + 2, valid_s[full], count)
     masks_ref[2] = short_mask(mine, valid_s[short], count)
@@ -136,21 +187,7 @@
     half = pl.ds((rows // 2) * section, rows // 2)
     z_ref[: rows // 2] = both_ref[full, half]
     z_ref[rows // 2 :] = both_ref[short, half]
-    for t in range(0, rows // 2, 2):
-        normed = [row_norm(both_ref[full, 2 * t + r]) for r in range(4)]
-        put_tiles(
-            turned,
-            [normed[:2], normed[2:]],
-            [full_mask(start + 2 * t + r, valid_s[full], count) for r in (0, 2)],
-            lr_ref,
-            t,
-            inner,
-        )
-    fours = [
-        row_norm(both_ref[short, 4 * h : 4 * h + 4, :SHORT].reshape(4 * SHORT, width))
-        for h in range(2)
-    ]
-    put_tiles(turned, [fours], [short_mask(start, valid_s[short], count)], lr_ref, rows // 2, inner)
+    rows_norm(z_ref, n_ref)
     for copy in packing:
         copy.wait()
 
@@ -188,7 +225,7 @@
     return results
 
 
-def first_triangle_kernel(in_ref, out_ref, wide_ref, few_ref, place_ref):
+def first_triangle_kernel(in_ref, after_ref, out_ref, wide_ref, few_ref, place_ref):
     peers, count = in_ref.shape[0], in_ref.shape[-1]
     rows = peers // 2
     tiles = in_ref.shape[1] - 1
@@ -246,26 +283,43 @@
     return pick
 
 
-def gates_kernel(block, inner, trans, z_ref, own_ref, other_ref, gate_ref):
-    rows, count, width = z_ref.shape
+def ready_kernel(block, inner, trans, n_ref, own_ref, other_ref, after_ref, gate_ref, in_ref, back_ref, w_out_ref, *more):
+    count = width = n_ref.shape[1]
+    rows = n_ref.shape[0] // count
     pick = picker(block, own_ref, other_ref)
-    weights = pick(3 * trans + inner + 2 * width, width)
-    for r in range(0, rows, 2):
-        normed = row_norm(z_ref[r : r + 2].reshape(2 * count, width))
-        gate_ref[r * count : (r + 2) * count, :] = jax.nn.sigmoid(
-            jnp.dot(normed, weights, preferred_element_type=F32)
-        )
-
-
-def join_kernel(keep_ref, other_ref, z_ref):
+    projections = 3 * trans + inner
+    weights = pick(projections + 2 * width, width)
+    for r in range(0, rows, 4):
+        here = slice(r * count, (r + 4) * count)
+        gate_ref[here, :] = jax.nn.sigmoid(
+            jnp.dot(n_ref[here, :], weights, preferred_element_type=F32)
+        )
+    for j in range(2 * trans // width):
+        in_ref[:, j * width : (j + 1) * width] = pick(j * width, width)
+    back_ref[...] = pick(2 * trans, trans)
+    w_out_ref[...] = pick(3 * trans, inner)
+    if more:
+        pick = picker(block + 1, own_ref, other_ref)
+        sides = [pick(projections + j * width, width) for j in range(2)]
+        more[0][...] = tile_weights(jnp.concatenate(sides, -1), inner)
+
+
+def rows_norm(z_ref, n_ref):
+    rows, count, _ = z_ref.shape
+    for r in range(rows):
+        n_ref[r * count : (r + 1) * count, :] = row_norm(z_ref[r])
+
+
+def join_kernel(keep_ref, other_ref, z_ref, n_ref):
     half = keep_ref.shape[0]
     first = lax.axis_index("section") == 0
     z_ref[:half] = jnp.where(first, keep_ref[...], other_ref[...])
     z_ref[half:] = jnp.where(first, other_ref[...], keep_ref[...])
+    rows_norm(z_ref, n_ref)
 
 
 def out_project(t_ref, offsets, stride, z_ref, gate_ref, w_out, z1_ref, n_ref):
-    rows, count, width = z_ref.shape
+    rows, count, _ = z_ref.shape
     inner = w_out.shape[0]
     for r in range(rows):
         here = slice(r * count, (r + 1) * count)
@@ -276,81 +330,70 @@
         n_ref[here, :] = row_norm(first)
 
 
-def transition(pick, trans, in_ref, back_ref, n_ref, z1_ref, width, finish):
-    hidden = 2 * trans
-    for j in range(hidden // width):
-        in_ref[:, j * width : (j + 1) * width] = pick(j * width, width)
-    back_ref[...] = pick(hidden, trans)
-
-    def run():
-        piece = 256
-        for m in range(n_ref.shape[0] // STEP):
-            here = slice(m * STEP, (m + 1) * STEP)
-            normed = n_ref[here, :]
-            acts = []
-            for j in range(trans // piece):
-                gate_w = in_ref[:, j * piece : (j + 1) * piece]
-                up_w = in_ref[:, trans + j * piece : trans + (j + 1) * piece]
-                gate = jnp.dot(normed, gate_w, preferred_element_type=F32)
-                up = jnp.dot(normed, up_w, preferred_element_type=F32)
-                acts.append((jax.nn.silu(gate) * up).astype(BF16))
-            back = jnp.dot(jnp.concatenate(acts, -1), back_ref[...], preferred_element_type=F32)
-            finish(m, (z1_ref[here, :].astype(F32) + back).astype(BF16))
-
-    return run
+def transition(in_ref, back_ref, n_ref, z1_ref, finish):
+    trans, piece = back_ref.shape[0], 256
+    for m in range(n_ref.shape[0] // STEP):
+        here = slice(m * STEP, (m + 1) * STEP)
+        normed = n_ref[here, :]
+        acts = []
+        for j in range(trans // piece):
+            gate_w = in_ref[:, j * piece : (j + 1) * piece]
+            up_w = in_ref[:, trans + j * piece : trans + (j + 1) * piece]
+            gate = jnp.dot(normed, gate_w, preferred_element_type=F32)
+            up = jnp.dot(normed, up_w, preferred_element_type=F32)
+            acts.append((jax.nn.silu(gate) * up).astype(BF16))
+        back = jnp.dot(jnp.concatenate(acts, -1), back_ref[...], preferred_element_type=F32)
+        finish(m, (z1_ref[here, :].astype(F32) + back).astype(BF16))
+
+
+def norm_kernel(inner, tri_ref, t_ref):
+    count = t_ref.shape[1]
+    for q in range(2):
+        part = tri_ref[:, q].astype(F32)
+
+        def mean(value):
+            total = jnp.sum(value, 0)
+            return (total + pltpu.roll(total, 4, 0)) * (1.0 / inner)
+
+        centred = part - mean(part)[None]
+        var = mean(centred * centred)
+        normed = centred * lax.rsqrt(var + 1e-05)[None]
+        t_ref[q * 4 * inner : (q + 1) * 4 * inner, :] = normed.reshape(4 * inner, count)
 
 
 def update_kernel(
     inner,
-    trans,
-    tri_ref,
+    t_ref,
+    z_ref,
     gate_ref,
-    z_ref,
-    own_ref,
-    other_ref,
+    in_ref,
+    back_ref,
+    w_out_ref,
+    turned_ref,
     masks_ref,
     owns_ref,
     lr_ref,
     keep_ref,
     send_ref,
-    t_ref,
-    in_ref,
-    back_ref,
     n_ref,
     z1_ref,
     o_ref,
 ):
     rows, count, width = z_ref.shape
     half = rows // 2
-    pick = picker(0, own_ref, other_ref)
+    offsets = [q * 4 * inner + r for q in range(2) for r in range(half)]
+    out_project(t_ref, offsets, 4, z_ref, gate_ref, w_out_ref[...], z1_ref, n_ref)
 
     def finish(m, done):
         o_ref[m * STEP : (m + 1) * STEP, :] = done
 
-    run = transition(pick, trans, in_ref, back_ref, n_ref, z1_ref, width, finish)
-    for q in range(2):
-        part = tri_ref[:, q].astype(F32)
-
-        def mean(value):
-            total = jnp.sum(value, 0)
-            return (total + pltpu.roll(total, 4, 0)) * (1.0 / inner)
-
-        centred = part - mean(part)[None]
-        var = mean(centred * centred)
-        normed = centred * lax.rsqrt(var + 1e-05)[None]
-        t_ref[q * 4 * inner : (q + 1) * 4 * inner, :] = normed.reshape(4 * inner, count)
-    offsets = [q * 4 * inner + r for q in range(2) for r in range(half)]
-    out_project(t_ref, offsets, 4, z_ref, gate_ref, pick(3 * trans, inner), z1_ref, n_ref)
-    run()
+    transition(in_ref, back_ref, n_ref, z1_ref, finish)
     owns = (owns_ref[:1, :] > 0.5)[None]
     full = o_ref[: half * count, :].reshape(half, count, width)
     short = o_ref[half * count :, :].reshape(half, count, width)
     keep_ref[...] = jnp.where(owns, full.astype(F32), short.astype(F32)).astype(BF16)
     send_ref[...] = jnp.where(owns, short.astype(F32), full.astype(F32)).astype(BF16)
-    next_pick = picker(1, own_ref, other_ref)
-    at = 3 * trans + inner
-    weights = jnp.concatenate([next_pick(at, width), next_pick(at + width, width)], -1)
-    turned = tile_weights(weights, inner)
+    turned = turned_ref[...]
     normed = [row_norm(o_ref[r * count : (r + 1) * count, :]) for r in range(half)]
     put_tiles(
         turned, [normed[:2], normed[2:]], [masks_ref[0], masks_ref[1]], lr_ref, 0, inner
@@ -365,23 +408,20 @@
 
 def last_kernel(
     inner,
-    trans,
     tri_ref,
+    z_ref,
     gate_ref,
-    z_ref,
-    own_ref,
-    other_ref,
+    in_ref,
+    back_ref,
+    w_out_ref,
     out_ref,
     t_ref,
-    in_ref,
-    back_ref,
     n_ref,
     z1_ref,
     o_ref,
     sems,
 ):
     rows, count, width = z_ref.shape
-    pick = picker(1, own_ref, other_ref)
     copies = []
 
     def finish(m, done):
@@ -390,20 +430,17 @@
         copies.append(pltpu.make_async_copy(o_ref.at[part], out_ref.at[part], sems.at[m]))
         copies[-1].start()
 
-    run = transition(pick, trans, in_ref, back_ref, n_ref, z1_ref, width, finish)
     t_ref[...] = layer_norm(tri_ref[...].reshape(inner, rows, count).astype(F32), 0).reshape(
         inner * rows, count
     )
-    out_project(
-        t_ref, range(rows), rows, z_ref, gate_ref, pick(3 * trans, inner), z1_ref, n_ref
-    )
-    run()
+    out_project(t_ref, range(rows), rows, z_ref, gate_ref, w_out_ref[...], z1_ref, n_ref)
+    transition(in_ref, back_ref, n_ref, z1_ref, finish)
     for copy in copies:
         copy.wait()
 
 
 def fast_body(pair, valid_tokens, crop_order, w_proj, w_out, w_in, w_back):
-    crops, rows, count, width = pair.shape
+    _, rows, count, width = pair.shape
     devices = lax.axis_size("section") * lax.axis_size("row")
     inner, trans = w_out.shape[1], w_back.shape[1]
     swap = [(0, 1), (1, 0)]
@@ -411,56 +448,72 @@
 
     vmem = pl.BlockSpec(memory_space=pltpu.VMEM)
     hbm = pl.BlockSpec(memory_space=pltpu.HBM)
+    anywhere = pl.BlockSpec(memory_space=pl.ANY)
     shape = jax.ShapeDtypeStruct
     flat = pltpu.VMEM((rows * count, width), BF16)
     gates = shape((rows * count, width), F32)
     sems = pltpu.SemaphoreType.DMA
 
-    def call(kernel, name, out_shape, n_in, scratch=(), out_specs=None, in_spec=vmem, cost=None):
+    def call(kernel, out_shape, n_in, scratch=(), out_specs=None, in_spec=vmem, cost=None):
         many = isinstance(out_shape, tuple)
         specs = out_specs or ((vmem,) * len(out_shape) if many else vmem)
         return pl.pallas_call(
             kernel,
             out_shape=out_shape,
-            in_specs=[in_spec] * n_in,
+            in_specs=[in_spec] * n_in if isinstance(n_in, int) else n_in,
             out_specs=specs,
             scratch_shapes=list(scratch),
             compiler_params=LIMIT,
             cost_estimate=cost,
-            name=name,
         )
 
     def exchange(value):
         return lax.all_to_all(value, ("section", "row"), split_axis=0, concat_axis=0, tiled=True)
 
-    inputs = (crop_order, valid_tokens, pair, w_proj, w_in, w_back, w_out)
-    lr, own, z, owns, masks = call(
+    inputs = [
+        pltpu.with_memory_space_constraint(x, pltpu.HBM)
+        for x in (crop_order, valid_tokens, pair, w_proj, w_in, w_back, w_out)
+    ]
+    scalars = [
+        pltpu.SMEM(crop_order.shape, jnp.int32),
+        pltpu.SMEM(valid_tokens.shape, jnp.int32),
+        pltpu.VMEM(pair.shape, BF16),
+    ]
+    tokens = shape((rows * count, width), BF16)
+    lr_shape = (devices, rows // 2 + 1, 8, count)
+    lr = call(
         functools.partial(first_kernel, inner),
-        "first",
+        shape(lr_shape, BF16),
+        4,
+        [pltpu.VMEM(lr_shape, BF16)]
+        + scalars
+        + [pltpu.VMEM(w_proj.shape[1:], BF16), sems((5 + rows // 4,))],
+        out_specs=hbm,
+        in_spec=hbm,
+    )(*inputs[:4])
+    light = pl.CostEstimate(flops=34 * 10**6, bytes_accessed=10**6, transcendentals=2 * 10**5)
+    own, z, normed, owns, masks = call(
+        stage_kernel,
         (
-            shape((devices, rows // 2 + 1, 8, count), BF16),
             shape((packed, width), BF16),
             shape((rows, count, width), BF16),
+            tokens,
             shape((8, count), F32),
             shape((3, 8, count), F32),
         ),
-        len(inputs),
-        [
-            pltpu.SMEM(crop_order.shape, jnp.int32),
-            pltpu.SMEM(valid_tokens.shape, jnp.int32),
-            pltpu.VMEM(pair.shape, BF16),
-            pltpu.VMEM(w_proj.shape[1:], BF16),
-            sems((6 + (2 * trans + w_proj.shape[2]) // width,)),
-        ],
-        in_spec=hbm,
-    )(*[pltpu.with_memory_space_constraint(x, pltpu.HBM) for x in inputs])
+        [hbm] * 7 + [anywhere],
+        scalars + [sems((5 + (2 * trans + w_proj.shape[2]) // width,))],
+        cost=light,
+    )(*inputs, lr)
 
     sides = exchange(lr)
     other = lax.ppermute(own, "section", swap)
-    light = pl.CostEstimate(flops=34 * 10**6, bytes_accessed=10**6, transcendentals=2 * 10**5)
-    gate = call(
-        functools.partial(gates_kernel, 0, inner, trans), "gates", gates, 3, cost=light
-    )(z, own, other)
+    readied = (
+        gates,
+        shape(w_in.shape[1:], BF16),
+        shape(w_back.shape[1:], BF16),
+        shape(w_out.shape[1:], BF16),
+    )
     tri_scratch = [
         pltpu.VMEM((4 * count, count), F32),
         pltpu.VMEM((32, count), F32),
@@ -468,49 +521,47 @@
     ]
     tri = exchange(
         call(
-            first_triangle_kernel, "triangle", shape((devices, 2, 8, count), BF16), 1, tri_scratch
-        )(sides)
-    )
-    work = [
-        pltpu.VMEM((8 * inner, count), F32),
-        pltpu.VMEM(w_in.shape[1:], BF16),
-        pltpu.VMEM(w_back.shape[1:], BF16),
-        flat,
-        flat,
-    ]
+            first_triangle_kernel,
+            shape((devices, 2, 8, count), BF16),
+            [vmem, anywhere],
+            tri_scratch,
+        )(sides, normed),
+    )
+    t = call(functools.partial(norm_kernel, inner), shape((8 * inner, count), F32), 1)(tri)
+    *ready, turned = call(
+        functools.partial(ready_kernel, 0, inner, trans),
+        readied + (shape((8 * inner, 2 * width), BF16),),
+        [vmem, vmem, vmem, anywhere],
+        cost=light,
+    )(normed, own, other, t)
+    work = [pltpu.VMEM((8 * inner, count), F32), flat, flat]
     halves = shape((rows // 2, count, width), BF16)
     lr, keep, send = call(
-        functools.partial(update_kernel, inner, trans),
-        "update",
+        functools.partial(update_kernel, inner),
         (shape((devices, 3, 8, count), BF16), halves, halves),
-        7,
-        work + [flat],
-    )(tri, gate, z, own, other, masks, owns)
+        9,
+        [flat] * 3,
+    )(t, z, *ready, turned, masks, owns)
 
     sides = exchange(lr)
     came = lax.ppermute(send, "section", swap)
-    z = call(join_kernel, "join", shape((rows, count, width), BF16), 2)(keep, came)
-    gate = call(
-        functools.partial(gates_kernel, 1, inner, trans), "gates_last", gates, 3, cost=light
-    )(z, own, other)
+    z, normed = call(join_kernel, (shape((rows, count, width), BF16), tokens), 2)(keep, came)
+    ready = call(
+        functools.partial(ready_kernel, 1, inner, trans), readied, [vmem, vmem, vmem, anywhere], cost=light
+    )(normed, own, other, normed)
     tri_scratch[1] = pltpu.VMEM((64, count), F32)
     tri = exchange(
         call(
-            last_triangle_kernel,
-            "triangle_last",
-            shape((devices, CHANNELS, 8, count), BF16),
-            2,
-            tri_scratch,
-        )(sides, owns)
+            last_triangle_kernel, shape((devices, CHANNELS, 8, count), BF16), 2, tri_scratch
+        )(sides, owns),
     )
     out = call(
-        functools.partial(last_kernel, inner, trans),
-        "last",
+        functools.partial(last_kernel, inner),
         shape((rows, count, width), BF16),
-        5,
+        6,
         work + [pltpu.VMEM((rows, count, width), BF16), sems((rows * count // STEP,))],
         out_specs=hbm,
-    )(tri, gate, z, own, other)
+    )(tri, z, *ready)
     return out[None]
 
 

time: 61.6 us -> 59.7 us (0.969)
  blocking collectives: 10.7 us -> 21.1 us
  waiting for transfers between devices: 23.5 us -> 13.4 us
  starting transfers between devices: 16 us -> 12.5 us
  Pallas kernels: 11.1 us -> 12.3 us
    all_to_all x1 -> x2, blocking collectives: 10.7 us -> 21.1 us  [exchange(): lax.all_to_all(value, ('section', 'row'), split_axis=0, concat_axis=0, ti...]
    all_to_all x3 -> x2, waiting for transfers between devices: 16.7 us -> 8.37 us  [exchange(): lax.all_to_all(value, ('section', 'row'), split_axis=0, concat_axis=0, ti...]
    all_to_all x3 -> x2, starting transfers between devices: 12.5 us -> 8.95 us  [exchange(): lax.all_to_all(value, ('section', 'row'), split_axis=0, concat_axis=0, ti...]
    ppermute x1, waiting for transfers between devices: 1.75 us -> 0.01 us  [fast_body(): other = lax.ppermute(own, 'section', swap)]
    pallas_call x8 -> x10, Pallas kernels: 11.1 us -> 12.3 us  [the longest x1 2.7 us: fast_body(): call(functools.partial(first_kernel, inner), shape(lr_shape, BF16), 4, [p...]
  transfers between devices with their start and end apart: 5 -> 4, of which waited for: 5 -> 3; matrix products, arithmetic and copies ran while one was open for 0% -> 0% of each run, Pallas kernels for 4% -> 6%
where the time goes in v5:
time: 59.7 us; the launch traced here: 59.4 us
  blocking collectives  21.1 us (35%)
  waiting for transfers between devices  13.4 us (22%)
  starting transfers between devices  12.5 us (21%)
  Pallas kernels  12.3 us (21%)
    all_to_all x2, blocking collectives, exchange(): lax.all_to_all(value, ('section', 'row'), split_axis=0, concat_axis=0, ti...  21.1 us
    all_to_all x2, starting transfers between devices, exchange(): lax.all_to_all(value, ('section', 'row'), split_axis=0, concat_axis=0, ti...  8.95 us
    all_to_all x2, waiting for transfers between devices, exchange(): lax.all_to_all(value, ('section', 'row'), split_axis=0, concat_axis=0, ti...  8.37 us
    ppermute x1, waiting for transfers between devices, fast_body(): came = lax.ppermute(send, 'section', swap)  5.01 us
    pallas_call x1, Pallas kernels, fast_body(): call(functools.partial(first_kernel, inner), shape(lr_shape, BF16), 4, [p...  2.7 us
    pallas_call x1, Pallas kernels, fast_body(): call(functools.partial(last_kernel, inner), shape((rows, count, width), B...  2.37 us
    pallas_call x1, Pallas kernels, fast_body(): call(stage_kernel, (shape((packed, width), BF16), shape((rows, count, wid...  2.03 us
    pallas_call x1, Pallas kernels, fast_body(): call(functools.partial(update_kernel, inner), (shape((devices, 3, 8, coun...  2 us
  transfers between devices with their start and end apart: 4, of which 3 were waited for; matrix products, arithmetic and copies ran while one was open for 0% of the time, Pallas kernels for 6%

profile of v5, /device:TPU:0, one launch (start us, length us, event | category | flops | bytes accessed | tf_op | source)
XLA Modules:
  0.0 59.4 jit_solution(6403001580424312451)
XLA Ops:
  0.0 2.7 %shard_map.73.after_ref = bf16[32,5,8,128]{3,2,1,0:T(8,128)(2,1)} custom-call(s32[2]{0:T(128)} %order_ref.3, s32[2]{0:T(128)} %valid_ref.3, bf16[2,8,128,128]{3,2,1,0:T(8,128)(2,1)} %pair_ref.3, bf16[1,128,384]{2,1,0:T(8,128)(2,1)} %wp_ref.3), custom_call_target="tpu_custom_call" | custom-call | tf_op jit(solution)/shard_map/pallas_call | solution.py:484
  2.7 6.4 %all-to-all-start = ((bf16[32,5,8,128]{3,2,1,0:T(8,128)(2,1)}), bf16[32,5,8,128]{3,2,1,0:T(8,128)(2,1)S(1)}, u32[]{:S(2)}, u32[]{:S(2)}) async-start(bf16[32,5,8,128]{3,2,1,0:T(8,128)(2,1)} %shard_map.73.after_ref), calls=%async_computation | async-start | bytes 655360 | tf_op jit(solution)/shard_map/all_to_all | solution.py:471
  9.1 2.0 %shard_map.74 = (bf16[1984,128]{1,0:T(8,128)(2,1)S(1)}, bf16[8,128,128]{2,1,0:T(8,128)(2,1)S(1)}, bf16[1024,128]{1,0:T(8,128)(2,1)S(1)}, f32[8,128]{1,0:T(8,128)S(1)}, f32[3,8,128]{2,1,0:T(8,128)S(1)}) custom-call(s32[2]{0:T(128)} %order_ref.3, s32[2]{0:T(128)} %valid_ref.3, bf16[2,8,128,128]{3,2,1,0:T(8,128)(2,1)} %pair_ref.3, bf16[1,128,384]{2,1,0:T(8,128)(2,1)} %wp_ref.3, ...), custom_call_target="tpu_custom_call" | custom-call | flops 34000000 | bytes 1000000 | tf_op jit(solution)/shard_map/pallas_call | solution.py:495
  11.1 1.8 %collective-permute-start = (bf16[1984,128]{1,0:T(8,128)(2,1)S(1)}, bf16[1984,128]{1,0:T(8,128)(2,1)S(1)}, u32[]{:S(2)}, u32[]{:S(2)}) collective-permute-start(bf16[1984,128]{1,0:T(8,128)(2,1)S(1)} %get-tuple-element.26.own_ref), channel_id=1, source_target_pairs={{0,16},{16,0},{1,17},{17,1},{2,18},{18,2},{3,19},{19,3},{4,20},{20... | collective-permute-start | bytes 1523720 | tf_op jit(solution)/shard_map/ppermute | solution.py:510
  13.0 7.8 %all-to-all-done.in_ref = bf16[32,5,8,128]{3,2,1,0:T(8,128)(2,1)S(1)} async-done(((bf16[32,5,8,128]{3,2,1,0:T(8,128)(2,1)}), bf16[32,5,8,128]{3,2,1,0:T(8,128)(2,1)S(1)}, u32[]{:S(2)}, u32[]{:S(2)}) %all-to-all-start) | async-done | bytes 327712 | tf_op jit(solution)/shard_map/all_to_all | solution.py:471
  20.8 0.6 shard_map.75
  21.3 10.5 %all_to_all.20.tri_ref = bf16[32,2,8,128]{3,2,1,0:T(8,128)(2,1)S(1)} all-to-all(bf16[32,2,8,128]{3,2,1,0:T(8,128)(2,1)S(1)} %shard_map.75), channel_id=1, replica_groups=mesh['section'=2,'row'=16] {'section','row'}, dimensions={0} | all-to-all | bytes 262144 | tf_op jit(solution)/shard_map/all_to_all | solution.py:471
  31.8 0.1 shard_map.76.after_ref.t_ref
  31.9 0.0 collective-permute-done.other_ref
  31.9 0.4 shard_map.77
  32.4 2.0 %shard_map.78 = (bf16[32,3,8,128]{3,2,1,0:T(8,128)(2,1)S(1)}, bf16[4,128,128]{2,1,0:T(8,128)(2,1)S(1)}, bf16[4,128,128]{2,1,0:T(8,128)(2,1)S(1)}) custom-call(f32[512,128]{1,0:T(8,128)S(1)} %shard_map.76.after_ref.t_ref, bf16[8,128,128]{2,1,0:T(8,128)(2,1)S(1)} %get-tuple-element.25.z_ref, f32[1024,128]{1,0:T(8,128)S(1)} %get-tuple-element.27.gate_ref, ...), custom_call_target="tpu_custom_call" | custom-call | tf_op jit(solution)/shard_map/pallas_call | solution.py:539
  34.4 10.7 %all_to_all.21.in_ref = bf16[32,3,8,128]{3,2,1,0:T(8,128)(2,1)S(1)} all-to-all(bf16[32,3,8,128]{3,2,1,0:T(8,128)(2,1)S(1)} %get-tuple-element.34), channel_id=1, replica_groups=mesh['section'=2,'row'=16] {'section','row'}, dimensions={0} | all-to-all | bytes 393216 | tf_op jit(solution)/shard_map/all_to_all | solution.py:471
  45.0 1.2 %shard_map.79 = bf16[32,2,8,128]{3,2,1,0:T(8,128)(2,1)} custom-call(bf16[32,3,8,128]{3,2,1,0:T(8,128)(2,1)S(1)} %all_to_all.21.in_ref, f32[8,128]{1,0:T(8,128)S(1)} %get-tuple-element.33.owns_ref), custom_call_target="tpu_custom_call" | custom-call | tf_op jit(solution)/shard_map/pallas_call | solution.py:554
  46.2 2.6 %all-to-all-start.3 = ((bf16[32,2,8,128]{3,2,1,0:T(8,128)(2,1)}), bf16[32,2,8,128]{3,2,1,0:T(8,128)(2,1)S(1)}, u32[]{:S(2)}, u32[]{:S(2)}) async-start(bf16[32,2,8,128]{3,2,1,0:T(8,128)(2,1)} %shard_map.79), calls=%async_computation.3 | async-start | bytes 262144 | tf_op jit(solution)/shard_map/all_to_all | solution.py:471
  48.8 1.7 %collective-permute-start.1 = (bf16[4,128,128]{2,1,0:T(8,128)(2,1)S(1)}, bf16[4,128,128]{2,1,0:T(8,128)(2,1)S(1)}, u32[]{:S(2)}, u32[]{:S(2)}) collective-permute-start(bf16[4,128,128]{2,1,0:T(8,128)(2,1)S(1)} %get-tuple-element.36), channel_id=1, source_target_pairs={{0,16},{16,0},{1,17},{17,1},{2,18},{18,2},{3,19},{19,3},{4,20},{20... | collective-permute-start | bytes 393224 | tf_op jit(solution)/shard_map/ppermute | solution.py:547
  50.5 5.0 %collective-permute-done.1.other_ref = bf16[4,128,128]{2,1,0:T(8,128)(2,1)S(1)} collective-permute-done((bf16[4,128,128]{2,1,0:T(8,128)(2,1)S(1)}, bf16[4,128,128]{2,1,0:T(8,128)(2,1)S(1)}, u32[]{:S(2)}, u32[]{:S(2)}) %collective-permute-start.1) | collective-permute-done | bytes 131104 | tf_op jit(solution)/shard_map/ppermute | solution.py:547
  55.5 0.6 shard_map.80
  56.1 0.4 shard_map.81
  56.5 0.6 all-to-all-done.3.tri_ref
  57.0 2.4 %shard_map.82 = bf16[8,128,128]{2,1,0:T(8,128)(2,1)} custom-call(bf16[32,2,8,128]{3,2,1,0:T(8,128)(2,1)S(1)} %all-to-all-done.3.tri_ref, bf16[8,128,128]{2,1,0:T(8,128)(2,1)S(1)} %get-tuple-element.37.z_ref, f32[1024,128]{1,0:T(8,128)S(1)} %get-tuple-element.39.gate_ref, bf16[128,1024]{1,0:T(8,128)(2,1)S(1)} %get-tuple-element.40.in_ref, ...), custom_call_target="tpu_custom_call" | custom-call | tf_op jit(solution)/shard_map/pallas_call | solution.py:558
Async XLA Ops:
  2.7 18.1 %all-to-all-start = ((bf16[32,5,8,128]{3,2,1,0:T(8,128)(2,1)}), bf16[32,5,8,128]{3,2,1,0:T(8,128)(2,1)S(1)}, u32[]{:S(2)}, u32[]{:S(2)}) async-start(bf16[32,5,8,128]{3,2,1,0:T(8,128)(2,1)} %shard_map.73.after_ref), calls=%async_computation | async-start | bytes 655360 | tf_op jit(solution)/shard_map/all_to_all | solution.py:471
  11.1 20.8 %collective-permute-start = (bf16[1984,128]{1,0:T(8,128)(2,1)S(1)}, bf16[1984,128]{1,0:T(8,128)(2,1)S(1)}, u32[]{:S(2)}, u32[]{:S(2)}) collective-permute-start(bf16[1984,128]{1,0:T(8,128)(2,1)S(1)} %get-tuple-element.26.own_ref), channel_id=1, source_target_pairs={{0,16},{16,0},{1,17},{17,1},{2,18},{18,2},{3,19},{19,3},{4,20},{20... | collective-permute-start | bytes 1523720 | tf_op jit(solution)/shard_map/ppermute | solution.py:510
  46.2 10.8 %all-to-all-start.3 = ((bf16[32,2,8,128]{3,2,1,0:T(8,128)(2,1)}), bf16[32,2,8,128]{3,2,1,0:T(8,128)(2,1)S(1)}, u32[]{:S(2)}, u32[]{:S(2)}) async-start(bf16[32,2,8,128]{3,2,1,0:T(8,128)(2,1)} %shard_map.79), calls=%async_computation.3 | async-start | bytes 262144 | tf_op jit(solution)/shard_map/all_to_all | solution.py:471
  48.8 6.7 %collective-permute-start.1 = (bf16[4,128,128]{2,1,0:T(8,128)(2,1)S(1)}, bf16[4,128,128]{2,1,0:T(8,128)(2,1)S(1)}, u32[]{:S(2)}, u32[]{:S(2)}) collective-permute-start(bf16[4,128,128]{2,1,0:T(8,128)(2,1)S(1)} %get-tuple-element.36), channel_id=1, source_target_pairs={{0,16},{16,0},{1,17},{17,1},{2,18},{18,2},{3,19},{19,3},{4,20},{20... | collective-permute-start | bytes 393224 | tf_op jit(solution)/shard_map/ppermute | solution.py:547

commit v6 on v5

--- a/solution.py
+++ b/solution.py
@@ -138,16 +138,31 @@
             copy.wait()
 
 
+def pack(sources, target_ref, sems, first):
+    copies, at = [], 0
+    for i, source in enumerate(sources):
+        part = target_ref.at[pl.ds(at, source.shape[0])]
+        copies.append(pltpu.make_async_copy(source, part, sems.at[first + i]))
+        copies[-1].start()
+        at += source.shape[0]
+    return copies
+
+
+def small_kernel(wp_ref, w_out_ref, after_ref, small_ref, sems):
+    width = small_ref.shape[1]
+    sources = [wp_ref.at[0, :, pl.ds(j * width, width)] for j in range(wp_ref.shape[2] // width)]
+    for copy in pack(sources + [w_out_ref.at[0]], small_ref, sems, 0):
+        copy.wait()
+
+
 def stage_kernel(
     order_ref,
     valid_ref,
     pair_ref,
-    wp_ref,
     w_in_ref,
     w_back_ref,
-    w_out_ref,
     after_ref,
-    pack_ref,
+    large_ref,
     z_ref,
     n_ref,
     owns_ref,
@@ -160,16 +175,7 @@
     rows, count, width = z_ref.shape
     trans = w_back_ref.shape[1]
     sources = [w_in_ref.at[0, :, pl.ds(j * width, width)] for j in range(2 * trans // width)]
-    sources += [w_back_ref.at[0], w_out_ref.at[0]]
-    sources += [wp_ref.at[0, :, pl.ds(j * width, width)] for j in range(wp_ref.shape[2] // width)]
-    packing, at = [], 0
-    for i, source in enumerate(sources):
-        size = source.shape[0]
-        packing.append(
-            pltpu.make_async_copy(source, pack_ref.at[pl.ds(at, size)], sems.at[3 + i])
-        )
-        packing[-1].start()
-        at += size
+    packing = pack(sources + [w_back_ref.at[0]], large_ref, sems, 3)
     scalars = read_scalars(order_ref, valid_ref, order_s, valid_s, sems)
     state = pltpu.make_async_copy(pair_ref, both_ref, sems.at[2])
     state.start()
@@ -283,25 +289,36 @@
     return pick
 
 
-def ready_kernel(block, inner, trans, n_ref, own_ref, other_ref, after_ref, gate_ref, in_ref, back_ref, w_out_ref, *more):
-    count = width = n_ref.shape[1]
-    rows = n_ref.shape[0] // count
+def gates_and_sides(block, inner, n_ref, own_ref, other_ref, gate_ref, w_out_ref, turned_ref=None):
+    width = n_ref.shape[1]
     pick = picker(block, own_ref, other_ref)
-    projections = 3 * trans + inner
-    weights = pick(projections + 2 * width, width)
-    for r in range(0, rows, 4):
-        here = slice(r * count, (r + 4) * count)
+    weights = pick(2 * width, width)
+    step = 512
+    for m in range(n_ref.shape[0] // step):
+        here = slice(m * step, (m + 1) * step)
         gate_ref[here, :] = jax.nn.sigmoid(
             jnp.dot(n_ref[here, :], weights, preferred_element_type=F32)
         )
-    for j in range(2 * trans // width):
+    w_out_ref[...] = pick(3 * width, inner)
+    if turned_ref is not None:
+        pick = picker(block + 1, own_ref, other_ref)
+        sides = [pick(j * width, width) for j in range(2)]
+        turned_ref[...] = tile_weights(jnp.concatenate(sides, -1), inner)
+
+
+def transition_weights(block, own_ref, other_ref, in_ref, back_ref):
+    width, hidden = in_ref.shape
+    pick = picker(block, own_ref, other_ref)
+    for j in range(hidden // width):
         in_ref[:, j * width : (j + 1) * width] = pick(j * width, width)
-    back_ref[...] = pick(2 * trans, trans)
-    w_out_ref[...] = pick(3 * trans, inner)
-    if more:
-        pick = picker(block + 1, own_ref, other_ref)
-        sides = [pick(projections + j * width, width) for j in range(2)]
-        more[0][...] = tile_weights(jnp.concatenate(sides, -1), inner)
+    back_ref[...] = pick(hidden, back_ref.shape[0])
+
+
+def ready_last_kernel(
+    inner, n_ref, own_ref, other_ref, large_ref, other_large_ref, gate_ref, w_out_ref, in_ref, back_ref
+):
+    gates_and_sides(1, inner, n_ref, own_ref, other_ref, gate_ref, w_out_ref)
+    transition_weights(1, large_ref, other_large_ref, in_ref, back_ref)
 
 
 def rows_norm(z_ref, n_ref):
@@ -318,10 +335,10 @@
     rows_norm(z_ref, n_ref)
 
 
-def out_project(t_ref, offsets, stride, z_ref, gate_ref, w_out, z1_ref, n_ref):
-    rows, count, _ = z_ref.shape
+def out_project(which, t_ref, offsets, stride, z_ref, gate_ref, w_out, z1_ref, n_ref):
+    _, count, _ = z_ref.shape
     inner = w_out.shape[0]
-    for r in range(rows):
+    for r in which:
         here = slice(r * count, (r + 1) * count)
         tri = t_ref[pl.ds(offsets[r], inner, stride=stride), :].astype(BF16)
         update = contract(tri, w_out, 0, 0)
@@ -330,9 +347,9 @@
         n_ref[here, :] = row_norm(first)
 
 
-def transition(in_ref, back_ref, n_ref, z1_ref, finish):
+def transition(which, in_ref, back_ref, n_ref, z1_ref, finish):
     trans, piece = back_ref.shape[0], 256
-    for m in range(n_ref.shape[0] // STEP):
+    for m in which:
         here = slice(m * STEP, (m + 1) * STEP)
         normed = n_ref[here, :]
         acts = []
@@ -366,10 +383,10 @@
     t_ref,
     z_ref,
     gate_ref,
-    in_ref,
-    back_ref,
     w_out_ref,
     turned_ref,
+    large_ref,
+    other_large_ref,
     masks_ref,
     owns_ref,
     lr_ref,
@@ -378,26 +395,44 @@
     n_ref,
     z1_ref,
     o_ref,
+    in_ref,
+    back_ref,
 ):
     rows, count, width = z_ref.shape
     half = rows // 2
+    transition_weights(0, large_ref, other_large_ref, in_ref, back_ref)
     offsets = [q * 4 * inner + r for q in range(2) for r in range(half)]
-    out_project(t_ref, offsets, 4, z_ref, gate_ref, w_out_ref[...], z1_ref, n_ref)
+    project = functools.partial(
+        out_project,
+        t_ref=t_ref,
+        offsets=offsets,
+        stride=4,
+        z_ref=z_ref,
+        gate_ref=gate_ref,
+        w_out=w_out_ref[...],
+        z1_ref=z1_ref,
+        n_ref=n_ref,
+    )
 
     def finish(m, done):
         o_ref[m * STEP : (m + 1) * STEP, :] = done
 
-    transition(in_ref, back_ref, n_ref, z1_ref, finish)
+    turned = turned_ref[...]
+
+    def tail_full():
+        normed = [row_norm(o_ref[r * count : (r + 1) * count, :]) for r in range(half)]
+        put_tiles(
+            turned, [normed[:2], normed[2:]], [masks_ref[0], masks_ref[1]], lr_ref, 0, inner
+        )
+
+    project(range(rows))
+    transition((0, 1), in_ref, back_ref, n_ref, z1_ref, finish)
+    tail_full()
     owns = (owns_ref[:1, :] > 0.5)[None]
     full = o_ref[: half * count, :].reshape(half, count, width)
     short = o_ref[half * count :, :].reshape(half, count, width)
     keep_ref[...] = jnp.where(owns, full.astype(F32), short.astype(F32)).astype(BF16)
     send_ref[...] = jnp.where(owns, short.astype(F32), full.astype(F32)).astype(BF16)
-    turned = turned_ref[...]
-    normed = [row_norm(o_ref[r * count : (r + 1) * count, :]) for r in range(half)]
-    put_tiles(
-        turned, [normed[:2], normed[2:]], [masks_ref[0], masks_ref[1]], lr_ref, 0, inner
-    )
     four = row_norm(
         jnp.concatenate(
             [o_ref[r * count : r * count + SHORT, :] for r in range(half, rows)], 0
@@ -411,9 +446,9 @@
     tri_ref,
     z_ref,
     gate_ref,
+    w_out_ref,
     in_ref,
     back_ref,
-    w_out_ref,
     out_ref,
     t_ref,
     n_ref,
@@ -433,8 +468,9 @@
     t_ref[...] = layer_norm(tri_ref[...].reshape(inner, rows, count).astype(F32), 0).reshape(
         inner * rows, count
     )
-    out_project(t_ref, range(rows), rows, z_ref, gate_ref, w_out_ref[...], z1_ref, n_ref)
-    transition(in_ref, back_ref, n_ref, z1_ref, finish)
+    args = (t_ref, range(rows), rows, z_ref, gate_ref, w_out_ref[...], z1_ref, n_ref)
+    out_project(range(rows), *args)
+    transition((0, 1), in_ref, back_ref, n_ref, z1_ref, finish)
     for copy in copies:
         copy.wait()
 
@@ -444,7 +480,6 @@
     devices = lax.axis_size("section") * lax.axis_size("row")
     inner, trans = w_out.shape[1], w_back.shape[1]
     swap = [(0, 1), (1, 0)]
-    packed = 3 * trans + inner + w_proj.shape[2]
 
     vmem = pl.BlockSpec(memory_space=pltpu.VMEM)
     hbm = pl.BlockSpec(memory_space=pltpu.HBM)
@@ -454,7 +489,9 @@
     gates = shape((rows * count, width), F32)
     sems = pltpu.SemaphoreType.DMA
 
-    def call(kernel, out_shape, n_in, scratch=(), out_specs=None, in_spec=vmem, cost=None):
+    def call(
+        kernel, out_shape, n_in, scratch=(), out_specs=None, in_spec=vmem, cost=None, params=LIMIT
+    ):
         many = isinstance(out_shape, tuple)
         specs = out_specs or ((vmem,) * len(out_shape) if many else vmem)
         return pl.pallas_call(
@@ -463,7 +500,7 @@
             in_specs=[in_spec] * n_in if isinstance(n_in, int) else n_in,
             out_specs=specs,
             scratch_shapes=list(scratch),
-            compiler_params=LIMIT,
+            compiler_params=params,
             cost_estimate=cost,
         )
 
@@ -492,28 +529,36 @@
         in_spec=hbm,
     )(*inputs[:4])
     light = pl.CostEstimate(flops=34 * 10**6, bytes_accessed=10**6, transcendentals=2 * 10**5)
-    own, z, normed, owns, masks = call(
+    small = call(
+        small_kernel,
+        shape((w_proj.shape[2] + inner, width), BF16),
+        [hbm] * 2 + [anywhere],
+        [sems((1 + w_proj.shape[2] // width,))],
+        cost=light,
+    )(inputs[3], inputs[6], lr)
+    large, z, normed, owns, masks = call(
         stage_kernel,
         (
-            shape((packed, width), BF16),
+            shape((3 * trans, width), BF16),
             shape((rows, count, width), BF16),
             tokens,
             shape((8, count), F32),
             shape((3, 8, count), F32),
         ),
-        [hbm] * 7 + [anywhere],
-        scalars + [sems((5 + (2 * trans + w_proj.shape[2]) // width,))],
+        [hbm] * 5 + [anywhere],
+        scalars + [sems((4 + 2 * trans // width,))],
         cost=light,
-    )(*inputs, lr)
+    )(*inputs[:3], *inputs[4:6], small)
 
     sides = exchange(lr)
-    other = lax.ppermute(own, "section", swap)
-    readied = (
-        gates,
-        shape(w_in.shape[1:], BF16),
-        shape(w_back.shape[1:], BF16),
-        shape(w_out.shape[1:], BF16),
-    )
+    other_small = lax.ppermute(small, "section", swap)
+    other_large = lax.ppermute(large, "section", swap)
+    gate, w_out_first, turned = call(
+        functools.partial(gates_and_sides, 0, inner),
+        (gates, shape(w_out.shape[1:], BF16), shape((8 * inner, 2 * width), BF16)),
+        3,
+        cost=light,
+    )(normed, small, other_small)
     tri_scratch = [
         pltpu.VMEM((4 * count, count), F32),
         pltpu.VMEM((32, count), F32),
@@ -525,30 +570,29 @@
             shape((devices, 2, 8, count), BF16),
             [vmem, anywhere],
             tri_scratch,
-        )(sides, normed),
+        )(sides, gate),
     )
     t = call(functools.partial(norm_kernel, inner), shape((8 * inner, count), F32), 1)(tri)
-    *ready, turned = call(
-        functools.partial(ready_kernel, 0, inner, trans),
-        readied + (shape((8 * inner, 2 * width), BF16),),
-        [vmem, vmem, vmem, anywhere],
-        cost=light,
-    )(normed, own, other, t)
     work = [pltpu.VMEM((8 * inner, count), F32), flat, flat]
     halves = shape((rows // 2, count, width), BF16)
     lr, keep, send = call(
         functools.partial(update_kernel, inner),
         (shape((devices, 3, 8, count), BF16), halves, halves),
         9,
-        [flat] * 3,
-    )(t, z, *ready, turned, masks, owns)
+        [flat] * 3 + [pltpu.VMEM(w_in.shape[1:], BF16), pltpu.VMEM(w_back.shape[1:], BF16)],
+    )(t, z, gate, w_out_first, turned, large, other_large, masks, owns)
 
     sides = exchange(lr)
     came = lax.ppermute(send, "section", swap)
     z, normed = call(join_kernel, (shape((rows, count, width), BF16), tokens), 2)(keep, came)
     ready = call(
-        functools.partial(ready_kernel, 1, inner, trans), readied, [vmem, vmem, vmem, anywhere], cost=light
-    )(normed, own, other, normed)
+        functools.partial(ready_last_kernel, inner),
+        tuple(shape(x, BF16 if i else F32) for i, x in enumerate(
+            ((rows * count, width), w_out.shape[1:], w_in.shape[1:], w_back.shape[1:])
+        )),
+        5,
+        cost=light,
+    )(normed, small, other_small, large, other_large)
     tri_scratch[1] = pltpu.VMEM((64, count), F32)
     tri = exchange(
         call(

time: 59.7 us -> 68.4 us (1.15)
  waiting for transfers between devices: 13.4 us -> 19.3 us
  blocking collectives: 21.1 us -> 23 us
    ppermute x1 -> x2, waiting for transfers between devices: 0.01 us -> 13.7 us  [the longest x1 13.7 us: fast_body(): other_small = lax.ppermute(small, 'section', swap)]
    all_to_all x2, waiting for transfers between devices: 8.37 us -> 0.56 us  [exchange(): lax.all_to_all(value, ('section', 'row'), split_axis=0, concat_axis=0, ti...]
    all_to_all x2, blocking collectives: 21.1 us -> 23 us  [exchange(): lax.all_to_all(value, ('section', 'row'), split_axis=0, concat_axis=0, ti...]
    pallas_call x3 -> x4, Pallas kernels: 2.77 us -> 3.4 us  [the longest x1 1.93 us: fast_body(): call(stage_kernel, (shape((3 * trans, width), BF16), shape((rows, count,...]
    ppermute x1 -> x2, starting transfers between devices: 1.83 us -> 2.09 us  [the longest x1 1.83 us: fast_body(): other_large = lax.ppermute(large, 'section', swap)]
  transfers between devices with their start and end apart: 4 -> 5, of which waited for: 3 -> 3; matrix products, arithmetic and copies ran while one was open for 0% -> 0% of each run, Pallas kernels for 6% -> 7%
where the time goes in v6:
time: 68.4 us; the launch traced here: 68 us
  blocking collectives  23 us (34%)
  waiting for transfers between devices  19.3 us (28%)
  Pallas kernels  12.9 us (19%)
  starting transfers between devices  12.8 us (19%)
    all_to_all x2, blocking collectives, exchange(): lax.all_to_all(value, ('section', 'row'), split_axis=0, concat_axis=0, ti...  23 us
    ppermute x1, waiting for transfers between devices, fast_body(): other_small = lax.ppermute(small, 'section', swap)  13.7 us
    all_to_all x2, starting transfers between devices, exchange(): lax.all_to_all(value, ('section', 'row'), split_axis=0, concat_axis=0, ti...  8.95 us
    ppermute x1, waiting for transfers between devices, fast_body(): came = lax.ppermute(send, 'section', swap)  5.01 us
    pallas_call x1, Pallas kernels, fast_body(): call(functools.partial(first_kernel, inner), shape(lr_shape, BF16), 4, [p...  2.68 us
    pallas_call x1, Pallas kernels, fast_body(): call(functools.partial(last_kernel, inner), shape((rows, count, width), B...  2.37 us
    pallas_call x1, Pallas kernels, fast_body(): call(functools.partial(update_kernel, inner), (shape((devices, 3, 8, coun...  2.02 us
    pallas_call x1, Pallas kernels, fast_body(): call(stage_kernel, (shape((3 * trans, width), BF16), shape((rows, count,...  1.93 us
  transfers between devices with their start and end apart: 5, of which 3 were waited for; matrix products, arithmetic and copies ran while one was open for 0% of the time, Pallas kernels for 7%

profile of v6, /device:TPU:0, one launch (start us, length us, event | category | flops | bytes accessed | tf_op | source)
XLA Modules:
  0.0 68.0 jit_solution(1794904580921510011)
XLA Ops:
  0.0 2.7 %shard_map.73.after_ref = bf16[32,5,8,128]{3,2,1,0:T(8,128)(2,1)} custom-call(s32[2]{0:T(128)} %order_ref.3, s32[2]{0:T(128)} %valid_ref.3, bf16[2,8,128,128]{3,2,1,0:T(8,128)(2,1)} %pair_ref.3, bf16[1,128,384]{2,1,0:T(8,128)(2,1)} %wp_ref.3), custom_call_target="tpu_custom_call" | custom-call | tf_op jit(solution)/shard_map/pallas_call | solution.py:521
  2.7 6.4 %all-to-all-start = ((bf16[32,5,8,128]{3,2,1,0:T(8,128)(2,1)}), bf16[32,5,8,128]{3,2,1,0:T(8,128)(2,1)S(1)}, u32[]{:S(2)}, u32[]{:S(2)}) async-start(bf16[32,5,8,128]{3,2,1,0:T(8,128)(2,1)} %shard_map.73.after_ref), calls=%async_computation | async-start | bytes 655360 | tf_op jit(solution)/shard_map/all_to_all | solution.py:508
  9.1 0.8 %shard_map.74.after_ref.own_ref = bf16[448,128]{1,0:T(8,128)(2,1)S(1)} custom-call(bf16[1,128,384]{2,1,0:T(8,128)(2,1)} %wp_ref.3, bf16[1,64,128]{2,1,0:T(8,128)(2,1)} %w_out_ref.1, bf16[32,5,8,128]{3,2,1,0:T(8,128)(2,1)} %shard_map.73.after_ref), custom_call_target="tpu_custom_call" | custom-call | flops 34000000 | bytes 1000000 | tf_op jit(solution)/shard_map/pallas_call | solution.py:532
  9.9 1.9 %shard_map.75 = (bf16[1536,128]{1,0:T(8,128)(2,1)S(1)}, bf16[8,128,128]{2,1,0:T(8,128)(2,1)S(1)}, bf16[1024,128]{1,0:T(8,128)(2,1)S(1)}, f32[8,128]{1,0:T(8,128)S(1)}, f32[3,8,128]{2,1,0:T(8,128)S(1)}) custom-call(s32[2]{0:T(128)} %order_ref.3, s32[2]{0:T(128)} %valid_ref.3, bf16[2,8,128,128]{3,2,1,0:T(8,128)(2,1)} %pair_ref.3, ...), custom_call_target="tpu_custom_call" | custom-call | flops 34000000 | bytes 1000000 | tf_op jit(solution)/shard_map/pallas_call | solution.py:539
  11.9 1.8 %collective-permute-start.1 = (bf16[1536,128]{1,0:T(8,128)(2,1)S(1)}, bf16[1536,128]{1,0:T(8,128)(2,1)S(1)}, u32[]{:S(2)}, u32[]{:S(2)}) collective-permute-start(bf16[1536,128]{1,0:T(8,128)(2,1)S(1)} %get-tuple-element.27.large_ref), channel_id=1, source_target_pairs={{0,16},{16,0},{1,17},{17,1},{2,18},{18,2},{3,19},{19,3},{4,20},{20... | collective-permute-start | bytes 1179656 | tf_op jit(solution)/shard_map/ppermute | solution.py:555
  13.7 0.3 collective-permute-start
  13.9 13.7 %collective-permute-done.other_ref = bf16[448,128]{1,0:T(8,128)(2,1)S(1)} collective-permute-done((bf16[448,128]{1,0:T(8,128)(2,1)S(1)}, bf16[448,128]{1,0:T(8,128)(2,1)S(1)}, u32[]{:S(2)}, u32[]{:S(2)}) %collective-permute-start) | collective-permute-done | bytes 114720 | tf_op jit(solution)/shard_map/ppermute | solution.py:554
  27.6 0.3 shard_map.76
  27.9 0.0 all-to-all-done.in_ref
  27.9 0.6 shard_map.77
  28.5 12.3 %all_to_all.20.tri_ref = bf16[32,2,8,128]{3,2,1,0:T(8,128)(2,1)S(1)} all-to-all(bf16[32,2,8,128]{3,2,1,0:T(8,128)(2,1)S(1)} %shard_map.77), channel_id=1, replica_groups=mesh['section'=2,'row'=16] {'section','row'}, dimensions={0} | all-to-all | bytes 262144 | tf_op jit(solution)/shard_map/all_to_all | solution.py:508
  40.8 0.1 shard_map.78.t_ref
  40.9 0.0 collective-permute-done.1.other_large_ref
  40.9 2.0 %shard_map.79 = (bf16[32,3,8,128]{3,2,1,0:T(8,128)(2,1)S(1)}, bf16[4,128,128]{2,1,0:T(8,128)(2,1)S(1)}, bf16[4,128,128]{2,1,0:T(8,128)(2,1)S(1)}) custom-call(f32[512,128]{1,0:T(8,128)S(1)} %shard_map.78.t_ref, bf16[8,128,128]{2,1,0:T(8,128)(2,1)S(1)} %get-tuple-element.24.z_ref, f32[1024,128]{1,0:T(8,128)S(1)} %get-tuple-element.23.after_ref.gate_ref, ...), custom_call_target="tpu_custom_call" | custom-call | tf_op jit(solution)/shard_map/pallas_call | solution.py:578
  43.0 10.7 %all_to_all.21.in_ref = bf16[32,3,8,128]{3,2,1,0:T(8,128)(2,1)S(1)} all-to-all(bf16[32,3,8,128]{3,2,1,0:T(8,128)(2,1)S(1)} %get-tuple-element.30), channel_id=1, replica_groups=mesh['section'=2,'row'=16] {'section','row'}, dimensions={0} | all-to-all | bytes 393216 | tf_op jit(solution)/shard_map/all_to_all | solution.py:508
  53.6 1.2 %shard_map.80 = bf16[32,2,8,128]{3,2,1,0:T(8,128)(2,1)} custom-call(bf16[32,3,8,128]{3,2,1,0:T(8,128)(2,1)S(1)} %all_to_all.21.in_ref, f32[8,128]{1,0:T(8,128)S(1)} %get-tuple-element.29.owns_ref), custom_call_target="tpu_custom_call" | custom-call | tf_op jit(solution)/shard_map/pallas_call | solution.py:598
  54.8 2.6 %all-to-all-start.3 = ((bf16[32,2,8,128]{3,2,1,0:T(8,128)(2,1)}), bf16[32,2,8,128]{3,2,1,0:T(8,128)(2,1)S(1)}, u32[]{:S(2)}, u32[]{:S(2)}) async-start(bf16[32,2,8,128]{3,2,1,0:T(8,128)(2,1)} %shard_map.80), calls=%async_computation.3 | async-start | bytes 262144 | tf_op jit(solution)/shard_map/all_to_all | solution.py:508
  57.4 1.7 %collective-permute-start.2 = (bf16[4,128,128]{2,1,0:T(8,128)(2,1)S(1)}, bf16[4,128,128]{2,1,0:T(8,128)(2,1)S(1)}, u32[]{:S(2)}, u32[]{:S(2)}) collective-permute-start(bf16[4,128,128]{2,1,0:T(8,128)(2,1)S(1)} %get-tuple-element.32), channel_id=1, source_target_pairs={{0,16},{16,0},{1,17},{17,1},{2,18},{18,2},{3,19},{19,3},{4,20},{20... | collective-permute-start | bytes 393224 | tf_op jit(solution)/shard_map/ppermute | solution.py:586
  59.1 5.0 %collective-permute-done.2.other_ref = bf16[4,128,128]{2,1,0:T(8,128)(2,1)S(1)} collective-permute-done((bf16[4,128,128]{2,1,0:T(8,128)(2,1)S(1)}, bf16[4,128,128]{2,1,0:T(8,128)(2,1)S(1)}, u32[]{:S(2)}, u32[]{:S(2)}) %collective-permute-start.2) | collective-permute-done | bytes 131104 | tf_op jit(solution)/shard_map/ppermute | solution.py:586
  64.1 0.6 shard_map.81
  64.7 0.3 shard_map.82
  65.1 0.6 all-to-all-done.3.tri_ref
  65.6 2.4 %shard_map.83 = bf16[8,128,128]{2,1,0:T(8,128)(2,1)} custom-call(bf16[32,2,8,128]{3,2,1,0:T(8,128)(2,1)S(1)} %all-to-all-done.3.tri_ref, bf16[8,128,128]{2,1,0:T(8,128)(2,1)S(1)} %get-tuple-element.33.z_ref, f32[1024,128]{1,0:T(8,128)S(1)} %get-tuple-element.35.gate_ref, bf16[64,128]{1,0:T(8,128)(2,1)S(1)} %get-tuple-element.36.w_out_ref, ...), custom_call_target="tpu_custom_call" | custom-call | tf_op jit(solution)/shard_map/pallas_call | solution.py:602
Async XLA Ops:
  2.7 25.2 %all-to-all-start = ((bf16[32,5,8,128]{3,2,1,0:T(8,128)(2,1)}), bf16[32,5,8,128]{3,2,1,0:T(8,128)(2,1)S(1)}, u32[]{:S(2)}, u32[]{:S(2)}) async-start(bf16[32,5,8,128]{3,2,1,0:T(8,128)(2,1)} %shard_map.73.after_ref), calls=%async_computation | async-start | bytes 655360 | tf_op jit(solution)/shard_map/all_to_all | solution.py:508
  11.9 29.1 %collective-permute-start.1 = (bf16[1536,128]{1,0:T(8,128)(2,1)S(1)}, bf16[1536,128]{1,0:T(8,128)(2,1)S(1)}, u32[]{:S(2)}, u32[]{:S(2)}) collective-permute-start(bf16[1536,128]{1,0:T(8,128)(2,1)S(1)} %get-tuple-element.27.large_ref), channel_id=1, source_target_pairs={{0,16},{16,0},{1,17},{17,1},{2,18},{18,2},{3,19},{19,3},{4,20},{20... | collective-permute-start | bytes 1179656 | tf_op jit(solution)/shard_map/ppermute | solution.py:555
  13.7 13.9 %collective-permute-start = (bf16[448,128]{1,0:T(8,128)(2,1)S(1)}, bf16[448,128]{1,0:T(8,128)(2,1)S(1)}, u32[]{:S(2)}, u32[]{:S(2)}) collective-permute-start(bf16[448,128]{1,0:T(8,128)(2,1)S(1)} %shard_map.74.after_ref.own_ref), channel_id=1, source_target_pairs={{0,16},{16,0},{1,17},{17,1},{2,18},{18,2},{3,19},{19,3},{4,20},{20... | collective-permute-start | bytes 344072 | tf_op jit(solution)/shard_map/ppermute | solution.py:554
  54.8 10.8 %all-to-all-start.3 = ((bf16[32,2,8,128]{3,2,1,0:T(8,128)(2,1)}), bf16[32,2,8,128]{3,2,1,0:T(8,128)(2,1)S(1)}, u32[]{:S(2)}, u32[]{:S(2)}) async-start(bf16[32,2,8,128]{3,2,1,0:T(8,128)(2,1)} %shard_map.80), calls=%async_computation.3 | async-start | bytes 262144 | tf_op jit(solution)/shard_map/all_to_all | solution.py:508
  57.4 6.7 %collective-permute-start.2 = (bf16[4,128,128]{2,1,0:T(8,128)(2,1)S(1)}, bf16[4,128,128]{2,1,0:T(8,128)(2,1)S(1)}, u32[]{:S(2)}, u32[]{:S(2)}) collective-permute-start(bf16[4,128,128]{2,1,0:T(8,128)(2,1)S(1)} %get-tuple-element.32), channel_id=1, source_target_pairs={{0,16},{16,0},{1,17},{17,1},{2,18},{18,2},{3,19},{19,3},{4,20},{20... | collective-permute-start | bytes 393224 | tf_op jit(solution)/shard_map/ppermute | solution.py:586

commit v7 on v6

--- a/solution.py
+++ b/solution.py
@@ -107,14 +107,14 @@
         state = pltpu.make_async_copy(pair_ref, both_ref, sems.at[3])
         state.start()
         scalars = read_scalars(order_ref, valid_ref, order_s, valid_s, sems)
-        weights.wait()
-        turned = tile_weights(w_ref[:, : 4 * inner], inner)
         for copy in scalars:
             copy.wait()
         full = jnp.where(valid_s[1] > valid_s[0], 1, 0)
         short = 1 - full
         start = lax.axis_index("row") * rows
+        weights.wait()
         state.wait()
+        turned = tile_weights(w_ref[:, : 4 * inner], inner)
         for t in range(0, rows // 2, 2):
             normed = [row_norm(both_ref[full, 2 * t + r]) for r in range(4)]
             put_tiles(
@@ -202,19 +202,20 @@
     count = left.shape[1]
     block = lax.div(lax.broadcasted_iota(jnp.int32, left.shape, 1), SHORT)
     lefts = jnp.concatenate([jnp.where(block == q, left, 0.0) for q in range(4)], 0)
-    rights = jnp.concatenate(
-        [right if q == 0 else pltpu.roll(right, SHORT * q, 1) for q in range(4)], 0
-    )
-    product = contract(lefts.astype(BF16), rights.astype(BF16), 1, 1).astype(BF16)
-    source = lax.broadcasted_iota(jnp.int32, (32, count), 0)
-    target = lax.broadcasted_iota(jnp.int32, (32, count), 1)
-    moved, token = lax.div(source, 8), lax.rem(source, 8)
+    turned = [right if q == 0 else pltpu.roll(right, SHORT * q, 1) for q in range(4)]
+    rights = jnp.concatenate(turned * 4, 0)
+    product = contract(lefts.astype(BF16), rights.astype(BF16), 1, 1)
+    row = lax.div(lax.broadcasted_iota(jnp.int32, product.shape, 0), 8)
+    group = lax.div(lax.broadcasted_iota(jnp.int32, product.shape, 1), SHORT)
+    product = jnp.where(row == group, product, 0.0).astype(BF16)
+    source = lax.broadcasted_iota(jnp.int32, (count, count), 0)
+    target = lax.broadcasted_iota(jnp.int32, (count, count), 1)
+    moved, token = lax.rem(lax.div(source, 8), 4), lax.rem(source, 8)
+    lane = 4 * token + lax.rem(lax.div(source, SHORT) - moved + 4, 4)
+    pick = jnp.where(target == lane, 1.0, 0.0).astype(BF16)
+    placed = jnp.dot(product, pick, preferred_element_type=F32)
     for q in range(4):
-        lane = 4 * token + lax.rem(q - moved + 4, 4)
-        pick = jnp.where(target == lane, 1.0, 0.0).astype(BF16)
-        place_ref[pl.ds(q, 8, stride=4), :] = jnp.dot(
-            product[8 * q : 8 * q + 8], pick, preferred_element_type=F32
-        )
+        place_ref[pl.ds(q, 8, stride=4), :] = placed[8 * q : 8 * q + 8]
 
 
 def triangles(wide_ref, few_ref, few_stride, place_ref, count):

time: 68.4 us -> 68.3 us (level)
  no operation moved by 1% of the time
where the time goes in v7:
time: 68.3 us; the launch traced here: 67.9 us
  blocking collectives  23 us (34%)
  waiting for transfers between devices  19.2 us (28%)
  Pallas kernels  12.8 us (19%)
  starting transfers between devices  12.8 us (19%)
    all_to_all x2, blocking collectives, exchange(): lax.all_to_all(value, ('section', 'row'), split_axis=0, concat_axis=0, ti...  23 us
    ppermute x1, waiting for transfers between devices, fast_body(): other_small = lax.ppermute(small, 'section', swap)  13.7 us
    all_to_all x2, starting transfers between devices, exchange(): lax.all_to_all(value, ('section', 'row'), split_axis=0, concat_axis=0, ti...  8.95 us
    ppermute x1, waiting for transfers between devices, fast_body(): came = lax.ppermute(send, 'section', swap)  5 us
    pallas_call x1, Pallas kernels, fast_body(): call(functools.partial(first_kernel, inner), shape(lr_shape, BF16), 4, [p...  2.68 us
    pallas_call x1, Pallas kernels, fast_body(): call(functools.partial(last_kernel, inner), shape((rows, count, width), B...  2.37 us
    pallas_call x1, Pallas kernels, fast_body(): call(functools.partial(update_kernel, inner), (shape((devices, 3, 8, coun...  2.01 us
    pallas_call x1, Pallas kernels, fast_body(): call(stage_kernel, (shape((3 * trans, width), BF16), shape((rows, count,...  1.93 us
  transfers between devices with their start and end apart: 5, of which 3 were waited for; matrix products, arithmetic and copies ran while one was open for 0% of the time, Pallas kernels for 7%

profile of v7, /device:TPU:0, one launch (start us, length us, event | category | flops | bytes accessed | tf_op | source)
XLA Modules:
  0.0 67.9 jit_solution(14218819175391652723)
XLA Ops:
  0.0 2.7 %shard_map.73.after_ref = bf16[32,5,8,128]{3,2,1,0:T(8,128)(2,1)} custom-call(s32[2]{0:T(128)} %order_ref.3, s32[2]{0:T(128)} %valid_ref.3, bf16[2,8,128,128]{3,2,1,0:T(8,128)(2,1)} %pair_ref.3, bf16[1,128,384]{2,1,0:T(8,128)(2,1)} %wp_ref.3), custom_call_target="tpu_custom_call" | custom-call | tf_op jit(solution)/shard_map/pallas_call | solution.py:522
  2.7 6.4 %all-to-all-start = ((bf16[32,5,8,128]{3,2,1,0:T(8,128)(2,1)}), bf16[32,5,8,128]{3,2,1,0:T(8,128)(2,1)S(1)}, u32[]{:S(2)}, u32[]{:S(2)}) async-start(bf16[32,5,8,128]{3,2,1,0:T(8,128)(2,1)} %shard_map.73.after_ref), calls=%async_computation | async-start | bytes 655360 | tf_op jit(solution)/shard_map/all_to_all | solution.py:509
  9.1 0.8 %shard_map.74.after_ref.own_ref = bf16[448,128]{1,0:T(8,128)(2,1)S(1)} custom-call(bf16[1,128,384]{2,1,0:T(8,128)(2,1)} %wp_ref.3, bf16[1,64,128]{2,1,0:T(8,128)(2,1)} %w_out_ref.1, bf16[32,5,8,128]{3,2,1,0:T(8,128)(2,1)} %shard_map.73.after_ref), custom_call_target="tpu_custom_call" | custom-call | flops 34000000 | bytes 1000000 | tf_op jit(solution)/shard_map/pallas_call | solution.py:533
  9.9 1.9 %shard_map.75 = (bf16[1536,128]{1,0:T(8,128)(2,1)S(1)}, bf16[8,128,128]{2,1,0:T(8,128)(2,1)S(1)}, bf16[1024,128]{1,0:T(8,128)(2,1)S(1)}, f32[8,128]{1,0:T(8,128)S(1)}, f32[3,8,128]{2,1,0:T(8,128)S(1)}) custom-call(s32[2]{0:T(128)} %order_ref.3, s32[2]{0:T(128)} %valid_ref.3, bf16[2,8,128,128]{3,2,1,0:T(8,128)(2,1)} %pair_ref.3, ...), custom_call_target="tpu_custom_call" | custom-call | flops 34000000 | bytes 1000000 | tf_op jit(solution)/shard_map/pallas_call | solution.py:540
  11.8 1.8 %collective-permute-start.1 = (bf16[1536,128]{1,0:T(8,128)(2,1)S(1)}, bf16[1536,128]{1,0:T(8,128)(2,1)S(1)}, u32[]{:S(2)}, u32[]{:S(2)}) collective-permute-start(bf16[1536,128]{1,0:T(8,128)(2,1)S(1)} %get-tuple-element.27.large_ref), channel_id=1, source_target_pairs={{0,16},{16,0},{1,17},{17,1},{2,18},{18,2},{3,19},{19,3},{4,20},{20... | collective-permute-start | bytes 1179656 | tf_op jit(solution)/shard_map/ppermute | solution.py:556
  13.7 0.3 collective-permute-start
  13.9 13.7 %collective-permute-done.other_ref = bf16[448,128]{1,0:T(8,128)(2,1)S(1)} collective-permute-done((bf16[448,128]{1,0:T(8,128)(2,1)S(1)}, bf16[448,128]{1,0:T(8,128)(2,1)S(1)}, u32[]{:S(2)}, u32[]{:S(2)}) %collective-permute-start) | collective-permute-done | bytes 114720 | tf_op jit(solution)/shard_map/ppermute | solution.py:555
  27.6 0.3 shard_map.76
  27.9 0.0 all-to-all-done.in_ref
  27.9 0.5 shard_map.77
  28.4 12.3 %all_to_all.20.tri_ref = bf16[32,2,8,128]{3,2,1,0:T(8,128)(2,1)S(1)} all-to-all(bf16[32,2,8,128]{3,2,1,0:T(8,128)(2,1)S(1)} %shard_map.77), channel_id=1, replica_groups=mesh['section'=2,'row'=16] {'section','row'}, dimensions={0} | all-to-all | bytes 262144 | tf_op jit(solution)/shard_map/all_to_all | solution.py:509
  40.7 0.1 shard_map.78.t_ref
  40.8 0.0 collective-permute-done.1.other_large_ref
  40.9 2.0 %shard_map.79 = (bf16[32,3,8,128]{3,2,1,0:T(8,128)(2,1)S(1)}, bf16[4,128,128]{2,1,0:T(8,128)(2,1)S(1)}, bf16[4,128,128]{2,1,0:T(8,128)(2,1)S(1)}) custom-call(f32[512,128]{1,0:T(8,128)S(1)} %shard_map.78.t_ref, bf16[8,128,128]{2,1,0:T(8,128)(2,1)S(1)} %get-tuple-element.24.z_ref, f32[1024,128]{1,0:T(8,128)S(1)} %get-tuple-element.23.after_ref.gate_ref, ...), custom_call_target="tpu_custom_call" | custom-call | tf_op jit(solution)/shard_map/pallas_call | solution.py:579
  42.9 10.7 %all_to_all.21.in_ref = bf16[32,3,8,128]{3,2,1,0:T(8,128)(2,1)S(1)} all-to-all(bf16[32,3,8,128]{3,2,1,0:T(8,128)(2,1)S(1)} %get-tuple-element.30), channel_id=1, replica_groups=mesh['section'=2,'row'=16] {'section','row'}, dimensions={0} | all-to-all | bytes 393216 | tf_op jit(solution)/shard_map/all_to_all | solution.py:509
  53.5 1.2 %shard_map.80 = bf16[32,2,8,128]{3,2,1,0:T(8,128)(2,1)} custom-call(bf16[32,3,8,128]{3,2,1,0:T(8,128)(2,1)S(1)} %all_to_all.21.in_ref, f32[8,128]{1,0:T(8,128)S(1)} %get-tuple-element.29.owns_ref), custom_call_target="tpu_custom_call" | custom-call | tf_op jit(solution)/shard_map/pallas_call | solution.py:599
  54.7 2.6 %all-to-all-start.3 = ((bf16[32,2,8,128]{3,2,1,0:T(8,128)(2,1)}), bf16[32,2,8,128]{3,2,1,0:T(8,128)(2,1)S(1)}, u32[]{:S(2)}, u32[]{:S(2)}) async-start(bf16[32,2,8,128]{3,2,1,0:T(8,128)(2,1)} %shard_map.80), calls=%async_computation.3 | async-start | bytes 262144 | tf_op jit(solution)/shard_map/all_to_all | solution.py:509
  57.3 1.7 %collective-permute-start.2 = (bf16[4,128,128]{2,1,0:T(8,128)(2,1)S(1)}, bf16[4,128,128]{2,1,0:T(8,128)(2,1)S(1)}, u32[]{:S(2)}, u32[]{:S(2)}) collective-permute-start(bf16[4,128,128]{2,1,0:T(8,128)(2,1)S(1)} %get-tuple-element.32), channel_id=1, source_target_pairs={{0,16},{16,0},{1,17},{17,1},{2,18},{18,2},{3,19},{19,3},{4,20},{20... | collective-permute-start | bytes 393224 | tf_op jit(solution)/shard_map/ppermute | solution.py:587
  59.0 5.0 %collective-permute-done.2.other_ref = bf16[4,128,128]{2,1,0:T(8,128)(2,1)S(1)} collective-permute-done((bf16[4,128,128]{2,1,0:T(8,128)(2,1)S(1)}, bf16[4,128,128]{2,1,0:T(8,128)(2,1)S(1)}, u32[]{:S(2)}, u32[]{:S(2)}) %collective-permute-start.2) | collective-permute-done | bytes 131104 | tf_op jit(solution)/shard_map/ppermute | solution.py:587
  64.0 0.6 shard_map.81
  64.6 0.4 shard_map.82
  64.9 0.6 all-to-all-done.3.tri_ref
  65.5 2.4 %shard_map.83 = bf16[8,128,128]{2,1,0:T(8,128)(2,1)} custom-call(bf16[32,2,8,128]{3,2,1,0:T(8,128)(2,1)S(1)} %all-to-all-done.3.tri_ref, bf16[8,128,128]{2,1,0:T(8,128)(2,1)S(1)} %get-tuple-element.33.z_ref, f32[1024,128]{1,0:T(8,128)S(1)} %get-tuple-element.35.gate_ref, bf16[64,128]{1,0:T(8,128)(2,1)S(1)} %get-tuple-element.36.w_out_ref, ...), custom_call_target="tpu_custom_call" | custom-call | tf_op jit(solution)/shard_map/pallas_call | solution.py:603
Async XLA Ops:
  2.7 25.2 %all-to-all-start = ((bf16[32,5,8,128]{3,2,1,0:T(8,128)(2,1)}), bf16[32,5,8,128]{3,2,1,0:T(8,128)(2,1)S(1)}, u32[]{:S(2)}, u32[]{:S(2)}) async-start(bf16[32,5,8,128]{3,2,1,0:T(8,128)(2,1)} %shard_map.73.after_ref), calls=%async_computation | async-start | bytes 655360 | tf_op jit(solution)/shard_map/all_to_all | solution.py:509
  11.8 29.0 %collective-permute-start.1 = (bf16[1536,128]{1,0:T(8,128)(2,1)S(1)}, bf16[1536,128]{1,0:T(8,128)(2,1)S(1)}, u32[]{:S(2)}, u32[]{:S(2)}) collective-permute-start(bf16[1536,128]{1,0:T(8,128)(2,1)S(1)} %get-tuple-element.27.large_ref), channel_id=1, source_target_pairs={{0,16},{16,0},{1,17},{17,1},{2,18},{18,2},{3,19},{19,3},{4,20},{20... | collective-permute-start | bytes 1179656 | tf_op jit(solution)/shard_map/ppermute | solution.py:556
  13.7 13.9 %collective-permute-start = (bf16[448,128]{1,0:T(8,128)(2,1)S(1)}, bf16[448,128]{1,0:T(8,128)(2,1)S(1)}, u32[]{:S(2)}, u32[]{:S(2)}) collective-permute-start(bf16[448,128]{1,0:T(8,128)(2,1)S(1)} %shard_map.74.after_ref.own_ref), channel_id=1, source_target_pairs={{0,16},{16,0},{1,17},{17,1},{2,18},{18,2},{3,19},{19,3},{4,20},{20... | collective-permute-start | bytes 344072 | tf_op jit(solution)/shard_map/ppermute | solution.py:555
  54.7 10.8 %all-to-all-start.3 = ((bf16[32,2,8,128]{3,2,1,0:T(8,128)(2,1)}), bf16[32,2,8,128]{3,2,1,0:T(8,128)(2,1)S(1)}, u32[]{:S(2)}, u32[]{:S(2)}) async-start(bf16[32,2,8,128]{3,2,1,0:T(8,128)(2,1)} %shard_map.80), calls=%async_computation.3 | async-start | bytes 262144 | tf_op jit(solution)/shard_map/all_to_all | solution.py:509
  57.3 6.7 %collective-permute-start.2 = (bf16[4,128,128]{2,1,0:T(8,128)(2,1)S(1)}, bf16[4,128,128]{2,1,0:T(8,128)(2,1)S(1)}, u32[]{:S(2)}, u32[]{:S(2)}) collective-permute-start(bf16[4,128,128]{2,1,0:T(8,128)(2,1)S(1)} %get-tuple-element.32), channel_id=1, source_target_pairs={{0,16},{16,0},{1,17},{17,1},{2,18},{18,2},{3,19},{19,3},{4,20},{20... | collective-permute-start | bytes 393224 | tf_op jit(solution)/shard_map/ppermute | solution.py:587

commit v8 on v7

--- a/solution.py
+++ b/solution.py
@@ -328,6 +328,15 @@
         n_ref[r * count : (r + 1) * count, :] = row_norm(z_ref[r])
 
 
+def split_kernel(o_ref, owns_ref, after_ref, keep_ref, send_ref):
+    half, count, width = keep_ref.shape
+    owns = (owns_ref[:1, :] > 0.5)[None]
+    full = o_ref[: half * count, :].reshape(half, count, width)
+    short = o_ref[half * count :, :].reshape(half, count, width)
+    keep_ref[...] = jnp.where(owns, full.astype(F32), short.astype(F32)).astype(BF16)
+    send_ref[...] = jnp.where(owns, short.astype(F32), full.astype(F32)).astype(BF16)
+
+
 def join_kernel(keep_ref, other_ref, z_ref, n_ref):
     half = keep_ref.shape[0]
     first = lax.axis_index("section") == 0
@@ -389,17 +398,14 @@
     large_ref,
     other_large_ref,
     masks_ref,
-    owns_ref,
     lr_ref,
-    keep_ref,
-    send_ref,
+    o_ref,
     n_ref,
     z1_ref,
-    o_ref,
     in_ref,
     back_ref,
 ):
-    rows, count, width = z_ref.shape
+    rows, count, _ = z_ref.shape
     half = rows // 2
     transition_weights(0, large_ref, other_large_ref, in_ref, back_ref)
     offsets = [q * 4 * inner + r for q in range(2) for r in range(half)]
@@ -429,11 +435,6 @@
     project(range(rows))
     transition((0, 1), in_ref, back_ref, n_ref, z1_ref, finish)
     tail_full()
-    owns = (owns_ref[:1, :] > 0.5)[None]
-    full = o_ref[: half * count, :].reshape(half, count, width)
-    short = o_ref[half * count :, :].reshape(half, count, width)
-    keep_ref[...] = jnp.where(owns, full.astype(F32), short.astype(F32)).astype(BF16)
-    send_ref[...] = jnp.where(owns, short.astype(F32), full.astype(F32)).astype(BF16)
     four = row_norm(
         jnp.concatenate(
             [o_ref[r * count : r * count + SHORT, :] for r in range(half, rows)], 0
@@ -576,14 +577,21 @@
     t = call(functools.partial(norm_kernel, inner), shape((8 * inner, count), F32), 1)(tri)
     work = [pltpu.VMEM((8 * inner, count), F32), flat, flat]
     halves = shape((rows // 2, count, width), BF16)
-    lr, keep, send = call(
+    lr, state = call(
         functools.partial(update_kernel, inner),
-        (shape((devices, 3, 8, count), BF16), halves, halves),
-        9,
-        [flat] * 3 + [pltpu.VMEM(w_in.shape[1:], BF16), pltpu.VMEM(w_back.shape[1:], BF16)],
-    )(t, z, gate, w_out_first, turned, large, other_large, masks, owns)
+        (shape((devices, 3, 8, count), BF16), tokens),
+        8,
+        [flat] * 2 + [pltpu.VMEM(w_in.shape[1:], BF16), pltpu.VMEM(w_back.shape[1:], BF16)],
+    )(t, z, gate, w_out_first, turned, large, other_large, masks)
 
     sides = exchange(lr)
+    tri_scratch[1] = pltpu.VMEM((64, count), F32)
+    part = call(
+        last_triangle_kernel, shape((devices, CHANNELS, 8, count), BF16), 2, tri_scratch
+    )(sides, owns)
+    keep, send = call(split_kernel, (halves, halves), [vmem, vmem, anywhere], cost=light)(
+        state, owns, part
+    )
     came = lax.ppermute(send, "section", swap)
     z, normed = call(join_kernel, (shape((rows, count, width), BF16), tokens), 2)(keep, came)
     ready = call(
@@ -594,12 +602,7 @@
         5,
         cost=light,
     )(normed, small, other_small, large, other_large)
-    tri_scratch[1] = pltpu.VMEM((64, count), F32)
-    tri = exchange(
-        call(
-            last_triangle_kernel, shape((devices, CHANNELS, 8, count), BF16), 2, tri_scratch
-        )(sides, owns),
-    )
+    tri = exchange(part)
     out = call(
         functools.partial(last_kernel, inner),
         shape((rows, count, width), BF16),

time: 68.3 us -> 68.3 us (level)
  no operation moved by 1% of the time
where the time goes in v8:
time: 68.3 us; the launch traced here: 67.9 us
  blocking collectives  23 us (34%)
  waiting for transfers between devices  19.2 us (28%)
  Pallas kernels  12.9 us (19%)
  starting transfers between devices  12.8 us (19%)
    all_to_all x2, blocking collectives, exchange(): lax.all_to_all(value, ('section', 'row'), split_axis=0, concat_axis=0, ti...  23 us
    ppermute x1, waiting for transfers between devices, fast_body(): other_small = lax.ppermute(small, 'section', swap)  13.7 us
    all_to_all x2, starting transfers between devices, exchange(): lax.all_to_all(value, ('section', 'row'), split_axis=0, concat_axis=0, ti...  8.95 us
    ppermute x1, waiting for transfers between devices, fast_body(): came = lax.ppermute(send, 'section', swap)  5.09 us
    pallas_call x1, Pallas kernels, fast_body(): call(functools.partial(first_kernel, inner), shape(lr_shape, BF16), 4, [p...  2.69 us
    pallas_call x1, Pallas kernels, fast_body(): call(functools.partial(last_kernel, inner), shape((rows, count, width), B...  2.38 us
    pallas_call x1, Pallas kernels, fast_body(): call(functools.partial(update_kernel, inner), (shape((devices, 3, 8, coun...  2.01 us
    pallas_call x1, Pallas kernels, fast_body(): call(stage_kernel, (shape((3 * trans, width), BF16), shape((rows, count,...  1.93 us
  transfers between devices with their start and end apart: 5, of which 3 were waited for; matrix products, arithmetic and copies ran while one was open for 0% of the time, Pallas kernels for 7%

profile of v8, /device:TPU:0, one launch (start us, length us, event | category | flops | bytes accessed | tf_op | source)
XLA Modules:
  0.0 67.9 jit_solution(11220961755449504574)
XLA Ops:
  0.0 2.7 %shard_map.73.after_ref = bf16[32,5,8,128]{3,2,1,0:T(8,128)(2,1)} custom-call(s32[2]{0:T(128)} %order_ref.3, s32[2]{0:T(128)} %valid_ref.3, bf16[2,8,128,128]{3,2,1,0:T(8,128)(2,1)} %pair_ref.3, bf16[1,128,384]{2,1,0:T(8,128)(2,1)} %wp_ref.3), custom_call_target="tpu_custom_call" | custom-call | tf_op jit(solution)/shard_map/pallas_call | solution.py:523
  2.7 6.4 %all-to-all-start = ((bf16[32,5,8,128]{3,2,1,0:T(8,128)(2,1)}), bf16[32,5,8,128]{3,2,1,0:T(8,128)(2,1)S(1)}, u32[]{:S(2)}, u32[]{:S(2)}) async-start(bf16[32,5,8,128]{3,2,1,0:T(8,128)(2,1)} %shard_map.73.after_ref), calls=%async_computation | async-start | bytes 655360 | tf_op jit(solution)/shard_map/all_to_all | solution.py:510
  9.1 0.8 %shard_map.74.after_ref.own_ref = bf16[448,128]{1,0:T(8,128)(2,1)S(1)} custom-call(bf16[1,128,384]{2,1,0:T(8,128)(2,1)} %wp_ref.3, bf16[1,64,128]{2,1,0:T(8,128)(2,1)} %w_out_ref.1, bf16[32,5,8,128]{3,2,1,0:T(8,128)(2,1)} %shard_map.73.after_ref), custom_call_target="tpu_custom_call" | custom-call | flops 34000000 | bytes 1000000 | tf_op jit(solution)/shard_map/pallas_call | solution.py:534
  9.9 1.9 %shard_map.75 = (bf16[1536,128]{1,0:T(8,128)(2,1)S(1)}, bf16[8,128,128]{2,1,0:T(8,128)(2,1)S(1)}, bf16[1024,128]{1,0:T(8,128)(2,1)S(1)}, f32[8,128]{1,0:T(8,128)S(1)}, f32[3,8,128]{2,1,0:T(8,128)S(1)}) custom-call(s32[2]{0:T(128)} %order_ref.3, s32[2]{0:T(128)} %valid_ref.3, bf16[2,8,128,128]{3,2,1,0:T(8,128)(2,1)} %pair_ref.3, ...), custom_call_target="tpu_custom_call" | custom-call | flops 34000000 | bytes 1000000 | tf_op jit(solution)/shard_map/pallas_call | solution.py:541
  11.9 1.8 %collective-permute-start.1 = (bf16[1536,128]{1,0:T(8,128)(2,1)S(1)}, bf16[1536,128]{1,0:T(8,128)(2,1)S(1)}, u32[]{:S(2)}, u32[]{:S(2)}) collective-permute-start(bf16[1536,128]{1,0:T(8,128)(2,1)S(1)} %get-tuple-element.28.large_ref), channel_id=1, source_target_pairs={{0,16},{16,0},{1,17},{17,1},{2,18},{18,2},{3,19},{19,3},{4,20},{20... | collective-permute-start | bytes 1179656 | tf_op jit(solution)/shard_map/ppermute | solution.py:557
  13.7 0.3 collective-permute-start
  13.9 13.7 %collective-permute-done.other_ref = bf16[448,128]{1,0:T(8,128)(2,1)S(1)} collective-permute-done((bf16[448,128]{1,0:T(8,128)(2,1)S(1)}, bf16[448,128]{1,0:T(8,128)(2,1)S(1)}, u32[]{:S(2)}, u32[]{:S(2)}) %collective-permute-start) | collective-permute-done | bytes 114720 | tf_op jit(solution)/shard_map/ppermute | solution.py:556
  27.6 0.3 shard_map.76
  27.9 0.0 all-to-all-done.in_ref
  27.9 0.5 shard_map.77
  28.4 12.3 %all_to_all.20.tri_ref = bf16[32,2,8,128]{3,2,1,0:T(8,128)(2,1)S(1)} all-to-all(bf16[32,2,8,128]{3,2,1,0:T(8,128)(2,1)S(1)} %shard_map.77), channel_id=1, replica_groups=mesh['section'=2,'row'=16] {'section','row'}, dimensions={0} | all-to-all | bytes 262144 | tf_op jit(solution)/shard_map/all_to_all | solution.py:510
  40.7 0.1 shard_map.78.t_ref
  40.9 0.0 collective-permute-done.1.other_large_ref
  40.9 2.0 %shard_map.79 = (bf16[32,3,8,128]{3,2,1,0:T(8,128)(2,1)S(1)}, bf16[1024,128]{1,0:T(8,128)(2,1)S(1)}) custom-call(f32[512,128]{1,0:T(8,128)S(1)} %shard_map.78.t_ref, bf16[8,128,128]{2,1,0:T(8,128)(2,1)S(1)} %get-tuple-element.25.z_ref, f32[1024,128]{1,0:T(8,128)S(1)} %get-tuple-element.24.after_ref.gate_ref, ...), custom_call_target="tpu_custom_call" | custom-call | tf_op jit(solution)/shard_map/pallas_call | solution.py:580
  42.9 10.7 %all_to_all.21.in_ref = bf16[32,3,8,128]{3,2,1,0:T(8,128)(2,1)S(1)} all-to-all(bf16[32,3,8,128]{3,2,1,0:T(8,128)(2,1)S(1)} %get-tuple-element.30), channel_id=1, replica_groups=mesh['section'=2,'row'=16] {'section','row'}, dimensions={0} | all-to-all | bytes 393216 | tf_op jit(solution)/shard_map/all_to_all | solution.py:510
  53.5 1.2 %shard_map.80.after_ref = bf16[32,2,8,128]{3,2,1,0:T(8,128)(2,1)} custom-call(bf16[32,3,8,128]{3,2,1,0:T(8,128)(2,1)S(1)} %all_to_all.21.in_ref, f32[8,128]{1,0:T(8,128)S(1)} %get-tuple-element.31.owns_ref), custom_call_target="tpu_custom_call" | custom-call | tf_op jit(solution)/shard_map/pallas_call | solution.py:589
  54.7 2.6 %all-to-all-start.3 = ((bf16[32,2,8,128]{3,2,1,0:T(8,128)(2,1)}), bf16[32,2,8,128]{3,2,1,0:T(8,128)(2,1)S(1)}, u32[]{:S(2)}, u32[]{:S(2)}) async-start(bf16[32,2,8,128]{3,2,1,0:T(8,128)(2,1)} %shard_map.80.after_ref), calls=%async_computation.3 | async-start | bytes 262144 | tf_op jit(solution)/shard_map/all_to_all | solution.py:510
  57.3 0.1 shard_map.81
  57.4 1.7 %collective-permute-start.2 = (bf16[4,128,128]{2,1,0:T(8,128)(2,1)S(1)}, bf16[4,128,128]{2,1,0:T(8,128)(2,1)S(1)}, u32[]{:S(2)}, u32[]{:S(2)}) collective-permute-start(bf16[4,128,128]{2,1,0:T(8,128)(2,1)S(1)} %get-tuple-element.34), channel_id=1, source_target_pairs={{0,16},{16,0},{1,17},{17,1},{2,18},{18,2},{3,19},{19,3},{4,20},{20... | collective-permute-start | bytes 393224 | tf_op jit(solution)/shard_map/ppermute | solution.py:595
  59.1 5.1 %collective-permute-done.2.other_ref = bf16[4,128,128]{2,1,0:T(8,128)(2,1)S(1)} collective-permute-done((bf16[4,128,128]{2,1,0:T(8,128)(2,1)S(1)}, bf16[4,128,128]{2,1,0:T(8,128)(2,1)S(1)}, u32[]{:S(2)}, u32[]{:S(2)}) %collective-permute-start.2) | collective-permute-done | bytes 131104 | tf_op jit(solution)/shard_map/ppermute | solution.py:595
  64.2 0.6 shard_map.82
  64.7 0.3 shard_map.83
  65.1 0.4 all-to-all-done.3.tri_ref
  65.5 2.4 %shard_map.84 = bf16[8,128,128]{2,1,0:T(8,128)(2,1)} custom-call(bf16[32,2,8,128]{3,2,1,0:T(8,128)(2,1)S(1)} %all-to-all-done.3.tri_ref, bf16[8,128,128]{2,1,0:T(8,128)(2,1)S(1)} %get-tuple-element.35.z_ref, f32[1024,128]{1,0:T(8,128)S(1)} %get-tuple-element.37.gate_ref, bf16[64,128]{1,0:T(8,128)(2,1)S(1)} %get-tuple-element.38.w_out_ref, ...), custom_call_target="tpu_custom_call" | custom-call | tf_op jit(solution)/shard_map/pallas_call | solution.py:606
Async XLA Ops:
  2.7 25.2 %all-to-all-start = ((bf16[32,5,8,128]{3,2,1,0:T(8,128)(2,1)}), bf16[32,5,8,128]{3,2,1,0:T(8,128)(2,1)S(1)}, u32[]{:S(2)}, u32[]{:S(2)}) async-start(bf16[32,5,8,128]{3,2,1,0:T(8,128)(2,1)} %shard_map.73.after_ref), calls=%async_computation | async-start | bytes 655360 | tf_op jit(solution)/shard_map/all_to_all | solution.py:510
  11.9 29.0 %collective-permute-start.1 = (bf16[1536,128]{1,0:T(8,128)(2,1)S(1)}, bf16[1536,128]{1,0:T(8,128)(2,1)S(1)}, u32[]{:S(2)}, u32[]{:S(2)}) collective-permute-start(bf16[1536,128]{1,0:T(8,128)(2,1)S(1)} %get-tuple-element.28.large_ref), channel_id=1, source_target_pairs={{0,16},{16,0},{1,17},{17,1},{2,18},{18,2},{3,19},{19,3},{4,20},{20... | collective-permute-start | bytes 1179656 | tf_op jit(solution)/shard_map/ppermute | solution.py:557
  13.7 13.9 %collective-permute-start = (bf16[448,128]{1,0:T(8,128)(2,1)S(1)}, bf16[448,128]{1,0:T(8,128)(2,1)S(1)}, u32[]{:S(2)}, u32[]{:S(2)}) collective-permute-start(bf16[448,128]{1,0:T(8,128)(2,1)S(1)} %shard_map.74.after_ref.own_ref), channel_id=1, source_target_pairs={{0,16},{16,0},{1,17},{17,1},{2,18},{18,2},{3,19},{19,3},{4,20},{20... | collective-permute-start | bytes 344072 | tf_op jit(solution)/shard_map/ppermute | solution.py:556
  54.7 10.8 %all-to-all-start.3 = ((bf16[32,2,8,128]{3,2,1,0:T(8,128)(2,1)}), bf16[32,2,8,128]{3,2,1,0:T(8,128)(2,1)S(1)}, u32[]{:S(2)}, u32[]{:S(2)}) async-start(bf16[32,2,8,128]{3,2,1,0:T(8,128)(2,1)} %shard_map.80.after_ref), calls=%async_computation.3 | async-start | bytes 262144 | tf_op jit(solution)/shard_map/all_to_all | solution.py:510
  57.4 6.8 %collective-permute-start.2 = (bf16[4,128,128]{2,1,0:T(8,128)(2,1)S(1)}, bf16[4,128,128]{2,1,0:T(8,128)(2,1)S(1)}, u32[]{:S(2)}, u32[]{:S(2)}) collective-permute-start(bf16[4,128,128]{2,1,0:T(8,128)(2,1)S(1)} %get-tuple-element.34), channel_id=1, source_target_pairs={{0,16},{16,0},{1,17},{17,1},{2,18},{18,2},{3,19},{19,3},{4,20},{20... | collective-permute-start | bytes 393224 | tf_op jit(solution)/shard_map/ppermute | solution.py:595
